TPU v7x, 128 devices: a whole 4x4x4 slice. The times are simulated.
128 devices in a mesh: grp: 4 (over z_hi, core), seq: 32 (over y, x, z_lo).
Axes of the slice: x: 4, y: 4, z: 4 (z_hi: 2, z_lo: 2; z = z_hi * 2 + z_lo), core: 2. Of those that a mesh axis runs over, the one named last changes fastest.
Arguments:
- tower_input: bfloat16 [262144, 1024], P(('grp', 'seq')), parts along dimension 0, may hold values from -6 to 6
- first_conv_taps: bfloat16 [3, 1024, 512], replicated, may hold values from -0.109375 to 0.109375
- first_conv_bias: float32 [512], replicated, may hold values from -4 to 4
- first_point_weight: bfloat16 [512, 1024], replicated, may hold values from -0.25 to 0.25
- first_point_bias: float32 [1024], replicated, may hold values from -3 to 3
- second_conv_taps: bfloat16 [3, 1024, 512], replicated, may hold values from -0.109375 to 0.109375
- second_conv_bias: float32 [512], replicated, may hold values from -4 to 4
- second_point_weight: bfloat16 [512, 1024], replicated, may hold values from -0.25 to 0.25
- second_point_bias: float32 [1024], replicated, may hold values from -3 to 3
Outputs:
- tower_out: bfloat16 [262144, 1024], P(('grp', 'seq')), parts along dimension 0
There are 4 independent parts, one for each index of `grp`. A program takes and returns all parts, laid end to end along the dimension named above; an argument that names none is the same for every part. Nothing has to cross between parts.
All inputs are finite; a program needn't handle non-finite values.
Results may differ from a plain program's by a relative error of at most 0.01.
Values may be sent and summed in bfloat16 or wider, within the bound.
No kernel may reach another device: no remote copies, remote signals or barrier semaphores. Data moves between devices by JAX's collectives and lax.ppermute only.
A program may use at most 128 MiB of HBM per device.

v0:
```python
import jax
import jax.numpy as jnp
from jax import lax
from jax.sharding import PartitionSpec as P


def with_halo(cells, sides, width):
    for axis, dim in sides:
        count = lax.axis_size(axis)
        head = lax.slice_in_dim(cells, 0, width, axis=dim)
        tail = lax.slice_in_dim(cells, cells.shape[dim] - width, cells.shape[dim], axis=dim)
        cells = jnp.concatenate(
            [
                lax.ppermute(tail, axis, [(i, (i + 1) % count) for i in range(count)]),
                cells,
                lax.ppermute(head, axis, [((i + 1) % count, i) for i in range(count)]),
            ],
            axis=dim,
        )
    return cells


def from_behind(value, axis, by):
    size = lax.axis_size(axis)
    return lax.ppermute(value, axis, [(i, (i + by) % size) for i in range(size)])


def activate(values):
    return jax.nn.gelu(values.astype(jnp.float32)).astype(jnp.bfloat16)


def rounded_product(acts, tap):
    return jnp.dot(acts, tap, preferred_element_type=jnp.float32).astype(jnp.bfloat16)


def widen(product):
    return lax.optimization_barrier(product).astype(jnp.float32)


def finish(block_in, total, bias_conv, point, bias_point):
    middle = jax.nn.gelu(total + bias_conv).astype(jnp.bfloat16)
    branch = jnp.dot(middle, point, preferred_element_type=jnp.float32)
    return (block_in.astype(jnp.float32) + branch + bias_point).astype(jnp.bfloat16)


def near_layer(block_in, rimmed, taps, bias_conv, point, bias_point):
    rows = block_in.shape[0]
    spacing = (rimmed.shape[0] - rows) // 2
    total = jnp.dot(rimmed[spacing : spacing + rows], taps[1], preferred_element_type=jnp.float32)
    total = total + jnp.dot(rimmed[0:rows], taps[0], preferred_element_type=jnp.float32)
    total = total + jnp.dot(
        rimmed[2 * spacing : 2 * spacing + rows], taps[2], preferred_element_type=jnp.float32
    )
    return finish(block_in, total, bias_conv, point, bias_point)


def per_device(
    tower_input,
    first_conv_taps,
    first_conv_bias,
    first_point_weight,
    first_point_bias,
    second_conv_taps,
    second_conv_bias,
    second_point_weight,
    second_point_bias,
):
    rows = tower_input.shape[0]
    spacing = rows // 4
    acts_near = activate(tower_input)
    rimmed = with_halo(acts_near, (("seq", 0),), spacing)
    single_residual_layer = near_layer(
        tower_input, rimmed, first_conv_taps, first_conv_bias, first_point_weight, first_point_bias
    )
    acts_far = activate(single_residual_layer)
    back_acts = from_behind(acts_far, "seq", 2)
    ahead_acts = from_behind(acts_far, "seq", -2)
    total = jnp.dot(acts_far, second_conv_taps[1], preferred_element_type=jnp.float32)
    total = total + widen(rounded_product(back_acts, second_conv_taps[0]))
    total = total + widen(rounded_product(ahead_acts, second_conv_taps[2]))
    return finish(
        single_residual_layer, total, second_conv_bias, second_point_weight, second_point_bias
    )


def solution(mesh):
    return jax.shard_map(
        per_device,
        mesh=mesh,
        in_specs=(P(("grp", "seq"), None), P(), P(), P(), P(), P(), P(), P(), P()),
        out_specs=P(("grp", "seq"), None),
        check_vma=False,
    )
```

profile of v0, /device:TPU:0, one launch (start us, length us, event | category | flops | bytes accessed | tf_op | source)
XLA Modules:
  0.0 188.1 jit_solution(363865932310207048)
XLA Ops:
  0.0 0.0 copy-start
  0.0 0.0 copy-start.3
  0.0 4.6 %fusion.5 = bf16[2048,1024]{1,0:T(8,128)(2,1)S(1)} fusion(bf16[2048,1024]{1,0:T(8,128)(2,1)} %param.9), kind=kLoop, calls=%fused_computation.15 | loop fusion | flops 20971520 | bytes 8388608 | tf_op jit(solution)/shard_map/convert_element_type | solution.py:29
  4.6 0.0 copy-start.1
  4.6 0.0 copy-start.2
  4.7 0.2 fusion.78
  4.8 2.1 %collective-permute-start = (bf16[512,1024]{1,0:T(8,128)(2,1)S(1)}, bf16[512,1024]{1,0:T(8,128)(2,1)S(1)}, u32[]{:S(2)}, u32[]{:S(2)}) collective-permute-start(bf16[512,1024]{1,0:T(8,128)(2,1)S(1)} %get-tuple-element.6), channel_id=1, source_target_pairs={{0,1},{1,2},{2,3},{3,4},{4,5},{5,6},{6,7},{7,8},{8,9},{9,10},{10,1... | collective-permute-start | bytes 3145736 | tf_op jit(solution)/shard_map/ppermute | solution.py:14
  6.9 4.7 %collective-permute-start.1 = (bf16[512,1024]{1,0:T(8,128)(2,1)S(1)}, bf16[512,1024]{1,0:T(8,128)(2,1)S(1)}, u32[]{:S(2)}, u32[]{:S(2)}) collective-permute-start(bf16[512,1024]{1,0:T(8,128)(2,1)S(1)} %get-tuple-element.5), channel_id=1, source_target_pairs={{1,0},{2,1},{3,2},{4,3},{5,4},{6,5},{7,6},{8,7},{9,8},{10,9},{11,1... | collective-permute-start | bytes 3145736 | tf_op jit(solution)/shard_map/ppermute | solution.py:16
  11.6 0.0 copy-done.3
  11.6 0.0 copy-done.2
  11.6 4.6 %fusion.54 = f32[2048,512]{1,0:T(8,128)} fusion(bf16[3,1024,512]{2,1,0:T(8,128)(2,1)S(1)} %copy-done.3, bf16[2048,1024]{1,0:T(8,128)(2,1)S(1)} %copy-done.2), kind=kOutput, calls=%fused_computation.63 | convolution fusion | flops 2168455168 | bytes 9437184 | tf_op jit(solution)/shard_map/dot_general | solution.py:49
  16.2 0.0 copy-start.5
  16.2 0.0 copy-start.7
  16.2 35.6 %collective-permute-done = bf16[512,1024]{1,0:T(8,128)(2,1)S(1)} collective-permute-done((bf16[512,1024]{1,0:T(8,128)(2,1)S(1)}, bf16[512,1024]{1,0:T(8,128)(2,1)S(1)}, u32[]{:S(2)}, u32[]{:S(2)}) %collective-permute-start) | collective-permute-done | bytes 1048608 | tf_op jit(solution)/shard_map/ppermute | solution.py:14
  51.8 0.0 copy-done.1
  51.8 4.4 %fusion.34 = f32[2048,512]{1,0:T(8,128)} fusion(bf16[2048,1024]{1,0:T(8,128)(2,1)S(1)} %fusion.5, bf16[512,1024]{1,0:T(8,128)(2,1)S(1)} %collective-permute-done, bf16[3,1024,512]{2,1,0:T(8,128)(2,1)S(1)} %copy-done.3), kind=kOutput, calls=%fused_computation.48 | convolution fusion | flops 2155872256 | bytes 10485760 | tf_op jit(solution)/shard_map/dot_general | solution.py:50
  56.2 0.0 collective-permute-done.1
  56.2 0.0 copy-done
  56.2 0.0 copy-done.5
  56.2 0.0 copy-done.7
  56.2 14.4 %fusion.13 = (bf16[2048,1024]{1,0:T(8,128)(2,1)}, bf16[2048,1024]{1,0:T(8,128)(2,1)}) fusion(f32[1024]{0:T(1024)S(1)} %copy-done.5, bf16[512,1024]{1,0:T(8,128)(2,1)S(1)} %copy-done, f32[2048,512]{1,0:T(8,128)} %fusion.54, f32[2048,512]{1,0:T(8,128)} %fusion.34, bf16[512,1024]{1,0:T(8,128)(2,1)S(1)} %collective-permute-done.1, ...), kind=kOutput, calls=%fused_computation.23 | convolution fusion | flops 4345298944 | bytes 28317696 | tf_op jit(solution)/shard_map/dot_general | solution.py:42
  70.6 1.5 collective-permute-start.2
  72.1 3.9 %collective-permute-start.3 = (bf16[2048,1024]{1,0:T(8,128)(2,1)}, bf16[2048,1024]{1,0:T(8,128)(2,1)S(1)}, u32[]{:S(2)}, u32[]{:S(2)}) collective-permute-start(bf16[2048,1024]{1,0:T(8,128)(2,1)} %get-tuple-element.7), channel_id=1, source_target_pairs={{0,30},{1,31},{2,0},{3,1},{4,2},{5,3},{6,4},{7,5},{8,6},{9,7},{10,... | collective-permute-start | bytes 12582920 | tf_op jit(solution)/shard_map/ppermute | solution.py:25
  76.0 89.7 %collective-permute-done.2 = bf16[2048,1024]{1,0:T(8,128)(2,1)S(1)} collective-permute-done((bf16[2048,1024]{1,0:T(8,128)(2,1)}, bf16[2048,1024]{1,0:T(8,128)(2,1)S(1)}, u32[]{:S(2)}, u32[]{:S(2)}) %collective-permute-start.2) | collective-permute-done | bytes 4194336 | tf_op jit(solution)/shard_map/ppermute | solution.py:25
  165.7 5.0 %convolution_convert_fusion.1 = bf16[2048,512]{1,0:T(8,128)(2,1)} fusion(bf16[2048,1024]{1,0:T(8,128)(2,1)S(1)} %collective-permute-done.2, bf16[3,1024,512]{2,1,0:T(8,128)(2,1)} %param.14), kind=kOutput, calls=%fused_computation.51 | convolution fusion | flops 2148532224 | bytes 7340032 | tf_op jit(solution)/shard_map/dot_general | solution.py:33
  170.7 0.0 copy-start.4
  170.7 0.0 copy-start.6
  170.7 0.0 copy-start.8
  170.7 0.0 collective-permute-done.3
  170.7 5.0 %convolution_convert_fusion = bf16[2048,512]{1,0:T(8,128)(2,1)} fusion(bf16[2048,1024]{1,0:T(8,128)(2,1)S(1)} %collective-permute-done.3, bf16[3,1024,512]{2,1,0:T(8,128)(2,1)} %param.14), kind=kOutput, calls=%fused_computation.50 | convolution fusion | flops 2148532224 | bytes 7340032 | tf_op jit(solution)/shard_map/dot_general | solution.py:33
  175.7 0.0 copy-done.4
  175.7 0.0 copy-done.6
  175.7 0.0 copy-done.8
  175.7 12.4 %fusion.15 = bf16[2048,1024]{1,0:T(8,128)(2,1)} fusion(bf16[2048,1024]{1,0:T(8,128)(2,1)} %get-tuple-element.8, f32[1024]{0:T(1024)S(1)} %copy-done.6, bf16[512,1024]{1,0:T(8,128)(2,1)S(1)} %copy-done.4, bf16[2048,512]{1,0:T(8,128)(2,1)} %convolution_convert_fusion, bf16[2048,512]{1,0:T(8,128)(2,1)} %convolution_convert_fusion.1, f32[512]{0:T(512)S(1)} %copy-done.8, ...), kind=kOutput, calls=%fused_computation.25 | convolution fusion | flops 4339007488 | bytes 18880512 | tf_op jit(solution)/shard_map/dot_general | solution.py:42
Async XLA Ops:
  0.0 56.2 %copy-start = (bf16[512,1024]{1,0:T(8,128)(2,1)S(1)}, bf16[512,1024]{1,0:T(8,128)(2,1)}, u32[]{:S(2)}) copy-start(bf16[512,1024]{1,0:T(8,128)(2,1)} %param.12) | copy-start | bytes 3145732
  0.0 11.6 %copy-start.3 = (bf16[3,1024,512]{2,1,0:T(8,128)(2,1)S(1)}, bf16[3,1024,512]{2,1,0:T(8,128)(2,1)}, u32[]{:S(2)}) copy-start(bf16[3,1024,512]{2,1,0:T(8,128)(2,1)} %param.10) | copy-start | bytes 9437188
  4.6 47.2 %copy-start.1 = (bf16[2048,1024]{1,0:T(8,128)(2,1)}, bf16[2048,1024]{1,0:T(8,128)(2,1)S(1)}, u32[]{:S(2)}) copy-start(bf16[2048,1024]{1,0:T(8,128)(2,1)S(1)} %fusion.5) | copy-start | bytes 12582916
  4.6 7.0 %copy-start.2 = (bf16[2048,1024]{1,0:T(8,128)(2,1)S(1)}, bf16[2048,1024]{1,0:T(8,128)(2,1)}, u32[]{:S(2)}) copy-start(bf16[2048,1024]{1,0:T(8,128)(2,1)} %param.9) | copy-start | bytes 12582916
  4.8 47.0 %collective-permute-start = (bf16[512,1024]{1,0:T(8,128)(2,1)S(1)}, bf16[512,1024]{1,0:T(8,128)(2,1)S(1)}, u32[]{:S(2)}, u32[]{:S(2)}) collective-permute-start(bf16[512,1024]{1,0:T(8,128)(2,1)S(1)} %get-tuple-element.6), channel_id=1, source_target_pairs={{0,1},{1,2},{2,3},{3,4},{4,5},{5,6},{6,7},{7,8},{8,9},{9,10},{10,1... | collective-permute-start | bytes 3145736 | tf_op jit(solution)/shard_map/ppermute | solution.py:14
  6.9 49.2 %collective-permute-start.1 = (bf16[512,1024]{1,0:T(8,128)(2,1)S(1)}, bf16[512,1024]{1,0:T(8,128)(2,1)S(1)}, u32[]{:S(2)}, u32[]{:S(2)}) collective-permute-start(bf16[512,1024]{1,0:T(8,128)(2,1)S(1)} %get-tuple-element.5), channel_id=1, source_target_pairs={{1,0},{2,1},{3,2},{4,3},{5,4},{6,5},{7,6},{8,7},{9,8},{10,9},{11,1... | collective-permute-start | bytes 3145736 | tf_op jit(solution)/shard_map/ppermute | solution.py:16
  16.2 40.0 %copy-start.5 = (f32[1024]{0:T(1024)S(1)}, f32[1024]{0:T(1024)}, u32[]{:S(2)}) copy-start(f32[1024]{0:T(1024)} %param.13) | copy-start | bytes 12292
  16.2 40.0 %copy-start.7 = (f32[512]{0:T(512)S(1)}, f32[512]{0:T(512)}, u32[]{:S(2)}) copy-start(f32[512]{0:T(512)} %param.11) | copy-start | bytes 6148
  70.6 95.1 %collective-permute-start.2 = (bf16[2048,1024]{1,0:T(8,128)(2,1)}, bf16[2048,1024]{1,0:T(8,128)(2,1)S(1)}, u32[]{:S(2)}, u32[]{:S(2)}) collective-permute-start(bf16[2048,1024]{1,0:T(8,128)(2,1)} %get-tuple-element.7), channel_id=1, source_target_pairs={{0,2},{1,3},{2,4},{3,5},{4,6},{5,7},{6,8},{7,9},{8,10},{9,11},{10,... | collective-permute-start | bytes 12582920 | tf_op jit(solution)/shard_map/ppermute | solution.py:25
  72.1 98.6 %collective-permute-start.3 = (bf16[2048,1024]{1,0:T(8,128)(2,1)}, bf16[2048,1024]{1,0:T(8,128)(2,1)S(1)}, u32[]{:S(2)}, u32[]{:S(2)}) collective-permute-start(bf16[2048,1024]{1,0:T(8,128)(2,1)} %get-tuple-element.7), channel_id=1, source_target_pairs={{0,30},{1,31},{2,0},{3,1},{4,2},{5,3},{6,4},{7,5},{8,6},{9,7},{10,... | collective-permute-start | bytes 12582920 | tf_op jit(solution)/shard_map/ppermute | solution.py:25
  170.7 5.1 %copy-start.4 = (bf16[512,1024]{1,0:T(8,128)(2,1)S(1)}, bf16[512,1024]{1,0:T(8,128)(2,1)}, u32[]{:S(2)}) copy-start(bf16[512,1024]{1,0:T(8,128)(2,1)} %param.16) | copy-start | bytes 3145732
  170.7 5.1 %copy-start.6 = (f32[1024]{0:T(1024)S(1)}, f32[1024]{0:T(1024)}, u32[]{:S(2)}) copy-start(f32[1024]{0:T(1024)} %param.17) | copy-start | bytes 12292
  170.7 5.1 %copy-start.8 = (f32[512]{0:T(512)S(1)}, f32[512]{0:T(512)}, u32[]{:S(2)}) copy-start(f32[512]{0:T(512)} %param.15) | copy-start | bytes 6148
where the time goes:
time: 189 us; the launch traced here: 188 us
  waiting for transfers between devices  125 us (66%)
  matrix products  45.7 us (24%)
  starting transfers between devices  12.3 us (7%)
  other arithmetic  4.62 us (2%)
    ppermute x2, waiting for transfers between devices, from_behind(): lax.ppermute(value, axis, [(i, (i + by) % size) for i in range(size)])  89.7 us
    ppermute x1, waiting for transfers between devices, with_halo(): lax.ppermute(tail, axis, [(i, (i + 1) % count) for i in range(count)])  35.6 us
    dot_general x2, matrix products, finish(): branch = jnp.dot(middle, point, preferred_element_type=jnp.float32)  26.8 us
    dot_general x2, matrix products, rounded_product(): jnp.dot(acts, tap, preferred_element_type=jnp.float32).astype(jnp.bfloat16)  10 us
    ppermute x2, starting transfers between devices, from_behind(): lax.ppermute(value, axis, [(i, (i + by) % size) for i in range(size)])  5.47 us
    ppermute x1, starting transfers between devices, with_halo(): lax.ppermute(head, axis, [((i + 1) % count, i) for i in range(count)])  4.73 us
    convert_element_type x1, other arithmetic, activate(): return jax.nn.gelu(values.astype(jnp.float32)).astype(jnp.bfloat16)  4.62 us
    dot_general x1, matrix products, near_layer(): jnp.dot(rimmed[spacing:spacing + rows], taps[1], preferred_element_type=j...  4.57 us
  transfers between devices with their start and end apart: 4, of which 2 were waited for; matrix products, arithmetic and copies ran while one was open for 7% of the time, Pallas kernels for 0%

commit v1 on v0

v1 whole, which is shorter than its diff:
```python
import math

import jax
import jax.numpy as jnp
from jax import lax
from jax.experimental import pallas as pl
from jax.experimental.pallas import tpu as pltpu
from jax.sharding import PartitionSpec as P

BLOCK = 256
LIMIT = 40 * 1024 * 1024
VMEM = pl.BlockSpec(memory_space=pltpu.VMEM)
BF16 = jnp.bfloat16
F32 = jnp.float32


def shift(value, axis, by):
    size = lax.axis_size(axis)
    return lax.ppermute(value, axis, [(i, (i + by) % size) for i in range(size)])


def gelu(v):
    inner = math.sqrt(2.0 / math.pi) * (v + 0.044715 * (v * v * v))
    return 0.5 * v * (1.0 + jnp.tanh(inner))


def dot(a, b):
    return jnp.dot(a, b, preferred_element_type=F32)


def rows_of(step):
    return pl.ds(pl.multiple_of(step * BLOCK, BLOCK), BLOCK)


def params(**kw):
    return pltpu.CompilerParams(vmem_limit_bytes=LIMIT, **kw)


def cost(flops, bytes_accessed):
    return pl.CostEstimate(flops=flops, bytes_accessed=bytes_accessed, transcendentals=0)


def rim_kernel(x_ref, tap_ref, act_ref, first_ref, last_ref):
    act = gelu(x_ref[...].astype(F32)).astype(BF16)
    act_ref[...] = act
    product = dot(act, tap_ref[0]).astype(BF16)

    @pl.when(pl.program_id(0) == 0)
    def _():
        first_ref[...] = product

    @pl.when(pl.program_id(0) == 1)
    def _():
        last_ref[...] = product


def rim(x, taps, spacing):
    rows, c = x.shape
    m = taps.shape[2]
    per = spacing // BLOCK
    jump = (rows - spacing) // BLOCK
    return pl.pallas_call(
        rim_kernel,
        grid=(2, per),
        in_specs=[
            pl.BlockSpec((BLOCK, c), lambda e, h: (jump * e + h, 0)),
            pl.BlockSpec((1, c, m), lambda e, h: (2 - 2 * e, 0, 0)),
        ],
        out_specs=[
            pl.BlockSpec((BLOCK, c), lambda e, h: (per * e + h, 0)),
            pl.BlockSpec((BLOCK, m), lambda e, h: (h + e * (per - 1 - h), 0)),
            pl.BlockSpec((BLOCK, m), lambda e, h: (e * h, 0)),
        ],
        out_shape=[
            jax.ShapeDtypeStruct((2 * spacing, c), BF16),
            jax.ShapeDtypeStruct((spacing, m), BF16),
            jax.ShapeDtypeStruct((spacing, m), BF16),
        ],
        compiler_params=params(),
        cost_estimate=cost(4 * spacing * c * m, 8 * spacing * c),
        name="rim",
    )(x, taps)


def after_total(total, x, bias_conv, point, bias_point, outer, refs, at):
    one_ref, act_ref, out0_ref, out2_ref = refs
    mid = gelu(total + bias_conv[...]).astype(BF16)
    one = (x.astype(F32) + dot(mid, point[...]) + bias_point[...]).astype(BF16)
    one_ref[at, :] = one
    act = gelu(one.astype(F32)).astype(BF16)
    act_ref[at, :] = act
    out0_ref[at, :] = dot(act, outer[0]).astype(BF16)
    out2_ref[at, :] = dot(act, outer[2]).astype(BF16)


def inner_kernel(
    per, x_ref, edge_ref, taps, bias_conv, point, bias_point, outer,
    near_ref, one_ref, act_ref, out0_ref, out2_ref,
):
    @pl.loop(0, 2 * per)
    def _(s):
        near_ref[rows_of(s), :] = gelu(x_ref[rows_of(s + per), :].astype(F32)).astype(BF16)

    refs = (one_ref, act_ref, out0_ref, out2_ref)

    @pl.loop(0, per)
    def _(s):
        total = dot(edge_ref[rows_of(s), :], taps[0])
        total = total + dot(near_ref[rows_of(s), :], taps[1])
        total = total + dot(near_ref[rows_of(s + per), :], taps[2])
        after_total(
            total, x_ref[rows_of(s + per), :], bias_conv, point, bias_point, outer, refs, rows_of(s)
        )

    @pl.loop(0, per)
    def _(s):
        total = dot(near_ref[rows_of(s), :], taps[0])
        total = total + dot(near_ref[rows_of(s + per), :], taps[1])
        total = total + dot(edge_ref[rows_of(s + per), :], taps[2])
        after_total(
            total, x_ref[rows_of(s + 2 * per), :], bias_conv, point, bias_point, outer, refs,
            rows_of(s + per),
        )


def edge_kernel(
    per, x_ref, edge_ref, near_ref, prev_ref, next_ref, taps, bias_conv, point, bias_point, outer,
    one_ref, act_ref, out0_ref, out2_ref,
):
    refs = (one_ref, act_ref, out0_ref, out2_ref)

    @pl.loop(0, per)
    def _(s):
        total = prev_ref[rows_of(s), :].astype(F32)
        total = total + dot(edge_ref[rows_of(s), :], taps[1])
        total = total + dot(near_ref[rows_of(s), :], taps[2])
        after_total(
            total, x_ref[rows_of(s), :], bias_conv, point, bias_point, outer, refs, rows_of(s)
        )

    @pl.loop(0, per)
    def _(s):
        total = dot(near_ref[rows_of(s + per), :], taps[0])
        total = total + dot(edge_ref[rows_of(s + per), :], taps[1])
        total = total + next_ref[rows_of(s), :].astype(F32)
        after_total(
            total, x_ref[rows_of(s + 3 * per), :], bias_conv, point, bias_point, outer, refs,
            rows_of(s + per),
        )


def layer_outputs(rows, c, m):
    return [
        jax.ShapeDtypeStruct((rows, c), BF16),
        jax.ShapeDtypeStruct((rows, c), BF16),
        jax.ShapeDtypeStruct((rows, m), BF16),
        jax.ShapeDtypeStruct((rows, m), BF16),
    ]


def inner(x, edge, taps, bias_conv, point, bias_point, outer, spacing):
    c, m = taps.shape[1:]
    rows = 2 * spacing

    def body(*refs):
        inner_kernel(spacing // BLOCK, *refs)

    return pl.pallas_call(
        body,
        in_specs=[VMEM] * 7,
        out_specs=[VMEM] * 5,
        out_shape=[jax.ShapeDtypeStruct((rows, c), BF16)] + layer_outputs(rows, c, m),
        compiler_params=params(),
        cost_estimate=cost(12 * rows * c * m, 10 * rows * c),
        name="inner",
    )(x, edge, taps, bias_conv, point, bias_point, outer)


def edges(x, edge, near, prev, following, taps, bias_conv, point, bias_point, outer, spacing):
    c, m = taps.shape[1:]
    rows = 2 * spacing

    def body(*refs):
        edge_kernel(spacing // BLOCK, *refs)

    return pl.pallas_call(
        body,
        in_specs=[VMEM] * 10,
        out_specs=[VMEM] * 4,
        out_shape=layer_outputs(rows, c, m),
        compiler_params=params(),
        cost_estimate=cost(10 * rows * c * m, 10 * rows * c),
        name="edges",
    )(x, edge, near, prev, following, taps, bias_conv, point, bias_point, outer)


def centre_kernel(act_ref, tap, bias_conv, out_ref):
    @pl.loop(0, act_ref.shape[0] // BLOCK)
    def _(s):
        out_ref[rows_of(s), :] = dot(act_ref[rows_of(s), :], tap[1]) + bias_conv[...]


def centre(act, outer, bias_conv):
    rows, c = act.shape
    m = outer.shape[2]
    return pl.pallas_call(
        centre_kernel,
        in_specs=[VMEM] * 3,
        out_specs=VMEM,
        out_shape=jax.ShapeDtypeStruct((rows, m), F32),
        compiler_params=params(),
        cost_estimate=cost(2 * rows * c * m, 4 * rows * c),
        name="centre",
    )(act, outer, bias_conv)


def finish_kernel(centre_ref, back_ref, ahead_ref, one_ref, point, bias_point, *rest):
    out_ref = rest[-1]
    at = rows_of(pl.program_id(0))
    total = centre_ref[at, :] + back_ref[at, :].astype(F32) + ahead_ref[at, :].astype(F32)
    mid = gelu(total).astype(BF16)
    out = one_ref[at, :].astype(F32) + dot(mid, point[...]) + bias_point[...]
    out_ref[...] = out.astype(BF16)


def finish(mid_sum, back, ahead, one, point, bias_point, whole, rows, block_of):
    c = one.shape[1]
    m = back.shape[1]
    own = one.shape[0]
    extra = [] if whole is None else [whole]
    return pl.pallas_call(
        finish_kernel,
        grid=(own // BLOCK,),
        in_specs=[VMEM] * 6 + [pl.BlockSpec(memory_space=pl.ANY)] * len(extra),
        out_specs=pl.BlockSpec((BLOCK, c), lambda s: (block_of(s), 0)),
        out_shape=jax.ShapeDtypeStruct((rows, c), BF16),
        input_output_aliases={6: 0} if extra else {},
        compiler_params=params(),
        cost_estimate=cost(2 * own * c * m, 8 * own * c),
        name="finish",
    )(mid_sum, back, ahead, one, point, bias_point, *extra)


def per_device(
    tower_input,
    first_conv_taps,
    first_conv_bias,
    first_point_weight,
    first_point_bias,
    second_conv_taps,
    second_conv_bias,
    second_point_weight,
    second_point_bias,
):
    rows = tower_input.shape[0]
    spacing = rows // 4
    per = spacing // BLOCK
    conv1, point1 = first_conv_bias[None, :], first_point_bias[None, :]
    conv2, point2 = second_conv_bias[None, :], second_point_bias[None, :]

    edge_act, first, last = rim(tower_input, first_conv_taps, spacing)
    following = shift(first, "seq", -1)
    prev = shift(last, "seq", 1)
    near, one_a, act_a, a0, a2 = inner(
        tower_input, edge_act, first_conv_taps, conv1, first_point_weight, point1, second_conv_taps, spacing
    )
    back_a = shift(a0, "seq", 2)
    ahead_a = shift(a2, "seq", -2)
    one_b, act_b, b0, b2 = edges(
        tower_input, edge_act, near, prev, following, first_conv_taps, conv1, first_point_weight, point1,
        second_conv_taps, spacing,
    )
    back_b = shift(b0, "seq", 2)
    ahead_b = shift(b2, "seq", -2)
    centre_a = centre(act_a, second_conv_taps, conv2)
    centre_b = centre(act_b, second_conv_taps, conv2)
    out = finish(
        centre_a, back_a, ahead_a, one_a, second_point_weight, point2, None, rows, lambda s: s + per
    )
    return finish(
        centre_b, back_b, ahead_b, one_b, second_point_weight, point2, out, rows,
        lambda s: s + 2 * per * (s // per),
    )


def solution(mesh):
    return jax.shard_map(
        per_device,
        mesh=mesh,
        in_specs=(P(("grp", "seq"), None), P(), P(), P(), P(), P(), P(), P(), P()),
        out_specs=P(("grp", "seq"), None),
        check_vma=False,
    )
```

time: 189 us -> 82.8 us (0.44)
  waiting for transfers between devices: 125 us -> 18.4 us
  matrix products: 45.7 us -> 0 us
  Pallas kernels: 0 us -> 40.9 us
  local copies, waits for them, and re-layouts: 0.21 us -> 5.7 us
  starting transfers between devices: 12.3 us -> 17.5 us
  other arithmetic: 4.62 us -> 0 us
    ppermute x4 -> x6, waiting for transfers between devices: 125 us -> 18.4 us  [shift(): lax.ppermute(value, axis, [(i, (i + by) % size) for i in range(size)])]
    dot_general x6 -> x0, matrix products: 45.7 us -> none  [the longest x2 26.8 us: finish(): branch = jnp.dot(middle, point, preferred_element_type=jnp.float32)]
    pallas_call x0 -> x7, Pallas kernels: none -> 40.9 us  [the longest x1 15.5 us: inner(): pl.pallas_call(body, in_specs=[VMEM] * 7, out_specs=[VMEM] * 5, out_shape...]
    unnamed x18 -> x24, local copies, waits for them, and re-layouts: 0.04 us -> 5.7 us
    ppermute x4 -> x6, starting transfers between devices: 12.3 us -> 17.5 us  [shift(): lax.ppermute(value, axis, [(i, (i + by) % size) for i in range(size)])]
    convert_element_type x1 -> x0, other arithmetic: 4.62 us -> none  [activate(): return jax.nn.gelu(values.astype(jnp.float32)).astype(jnp.bfloat16)]
  transfers between devices with their start and end apart: 4 -> 6, of which waited for: 2 -> 2; matrix products, arithmetic and copies ran while one was open for 7% -> 0% of each run, Pallas kernels for 0% -> 43%
where the time goes in v1:
time: 82.8 us; the launch traced here: 82.6 us
  Pallas kernels  40.9 us (49%)
  waiting for transfers between devices  18.4 us (22%)
  starting transfers between devices  17.5 us (21%)
  local copies, waits for them, and re-layouts  5.7 us (7%)
    ppermute x6, waiting for transfers between devices, shift(): lax.ppermute(value, axis, [(i, (i + by) % size) for i in range(size)])  18.4 us
    ppermute x6, starting transfers between devices, shift(): lax.ppermute(value, axis, [(i, (i + by) % size) for i in range(size)])  17.5 us
    pallas_call x1, Pallas kernels, inner(): pl.pallas_call(body, in_specs=[VMEM] * 7, out_specs=[VMEM] * 5, out_shape...  15.5 us
    pallas_call x1, Pallas kernels, edges(): pl.pallas_call(body, in_specs=[VMEM] * 10, out_specs=[VMEM] * 4, out_shap...  13 us
    pallas_call x2, Pallas kernels, finish(): pl.pallas_call(finish_kernel, grid=(own // BLOCK,), in_specs=[VMEM] * 6 +...  6.65 us
    unnamed x24, local copies, waits for them, and re-layouts  5.7 us
    pallas_call x2, Pallas kernels, centre(): pl.pallas_call(centre_kernel, in_specs=[VMEM] * 3, out_specs=VMEM, out_sh...  3.49 us
    pallas_call x1, Pallas kernels, rim(): pl.pallas_call(rim_kernel, grid=(2, per), in_specs=[pl.BlockSpec((BLOCK,...  2.28 us
  transfers between devices with their start and end apart: 6, of which 2 were waited for; matrix products, arithmetic and copies ran while one was open for 0% of the time, Pallas kernels for 43%

profile of v1, /device:TPU:0, one launch (start us, length us, event | category | flops | bytes accessed | tf_op | source)
XLA Modules:
  0.0 82.6 jit_solution(14581135372978164802)
XLA Ops:
  0.0 0.0 copy-start.1
  0.0 2.2 %copy-done.1 = bf16[2048,1024]{1,0:T(8,128)(2,1)S(1)} copy-done((bf16[2048,1024]{1,0:T(8,128)(2,1)S(1)}, bf16[2048,1024]{1,0:T(8,128)(2,1)}, u32[]{:S(2)}) %copy-start.1) | copy-done | bytes 4194328
  2.2 0.0 copy-start.3
  2.2 1.9 %copy-done.3 = bf16[3,1024,512]{2,1,0:T(8,128)(2,1)S(1)} copy-done((bf16[3,1024,512]{2,1,0:T(8,128)(2,1)S(1)}, bf16[3,1024,512]{2,1,0:T(8,128)(2,1)}, u32[]{:S(2)}) %copy-start.3) | copy-done | bytes 3145752
  4.1 0.0 copy-start.8
  4.1 0.0 copy-start.10
  4.1 0.0 copy-start.11
  4.1 2.3 %rim.1 = (bf16[1024,1024]{1,0:T(8,128)(2,1)S(1)}, bf16[512,512]{1,0:T(8,128)(2,1)S(1)}, bf16[512,512]{1,0:T(8,128)(2,1)S(1)}) custom-call(bf16[2048,1024]{1,0:T(8,128)(2,1)S(1)} %copy-done.1, bf16[3,1024,512]{2,1,0:T(8,128)(2,1)S(1)} %copy-done.3), custom_call_target="tpu_custom_call" | custom-call | flops 1073741824 | bytes 4194304 | tf_op jit(solution)/shard_map/rim/pallas_call | solution.py:62
  6.4 0.0 copy-start.6
  6.4 2.1 %collective-permute-start = (bf16[512,512]{1,0:T(8,128)(2,1)S(1)}, bf16[512,512]{1,0:T(8,128)(2,1)S(1)}, u32[]{:S(2)}, u32[]{:S(2)}) collective-permute-start(bf16[512,512]{1,0:T(8,128)(2,1)S(1)} %get-tuple-element.19), channel_id=1, source_target_pairs={{0,1},{1,2},{2,3},{3,4},{4,5},{5,6},{6,7},{7,8},{8,9},{9,10},{10,1... | collective-permute-start | bytes 1572872 | tf_op jit(solution)/shard_map/ppermute | solution.py:19
  8.5 4.7 %collective-permute-start.1 = (bf16[512,512]{1,0:T(8,128)(2,1)S(1)}, bf16[512,512]{1,0:T(8,128)(2,1)S(1)}, u32[]{:S(2)}, u32[]{:S(2)}) collective-permute-start(bf16[512,512]{1,0:T(8,128)(2,1)S(1)} %get-tuple-element.20), channel_id=1, source_target_pairs={{0,31},{1,0},{2,1},{3,2},{4,3},{5,4},{6,5},{7,6},{8,7},{9,8},{10,9... | collective-permute-start | bytes 1572872 | tf_op jit(solution)/shard_map/ppermute | solution.py:19
  13.2 0.0 copy-done.8
  13.2 0.0 copy-done.10
  13.2 0.0 copy-done.11
  13.2 0.0 copy-start.9
  13.2 15.5 %inner.1 = (bf16[1024,1024]{1,0:T(8,128)(2,1)S(1)}, bf16[1024,1024]{1,0:T(8,128)(2,1)S(1)}, bf16[1024,1024]{1,0:T(8,128)(2,1)S(1)}, bf16[1024,512]{1,0:T(8,128)(2,1)}, bf16[1024,512]{1,0:T(8,128)(2,1)}) custom-call(bf16[2048,1024]{1,0:T(8,128)(2,1)} %refs_0_.3, bf16[1024,1024]{1,0:T(8,128)(2,1)S(1)} %get-tuple-element.17.refs_1_, ...), custom_call_target="tpu_custom_call" | custom-call | flops 6442450944 | bytes 10485760 | tf_op jit(solution)/shard_map/inner/pallas_call | solution.py:168
  28.7 0.0 copy-done.6
  28.7 0.0 collective-permute-start.4
  28.7 5.3 %collective-permute-start.5 = (bf16[1024,512]{1,0:T(8,128)(2,1)}, bf16[1024,512]{1,0:T(8,128)(2,1)S(1)}, u32[]{:S(2)}, u32[]{:S(2)}) collective-permute-start(bf16[1024,512]{1,0:T(8,128)(2,1)} %get-tuple-element.27), channel_id=1, source_target_pairs={{0,30},{1,31},{2,0},{3,1},{4,2},{5,3},{6,4},{7,5},{8,6},{9,7},{10,... | collective-permute-start | bytes 3145736 | tf_op jit(solution)/shard_map/ppermute | solution.py:19
  34.0 0.0 collective-permute-done.refs_3_
  34.0 0.0 collective-permute-done.1.refs_4_
  34.0 0.0 copy-done.9
  34.0 0.0 copy-start.7
  34.0 1.6 %copy-done.7 = bf16[1024,1024]{1,0:T(8,128)(2,1)S(1)} copy-done((bf16[1024,1024]{1,0:T(8,128)(2,1)S(1)}, bf16[1024,1024]{1,0:T(8,128)(2,1)}, u32[]{:S(2)}) %copy-start.7) | copy-done | bytes 2097176
  35.6 0.0 copy-start
  35.6 0.0 copy-start.5
  35.6 13.0 %edges.1 = (bf16[1024,1024]{1,0:T(8,128)(2,1)S(1)}, bf16[1024,1024]{1,0:T(8,128)(2,1)S(1)}, bf16[1024,512]{1,0:T(8,128)(2,1)}, bf16[1024,512]{1,0:T(8,128)(2,1)}) custom-call(bf16[2048,1024]{1,0:T(8,128)(2,1)} %refs_0_.3, bf16[1024,1024]{1,0:T(8,128)(2,1)S(1)} %copy-done.7, bf16[1024,1024]{1,0:T(8,128)(2,1)S(1)} %get-tuple-element.18.refs_2_, ...), custom_call_target="tpu_custom_call" | custom-call | flops 5368709120 | bytes 10485760 | tf_op jit(solution)/shard_map/edges/pallas_call | solution.py:186
  48.7 0.0 collective-permute-start.2
  48.7 5.3 %collective-permute-start.3 = (bf16[1024,512]{1,0:T(8,128)(2,1)}, bf16[1024,512]{1,0:T(8,128)(2,1)S(1)}, u32[]{:S(2)}, u32[]{:S(2)}) collective-permute-start(bf16[1024,512]{1,0:T(8,128)(2,1)} %get-tuple-element.23), channel_id=1, source_target_pairs={{0,30},{1,31},{2,0},{3,1},{4,2},{5,3},{6,4},{7,5},{8,6},{9,7},{10,... | collective-permute-start | bytes 3145736 | tf_op jit(solution)/shard_map/ppermute | solution.py:19
  54.0 0.0 copy-done
  54.0 0.0 copy-done.5
  54.0 1.7 %centre.3.centre_ref = f32[1024,512]{1,0:T(8,128)S(1)} custom-call(bf16[1024,1024]{1,0:T(8,128)(2,1)S(1)} %get-tuple-element.25.act_ref, bf16[3,1024,512]{2,1,0:T(8,128)(2,1)S(1)} %copy-done, f32[1,512]{1,0:T(1,128)S(1)} %bitcast.6), custom_call_target="tpu_custom_call" | custom-call | flops 1073741824 | bytes 4194304 | tf_op jit(solution)/shard_map/centre/pallas_call | solution.py:206
  55.8 0.0 copy-start.2
  55.8 0.0 copy-start.4
  55.8 1.7 %centre.2.centre_ref = f32[1024,512]{1,0:T(8,128)S(1)} custom-call(bf16[1024,1024]{1,0:T(8,128)(2,1)S(1)} %get-tuple-element.21.act_ref, bf16[3,1024,512]{2,1,0:T(8,128)(2,1)S(1)} %copy-done, f32[1,512]{1,0:T(1,128)S(1)} %bitcast.7), custom_call_target="tpu_custom_call" | custom-call | flops 1073741824 | bytes 4194304 | tf_op jit(solution)/shard_map/centre/pallas_call | solution.py:206
  57.6 0.7 collective-permute-done.4.back_ref
  58.3 0.0 collective-permute-done.5.ahead_ref
  58.3 0.0 copy-done.2
  58.3 0.0 copy-done.4
  58.3 3.4 %finish.2.rest_0_ = bf16[2048,1024]{1,0:T(8,128)(2,1)} custom-call(f32[1024,512]{1,0:T(8,128)S(1)} %centre.3.centre_ref, bf16[1024,512]{1,0:T(8,128)(2,1)S(1)} %collective-permute-done.4.back_ref, bf16[1024,512]{1,0:T(8,128)(2,1)S(1)} %collective-permute-done.5.ahead_ref, bf16[1024,1024]{1,0:T(8,128)(2,1)S(1)} %get-tuple-element.28.one_ref, ...), custom_call_target="tpu_custom_call" | custom-call | flops 1073741824 | bytes 8388608 | tf_op jit(solution)/shard_map/finish/pallas_call | solution.py:231
  61.7 17.7 %collective-permute-done.2.back_ref = bf16[1024,512]{1,0:T(8,128)(2,1)S(1)} collective-permute-done((bf16[1024,512]{1,0:T(8,128)(2,1)}, bf16[1024,512]{1,0:T(8,128)(2,1)S(1)}, u32[]{:S(2)}, u32[]{:S(2)}) %collective-permute-start.2) | collective-permute-done | bytes 1048608 | tf_op jit(solution)/shard_map/ppermute | solution.py:19
  79.3 0.0 collective-permute-done.3.ahead_ref
  79.3 3.3 %finish.3 = bf16[2048,1024]{1,0:T(8,128)(2,1)} custom-call(f32[1024,512]{1,0:T(8,128)S(1)} %centre.2.centre_ref, bf16[1024,512]{1,0:T(8,128)(2,1)S(1)} %collective-permute-done.2.back_ref, bf16[1024,512]{1,0:T(8,128)(2,1)S(1)} %collective-permute-done.3.ahead_ref, bf16[1024,1024]{1,0:T(8,128)(2,1)S(1)} %get-tuple-element.24.one_ref, ...), custom_call_target="tpu_custom_call", output_to_operand_aliasing={{}: (6, {})} | custom-call | flops 1073741824 | bytes 8388608 | tf_op jit(solution)/shard_map/finish/pallas_call | solution.py:231
Async XLA Ops:
  0.0 2.2 %copy-start.1 = (bf16[2048,1024]{1,0:T(8,128)(2,1)S(1)}, bf16[2048,1024]{1,0:T(8,128)(2,1)}, u32[]{:S(2)}) copy-start(bf16[2048,1024]{1,0:T(8,128)(2,1)} %refs_0_.3) | copy-start | bytes 12582916
  2.2 1.9 %copy-start.3 = (bf16[3,1024,512]{2,1,0:T(8,128)(2,1)S(1)}, bf16[3,1024,512]{2,1,0:T(8,128)(2,1)}, u32[]{:S(2)}) copy-start(bf16[3,1024,512]{2,1,0:T(8,128)(2,1)} %refs_5_.1) | copy-start | bytes 9437188
  4.1 9.1 %copy-start.8 = (bf16[512,1024]{1,0:T(8,128)(2,1)S(1)}, bf16[512,1024]{1,0:T(8,128)(2,1)}, u32[]{:S(2)}) copy-start(bf16[512,1024]{1,0:T(8,128)(2,1)} %refs_7_.1) | copy-start | bytes 3145732
  4.1 9.1 %copy-start.10 = (f32[1024]{0:T(1024)S(1)}, f32[1024]{0:T(1024)}, u32[]{:S(2)}) copy-start(f32[1024]{0:T(1024)} %param.13) | copy-start | bytes 12292
  4.1 9.1 %copy-start.11 = (f32[512]{0:T(512)S(1)}, f32[512]{0:T(512)}, u32[]{:S(2)}) copy-start(f32[512]{0:T(512)} %param.11) | copy-start | bytes 6148
  6.4 22.3 %copy-start.6 = (bf16[1024,1024]{1,0:T(8,128)(2,1)}, bf16[1024,1024]{1,0:T(8,128)(2,1)S(1)}, u32[]{:S(2)}) copy-start(bf16[1024,1024]{1,0:T(8,128)(2,1)S(1)} %get-tuple-element.17.refs_1_) | copy-start | bytes 6291460
  6.4 27.6 %collective-permute-start = (bf16[512,512]{1,0:T(8,128)(2,1)S(1)}, bf16[512,512]{1,0:T(8,128)(2,1)S(1)}, u32[]{:S(2)}, u32[]{:S(2)}) collective-permute-start(bf16[512,512]{1,0:T(8,128)(2,1)S(1)} %get-tuple-element.19), channel_id=1, source_target_pairs={{0,1},{1,2},{2,3},{3,4},{4,5},{5,6},{6,7},{7,8},{8,9},{9,10},{10,1... | collective-permute-start | bytes 1572872 | tf_op jit(solution)/shard_map/ppermute | solution.py:19
  8.5 25.6 %collective-permute-start.1 = (bf16[512,512]{1,0:T(8,128)(2,1)S(1)}, bf16[512,512]{1,0:T(8,128)(2,1)S(1)}, u32[]{:S(2)}, u32[]{:S(2)}) collective-permute-start(bf16[512,512]{1,0:T(8,128)(2,1)S(1)} %get-tuple-element.20), channel_id=1, source_target_pairs={{0,31},{1,0},{2,1},{3,2},{4,3},{5,4},{6,5},{7,6},{8,7},{9,8},{10,9... | collective-permute-start | bytes 1572872 | tf_op jit(solution)/shard_map/ppermute | solution.py:19
  13.2 20.8 %copy-start.9 = (bf16[512,1024]{1,0:T(8,128)(2,1)S(1)}, bf16[512,1024]{1,0:T(8,128)(2,1)}, u32[]{:S(2)}) copy-start(bf16[512,1024]{1,0:T(8,128)(2,1)} %refs_7_.1) | copy-start | bytes 3145732
  28.7 29.6 %collective-permute-start.4 = (bf16[1024,512]{1,0:T(8,128)(2,1)}, bf16[1024,512]{1,0:T(8,128)(2,1)S(1)}, u32[]{:S(2)}, u32[]{:S(2)}) collective-permute-start(bf16[1024,512]{1,0:T(8,128)(2,1)} %get-tuple-element.26), channel_id=1, source_target_pairs={{0,2},{1,3},{2,4},{3,5},{4,6},{5,7},{6,8},{7,9},{8,10},{9,11},{10,... | collective-permute-start | bytes 3145736 | tf_op jit(solution)/shard_map/ppermute | solution.py:19
  28.7 29.6 %collective-permute-start.5 = (bf16[1024,512]{1,0:T(8,128)(2,1)}, bf16[1024,512]{1,0:T(8,128)(2,1)S(1)}, u32[]{:S(2)}, u32[]{:S(2)}) collective-permute-start(bf16[1024,512]{1,0:T(8,128)(2,1)} %get-tuple-element.27), channel_id=1, source_target_pairs={{0,30},{1,31},{2,0},{3,1},{4,2},{5,3},{6,4},{7,5},{8,6},{9,7},{10,... | collective-permute-start | bytes 3145736 | tf_op jit(solution)/shard_map/ppermute | solution.py:19
  34.0 1.6 %copy-start.7 = (bf16[1024,1024]{1,0:T(8,128)(2,1)S(1)}, bf16[1024,1024]{1,0:T(8,128)(2,1)}, u32[]{:S(2)}) copy-start(bf16[1024,1024]{1,0:T(8,128)(2,1)} %copy-done.6) | copy-start | bytes 6291460
  35.6 18.4 %copy-start = (bf16[3,1024,512]{2,1,0:T(8,128)(2,1)S(1)}, bf16[3,1024,512]{2,1,0:T(8,128)(2,1)}, u32[]{:S(2)}) copy-start(bf16[3,1024,512]{2,1,0:T(8,128)(2,1)} %tap.3) | copy-start | bytes 9437188
  35.6 18.4 %copy-start.5 = (f32[512]{0:T(512)S(1)}, f32[512]{0:T(512)}, u32[]{:S(2)}) copy-start(f32[512]{0:T(512)} %param.15) | copy-start | bytes 6148
  48.7 30.6 %collective-permute-start.2 = (bf16[1024,512]{1,0:T(8,128)(2,1)}, bf16[1024,512]{1,0:T(8,128)(2,1)S(1)}, u32[]{:S(2)}, u32[]{:S(2)}) collective-permute-start(bf16[1024,512]{1,0:T(8,128)(2,1)} %get-tuple-element.22), channel_id=1, source_target_pairs={{0,2},{1,3},{2,4},{3,5},{4,6},{5,7},{6,8},{7,9},{8,10},{9,11},{10,... | collective-permute-start | bytes 3145736 | tf_op jit(solution)/shard_map/ppermute | solution.py:19
  48.7 30.6 %collective-permute-start.3 = (bf16[1024,512]{1,0:T(8,128)(2,1)}, bf16[1024,512]{1,0:T(8,128)(2,1)S(1)}, u32[]{:S(2)}, u32[]{:S(2)}) collective-permute-start(bf16[1024,512]{1,0:T(8,128)(2,1)} %get-tuple-element.23), channel_id=1, source_target_pairs={{0,30},{1,31},{2,0},{3,1},{4,2},{5,3},{6,4},{7,5},{8,6},{9,7},{10,... | collective-permute-start | bytes 3145736 | tf_op jit(solution)/shard_map/ppermute | solution.py:19
  55.8 2.5 %copy-start.2 = (bf16[512,1024]{1,0:T(8,128)(2,1)S(1)}, bf16[512,1024]{1,0:T(8,128)(2,1)}, u32[]{:S(2)}) copy-start(bf16[512,1024]{1,0:T(8,128)(2,1)} %point.3) | copy-start | bytes 3145732
  55.8 2.5 %copy-start.4 = (f32[1024]{0:T(1024)S(1)}, f32[1024]{0:T(1024)}, u32[]{:S(2)}) copy-start(f32[1024]{0:T(1024)} %param.17) | copy-start | bytes 12292

commit v2 on v0

v2 whole, which is shorter than its diff:
```python
import math

import jax
import jax.numpy as jnp
from jax import lax
from jax.experimental import pallas as pl
from jax.experimental.pallas import tpu as pltpu
from jax.sharding import PartitionSpec as P

LIMIT = 16 * 1024 * 1024
VMEM = pl.BlockSpec(memory_space=pltpu.VMEM)
ANY = pl.BlockSpec(memory_space=pl.ANY)
HBM = pl.BlockSpec(memory_space=pltpu.HBM)
BF16 = jnp.bfloat16
F32 = jnp.float32


def swap(value, first, step):
    size = lax.axis_size("seq")
    pairs = []
    for i in range(size):
        if first(i):
            j = (i + step) % size
            pairs += [(i, j), (j, i)]
    return lax.ppermute(value, "seq", sorted(pairs))


def gelu(v):
    inner = math.sqrt(2.0 / math.pi) * (v + 0.044715 * (v * v * v))
    return 0.5 * v * (1.0 + jnp.tanh(inner))


def dot(a, b):
    return jnp.dot(a, b, preferred_element_type=F32)


def odd_position():
    return lax.rem(lax.axis_index("seq"), 2)


def quarter_rows(quarter, size):
    at = quarter + odd_position() * (3 - 2 * quarter)
    return pl.ds(pl.multiple_of(at * size, size), size)


def call(body, name, out_shape, args, flops, scratch, aliases=None, out_specs=None, specs=None):
    moved = sum(a.size * a.dtype.itemsize for a in args)
    return pl.pallas_call(
        body,
        in_specs=specs,
        out_specs=[VMEM] * len(out_shape) if out_specs is None else out_specs,
        out_shape=out_shape,
        scratch_shapes=scratch,
        input_output_aliases=aliases or {},
        compiler_params=pltpu.CompilerParams(vmem_limit_bytes=LIMIT),
        cost_estimate=pl.CostEstimate(flops=flops, bytes_accessed=moved, transcendentals=0),
        name=name,
    )(*args)


def shape(rows, columns, dtype=BF16):
    return jax.ShapeDtypeStruct((rows, columns), dtype)


def rim(x, taps, quarter):
    size, (c, m) = x.shape[0] // 4, taps.shape[1:]
    tap = 2 if quarter == 0 else 0

    def body(x_hbm, taps_hbm, act_ref, product_ref, x_own, tap_own, sems):
        which = tap + odd_position() * (2 - 2 * tap)
        half = size // 2
        rows = quarter_rows(quarter, size)
        copies = [
            pltpu.make_async_copy(x_hbm.at[rows], x_own, sems.at[0]),
            pltpu.make_async_copy(taps_hbm.at[which], tap_own, sems.at[1]),
        ]
        for copy in copies:
            copy.start()
        copies[0].wait()
        for k in range(2):
            part = pl.ds(k * half, half)
            act_ref[part, :] = gelu(x_own[part, :].astype(F32)).astype(BF16)
        copies[1].wait()
        product_ref[...] = dot(act_ref[...], tap_own[...]).astype(BF16)

    return call(
        body, f"rim{quarter}", [shape(size, c), shape(size, m)], (x, taps), 2 * size * c * m,
        [pltpu.VMEM((size, c), BF16), pltpu.VMEM((c, m), BF16), pltpu.SemaphoreType.DMA((2,))],
        specs=[HBM, HBM],
    )


def after_total(total, x, point, bias_point, outer, one_ref, act_ref, first_ref, second_ref):
    mid = gelu(total).astype(BF16)
    one = (x.astype(F32) + dot(mid, point[...]) + bias_point[...]).astype(BF16)
    one_ref[...] = one
    act = gelu(one.astype(F32)).astype(BF16)
    act_ref[...] = act
    odd_pair = lax.rem(lax.div(lax.axis_index("seq"), 2), 2)
    first_ref[...] = dot(act, outer[2 * odd_pair]).astype(BF16)
    second_ref[...] = dot(act, outer[2 - 2 * odd_pair]).astype(BF16)


def layer(x, quarter, acts, arrived, weights, fresh=False):
    taps, bias_conv, point, bias_point, outer = weights
    size, (c, m) = x.shape[0] // 4, taps.shape[1:]
    given = [a for a in acts if a is not None]
    known = [a is not None for a in acts]
    loads = (quarter, quarter + 1) if fresh else (quarter,)

    def body(*refs):
        refs = list(refs)
        x_hbm = refs.pop(0)
        sources = [refs.pop(0) if k else None for k in known]
        arrived_ref = None if arrived is None else refs.pop(0)
        taps_ref, bias_conv_ref, point_ref, bias_point_ref, outer_ref = refs[:5]
        refs = refs[5:]
        made = [refs.pop(0), refs.pop(0)] if fresh else []
        one_ref, act_ref, first_ref, second_ref = refs[:4]
        x_own, sems = refs[4:]
        copies = [
            pltpu.make_async_copy(x_hbm.at[quarter_rows(q, size)], x_own.at[k], sems.at[k])
            for k, q in enumerate(loads)
        ]
        for copy in copies:
            copy.start()
        if fresh:
            for k in range(2):
                copies[k].wait()
                made[k][...] = gelu(x_own[k].astype(F32)).astype(BF16)
            sources[1:] = made
        odd = odd_position()
        total = None if arrived is None else arrived_ref[...].astype(F32)
        for k, source in enumerate(sources):
            if source is not None:
                term = dot(source[...], taps_ref[k + odd * (2 - 2 * k)])
                total = term if total is None else total + term
        if not fresh:
            copies[0].wait()
        after_total(
            total + bias_conv_ref[...], x_own[0], point_ref, bias_point_ref, outer_ref, one_ref, act_ref, first_ref,
            second_ref,
        )

    args = [x] + given + ([] if arrived is None else [arrived]) + list(weights)
    outs = ([shape(size, c)] * 2 if fresh else []) + [shape(size, c)] * 2 + [shape(size, m)] * 2
    return call(
        body, f"layer{quarter}", outs, args, 12 * size * c * m,
        [pltpu.VMEM((len(loads), size, c), BF16), pltpu.SemaphoreType.DMA((len(loads),))],
        specs=[HBM] + [VMEM] * (len(args) - 1),
    )


def centre(acts, outer, bias_conv):
    size, c = acts[0].shape
    m = outer.shape[2]
    n = len(acts)

    def body(*refs):
        outer_ref, bias_ref = refs[n : n + 2]
        for act_ref, out_ref in zip(refs[:n], refs[n + 2 :]):
            out_ref[...] = dot(act_ref[...], outer_ref[1]) + bias_ref[...]

    args = list(acts) + [outer, bias_conv]
    return call(body, "centre", [shape(size, m, F32)] * n, args, 2 * n * size * c * m, [], specs=[VMEM] * len(args))


def finish(quarter, centre_sum, one_side, other_side, one, point, bias_point, whole):
    size, c = one.shape
    m = centre_sum.shape[1]
    half = size // 2

    def body(centre_ref, one_side_ref, other_side_ref, one_ref, point_ref, bias_ref, *rest):
        out_hbm, held, sems = rest[-3:]
        start = quarter_rows(quarter, size).start
        copies = []
        for k in range(2):
            part = pl.ds(k * half, half)
            total = centre_ref[part, :] + one_side_ref[part, :].astype(F32) + other_side_ref[part, :].astype(F32)
            mid = gelu(total).astype(BF16)
            out = one_ref[part, :].astype(F32) + dot(mid, point_ref[...]) + bias_ref[...]
            held[k] = out.astype(BF16)
            to = pl.ds(pl.multiple_of(start + k * half, half), half)
            copies.append(pltpu.make_async_copy(held.at[k], out_hbm.at[to], sems.at[k]))
            copies[k].start()
        for copy in copies:
            copy.wait()

    args = [centre_sum, one_side, other_side, one, point, bias_point] + ([] if whole is None else [whole])
    return call(
        body, f"finish{quarter}", [shape(4 * size, c)], args, 2 * size * c * m,
        [pltpu.VMEM((2, half, c), BF16), pltpu.SemaphoreType.DMA((2,))],
        aliases={} if whole is None else {6: 0}, out_specs=[ANY], specs=[VMEM] * 6 + [ANY] * (len(args) - 6),
    )[0]


def per_device(
    tower_input,
    first_conv_taps,
    first_conv_bias,
    first_point_weight,
    first_point_bias,
    second_conv_taps,
    second_conv_bias,
    second_point_weight,
    second_point_bias,
):
    near = (first_conv_taps, first_conv_bias[None, :], first_point_weight, first_point_bias[None, :], second_conv_taps)

    tower_input = pltpu.with_memory_space_constraint(tower_input, pltpu.HBM)
    rim_taps = pltpu.with_memory_space_constraint(first_conv_taps, pltpu.HBM)
    act0, to_pair = rim(tower_input, rim_taps, 0)
    later, to_pair = lax.optimization_barrier((tower_input, to_pair))
    from_pair = swap(to_pair, lambda i: i % 2 == 1, 1)
    act3, to_partner = rim(later, rim_taps, 3)
    from_partner = swap(to_partner, lambda i: i % 2 == 0, 1)

    def send(products):
        return (
            swap(products[0], lambda i: i // 2 % 2 == 0, 2),
            swap(products[1], lambda i: i // 2 % 2 == 1, 2),
        )

    act1, act2, one1, far1, *products1 = layer(tower_input, 1, (act0, None, None), None, near, fresh=True)
    sides1 = send(products1)
    one2, far2, *products2 = layer(tower_input, 2, (act1, act2, act3), None, near)
    sides2 = send(products2)
    one3, far3, *products3 = layer(tower_input, 3, (act2, act3, None), from_partner, near)
    sides3 = send(products3)
    one0, far0, *products0 = layer(tower_input, 0, (None, act0, act1), from_pair, near)
    sides0 = send(products0)

    centres = centre((far1, far2, far3, far0), second_conv_taps, second_conv_bias[None, :])
    out = None
    for quarter, total, sides, one in zip((1, 2, 3, 0), centres, (sides1, sides2, sides3, sides0), (one1, one2, one3, one0)):
        out = finish(quarter, total, *sides, one, second_point_weight, second_point_bias[None, :], out)
    return out


def solution(mesh):
    return jax.shard_map(
        per_device,
        mesh=mesh,
        in_specs=(P(("grp", "seq"), None), P(), P(), P(), P(), P(), P(), P(), P()),
        out_specs=P(("grp", "seq"), None),
        check_vma=False,
    )
```

time: 189 us -> 74.6 us (0.39)
  waiting for transfers between devices: 125 us -> 22 us
  matrix products: 45.7 us -> 0 us
  Pallas kernels: 0 us -> 33.6 us
  starting transfers between devices: 12.3 us -> 18.1 us
  other arithmetic: 4.62 us -> 0 us
    ppermute x4 -> x10, waiting for transfers between devices: 125 us -> 22 us  [swap(): return lax.ppermute(value, 'seq', sorted(pairs))]
    dot_general x6 -> x0, matrix products: 45.7 us -> none  [the longest x2 26.8 us: finish(): branch = jnp.dot(middle, point, preferred_element_type=jnp.float32)]
    pallas_call x0 -> x11, Pallas kernels: none -> 33.6 us  [call(): pl.pallas_call(body, in_specs=specs, out_specs=[VMEM] * len(out_shape) if...]
    ppermute x4 -> x10, starting transfers between devices: 12.3 us -> 18.1 us  [swap(): return lax.ppermute(value, 'seq', sorted(pairs))]
    convert_element_type x1 -> x0, other arithmetic: 4.62 us -> none  [activate(): return jax.nn.gelu(values.astype(jnp.float32)).astype(jnp.bfloat16)]
  transfers between devices with their start and end apart: 4 -> 10, of which waited for: 2 -> 5; matrix products, arithmetic and copies ran while one was open for 7% -> 0% of each run, Pallas kernels for 0% -> 39%
where the time goes in v2:
time: 74.6 us; the launch traced here: 74.2 us
  Pallas kernels  33.6 us (45%)
  waiting for transfers between devices  22 us (29%)
  starting transfers between devices  18.1 us (24%)
    pallas_call x11, Pallas kernels, call(): pl.pallas_call(body, in_specs=specs, out_specs=[VMEM] * len(out_shape) if...  33.6 us
    ppermute x10, waiting for transfers between devices, swap(): return lax.ppermute(value, 'seq', sorted(pairs))  22 us
    ppermute x10, starting transfers between devices, swap(): return lax.ppermute(value, 'seq', sorted(pairs))  18.1 us
  transfers between devices with their start and end apart: 10, of which 5 were waited for; matrix products, arithmetic and copies ran while one was open for 0% of the time, Pallas kernels for 39%

profile of v2, /device:TPU:0, one launch (start us, length us, event | category | flops | bytes accessed | tf_op | source)
XLA Modules:
  0.0 74.2 jit_solution(6168239046409365265)
XLA Ops:
  0.0 2.7 %rim0.1 = (bf16[512,1024]{1,0:T(8,128)(2,1)S(1)}, bf16[512,512]{1,0:T(8,128)(2,1)S(1)}) custom-call(bf16[2048,1024]{1,0:T(8,128)(2,1)} %refs_0_.7, bf16[3,1024,512]{2,1,0:T(8,128)(2,1)} %refs_4_.8), custom_call_target="tpu_custom_call" | custom-call | flops 536870912 | bytes 7340032 | tf_op jit(solution)/shard_map/rim0/pallas_call | solution.py:48
  2.7 0.0 copy-start
  2.7 0.0 copy-start.1
  2.7 0.0 copy-start.3
  2.7 0.0 copy-start.4
  2.7 0.0 copy-start.6
  2.7 6.7 %collective-permute-start.1 = (bf16[512,512]{1,0:T(8,128)(2,1)S(1)}, bf16[512,512]{1,0:T(8,128)(2,1)S(1)}, u32[]{:S(2)}, u32[]{:S(2)}) collective-permute-start(bf16[512,512]{1,0:T(8,128)(2,1)S(1)} %get-tuple-element.43), channel_id=1, source_target_pairs={{0,31},{1,2},{2,1},{3,4},{4,3},{5,6},{6,5},{7,8},{8,7},{9,10},{10,... | collective-permute-start | bytes 1572872 | tf_op jit(solution)/shard_map/ppermute | solution.py:25
  9.5 2.7 %rim3.1 = (bf16[512,1024]{1,0:T(8,128)(2,1)S(1)}, bf16[512,512]{1,0:T(8,128)(2,1)S(1)}) custom-call(bf16[2048,1024]{1,0:T(8,128)(2,1)} %refs_0_.7, bf16[3,1024,512]{2,1,0:T(8,128)(2,1)} %refs_4_.8), custom_call_target="tpu_custom_call" | custom-call | flops 536870912 | bytes 7340032 | tf_op jit(solution)/shard_map/rim3/pallas_call | solution.py:48
  12.1 0.1 collective-permute-start
  12.2 0.0 copy-done
  12.2 0.0 copy-done.1
  12.2 0.0 copy-done.3
  12.3 0.0 copy-done.4
  12.3 0.0 copy-done.6
  12.3 6.0 %layer1.1 = (bf16[512,1024]{1,0:T(8,128)(2,1)S(1)}, bf16[512,1024]{1,0:T(8,128)(2,1)S(1)}, bf16[512,1024]{1,0:T(8,128)(2,1)S(1)}, bf16[512,1024]{1,0:T(8,128)(2,...) custom-call(bf16[2048,1024]{1,0:T(8,128)(2,1)} %refs_0_.7, ...), custom_call_target="tpu_custom_call" | custom-call | flops 3221225472 | bytes 12589056 | tf_op jit(solution)/shard_map/layer1/pallas_call | solution.py:48
  18.2 0.1 collective-permute-start.8
  18.3 2.5 %collective-permute-start.9 = (bf16[512,512]{1,0:T(8,128)(2,1)S(1)}, bf16[512,512]{1,0:T(8,128)(2,1)S(1)}, u32[]{:S(2)}, u32[]{:S(2)}) collective-permute-start(bf16[512,512]{1,0:T(8,128)(2,1)S(1)} %get-tuple-element.59), channel_id=1, source_target_pairs={{0,30},{1,31},{2,4},{3,5},{4,2},{5,3},{6,8},{7,9},{8,6},{9,7},{10,... | collective-permute-start | bytes 1572872 | tf_op jit(solution)/shard_map/ppermute | solution.py:25
  20.8 5.0 %layer2.1 = (bf16[512,1024]{1,0:T(8,128)(2,1)S(1)}, bf16[512,1024]{1,0:T(8,128)(2,1)S(1)}, bf16[512,512]{1,0:T(8,128)(2,1)S(1)}, bf16[512,512]{1,0:T(8,128)(2,1)S(1)}) custom-call(bf16[2048,1024]{1,0:T(8,128)(2,1)} %refs_0_.7, bf16[512,1024]{1,0:T(8,128)(2,1)S(1)} %get-tuple-element.35.refs_1_.refs_2_, ...), custom_call_target="tpu_custom_call" | custom-call | flops 3221225472 | bytes 14686208 | tf_op jit(solution)/shard_map/layer2/pallas_call | solution.py:48
  25.8 0.1 collective-permute-start.6
  25.9 6.7 %collective-permute-done.refs_3_ = bf16[512,512]{1,0:T(8,128)(2,1)S(1)} collective-permute-done((bf16[512,512]{1,0:T(8,128)(2,1)S(1)}, bf16[512,512]{1,0:T(8,128)(2,1)S(1)}, u32[]{:S(2)}, u32[]{:S(2)}) %collective-permute-start) | collective-permute-done | bytes 524320 | tf_op jit(solution)/shard_map/ppermute | solution.py:25
  32.6 3.0 %collective-permute-start.7 = (bf16[512,512]{1,0:T(8,128)(2,1)S(1)}, bf16[512,512]{1,0:T(8,128)(2,1)S(1)}, u32[]{:S(2)}, u32[]{:S(2)}) collective-permute-start(bf16[512,512]{1,0:T(8,128)(2,1)S(1)} %get-tuple-element.55), channel_id=1, source_target_pairs={{0,30},{1,31},{2,4},{3,5},{4,2},{5,3},{6,8},{7,9},{8,6},{9,7},{10,... | collective-permute-start | bytes 1572872 | tf_op jit(solution)/shard_map/ppermute | solution.py:25
  35.6 3.9 %layer3.1 = (bf16[512,1024]{1,0:T(8,128)(2,1)S(1)}, bf16[512,1024]{1,0:T(8,128)(2,1)S(1)}, bf16[512,512]{1,0:T(8,128)(2,1)S(1)}, bf16[512,512]{1,0:T(8,128)(2,1)S(1)}) custom-call(bf16[2048,1024]{1,0:T(8,128)(2,1)} %refs_0_.7, bf16[512,1024]{1,0:T(8,128)(2,1)S(1)} %get-tuple-element.36.refs_2_.refs_1_, ...), custom_call_target="tpu_custom_call" | custom-call | flops 3221225472 | bytes 14161920 | tf_op jit(solution)/shard_map/layer3/pallas_call | solution.py:48
  39.6 0.0 collective-permute-done.1.refs_3_
  39.6 0.1 collective-permute-start.4
  39.7 0.0 collective-permute-done.8.one_side_ref
  39.7 0.0 copy-start.7
  39.7 2.4 %collective-permute-start.5 = (bf16[512,512]{1,0:T(8,128)(2,1)S(1)}, bf16[512,512]{1,0:T(8,128)(2,1)S(1)}, u32[]{:S(2)}, u32[]{:S(2)}) collective-permute-start(bf16[512,512]{1,0:T(8,128)(2,1)S(1)} %get-tuple-element.51), channel_id=1, source_target_pairs={{0,30},{1,31},{2,4},{3,5},{4,2},{5,3},{6,8},{7,9},{8,6},{9,7},{10,... | collective-permute-start | bytes 1572872 | tf_op jit(solution)/shard_map/ppermute | solution.py:25
  42.1 3.8 %layer0.1 = (bf16[512,1024]{1,0:T(8,128)(2,1)S(1)}, bf16[512,1024]{1,0:T(8,128)(2,1)S(1)}, bf16[512,512]{1,0:T(8,128)(2,1)S(1)}, bf16[512,512]{1,0:T(8,128)(2,1)S(1)}) custom-call(bf16[2048,1024]{1,0:T(8,128)(2,1)} %refs_0_.7, bf16[512,1024]{1,0:T(8,128)(2,1)S(1)} %get-tuple-element.33.refs_1_, bf16[512,1024]{1,0:T(8,128)(2,1)S(1)} %get-tuple-element.35.refs_1_.refs_2_, ...), custom_call_target="tpu_custom_call" | custom-call | flops 3221225472 | bytes 14161920 | tf_op jit(solution)/shard_map/layer0/pallas_call | solution.py:48
  45.9 0.0 copy-start.2
  45.9 0.0 copy-start.5
  45.9 0.0 collective-permute-done.9.other_side_ref
  45.9 0.1 collective-permute-start.2
  46.0 0.0 collective-permute-done.6.one_side_ref
  46.0 3.1 %collective-permute-start.3 = (bf16[512,512]{1,0:T(8,128)(2,1)S(1)}, bf16[512,512]{1,0:T(8,128)(2,1)S(1)}, u32[]{:S(2)}, u32[]{:S(2)}) collective-permute-start(bf16[512,512]{1,0:T(8,128)(2,1)S(1)} %get-tuple-element.47), channel_id=1, source_target_pairs={{0,30},{1,31},{2,4},{3,5},{4,2},{5,3},{6,8},{7,9},{8,6},{9,7},{10,... | collective-permute-start | bytes 1572872 | tf_op jit(solution)/shard_map/ppermute | solution.py:25
  49.1 0.0 copy-done.7
  49.1 2.3 %centre.1 = (f32[512,512]{1,0:T(8,128)S(1)}, f32[512,512]{1,0:T(8,128)S(1)}, f32[512,512]{1,0:T(8,128)S(1)}, f32[512,512]{1,0:T(8,128)S(1)}) custom-call(bf16[512,1024]{1,0:T(8,128)(2,1)S(1)} %get-tuple-element.34.refs_0_, bf16[512,1024]{1,0:T(8,128)(2,1)S(1)} %get-tuple-element.40.refs_1_, bf16[512,1024]{1,0:T(8,128)(2,1)S(1)} %get-tuple-element.42.refs_2_, ...), custom_call_target="tpu_custom_call" | custom-call | flops 2147483648 | bytes 7342080 | tf_op jit(solution)/shard_map/centre/pallas_call | solution.py:48
  51.4 0.0 copy-done.2
  51.5 0.0 copy-done.5
  51.5 1.8 %finish1.1.rest_0_ = bf16[2048,1024]{1,0:T(8,128)(2,1)} custom-call(f32[512,512]{1,0:T(8,128)S(1)} %get-tuple-element.57.centre_ref, bf16[512,512]{1,0:T(8,128)(2,1)S(1)} %collective-permute-done.8.one_side_ref, bf16[512,512]{1,0:T(8,128)(2,1)S(1)} %collective-permute-done.9.other_side_ref, bf16[512,1024]{1,0:T(8,128)(2,1)S(1)} %get-tuple-element.60.one_ref, ...), custom_call_target="tpu_custom_call" | custom-call | flops 536870912 | bytes 4198400 | tf_op jit(solution)/shard_map/finish1/pallas_call | solution.py:48
  53.3 0.0 collective-permute-done.7.other_side_ref
  53.3 1.8 %finish2.1.rest_0_ = bf16[2048,1024]{1,0:T(8,128)(2,1)} custom-call(f32[512,512]{1,0:T(8,128)S(1)} %get-tuple-element.53.centre_ref, bf16[512,512]{1,0:T(8,128)(2,1)S(1)} %collective-permute-done.6.one_side_ref, bf16[512,512]{1,0:T(8,128)(2,1)S(1)} %collective-permute-done.7.other_side_ref, ...), custom_call_target="tpu_custom_call", output_to_operand_aliasing={{}: (6, {})} | custom-call | flops 536870912 | bytes 8392704 | tf_op jit(solution)/shard_map/finish2/pallas_call | solution.py:48
  55.2 0.5 collective-permute-done.4.one_side_ref
  55.6 6.3 %collective-permute-done.5.other_side_ref = bf16[512,512]{1,0:T(8,128)(2,1)S(1)} collective-permute-done((bf16[512,512]{1,0:T(8,128)(2,1)S(1)}, bf16[512,512]{1,0:T(8,128)(2,1)S(1)}, u32[]{:S(2)}, u32[]{:S(2)}) %collective-permute-start.5) | collective-permute-done | bytes 524320 | tf_op jit(solution)/shard_map/ppermute | solution.py:25
  62.0 1.8 %finish3.1.rest_0_ = bf16[2048,1024]{1,0:T(8,128)(2,1)} custom-call(f32[512,512]{1,0:T(8,128)S(1)} %get-tuple-element.49.centre_ref, bf16[512,512]{1,0:T(8,128)(2,1)S(1)} %collective-permute-done.4.one_side_ref, bf16[512,512]{1,0:T(8,128)(2,1)S(1)} %collective-permute-done.5.other_side_ref, ...), custom_call_target="tpu_custom_call", output_to_operand_aliasing={{}: (6, {})} | custom-call | flops 536870912 | bytes 8392704 | tf_op jit(solution)/shard_map/finish3/pallas_call | solution.py:48
  63.8 1.6 %collective-permute-done.2.one_side_ref = bf16[512,512]{1,0:T(8,128)(2,1)S(1)} collective-permute-done((bf16[512,512]{1,0:T(8,128)(2,1)S(1)}, bf16[512,512]{1,0:T(8,128)(2,1)S(1)}, u32[]{:S(2)}, u32[]{:S(2)}) %collective-permute-start.2) | collective-permute-done | bytes 524320 | tf_op jit(solution)/shard_map/ppermute | solution.py:25
  65.4 6.8 %collective-permute-done.3.other_side_ref = bf16[512,512]{1,0:T(8,128)(2,1)S(1)} collective-permute-done((bf16[512,512]{1,0:T(8,128)(2,1)S(1)}, bf16[512,512]{1,0:T(8,128)(2,1)S(1)}, u32[]{:S(2)}, u32[]{:S(2)}) %collective-permute-start.3) | collective-permute-done | bytes 524320 | tf_op jit(solution)/shard_map/ppermute | solution.py:25
  72.3 1.8 %finish0.1 = bf16[2048,1024]{1,0:T(8,128)(2,1)} custom-call(f32[512,512]{1,0:T(8,128)S(1)} %get-tuple-element.45.centre_ref, bf16[512,512]{1,0:T(8,128)(2,1)S(1)} %collective-permute-done.2.one_side_ref, bf16[512,512]{1,0:T(8,128)(2,1)S(1)} %collective-permute-done.3.other_side_ref, ...), custom_call_target="tpu_custom_call", output_to_operand_aliasing={{}: (6, {})} | custom-call | flops 536870912 | bytes 8392704 | tf_op jit(solution)/shard_map/finish0/pallas_call | solution.py:48
Async XLA Ops:
  2.7 9.6 %copy-start = (bf16[3,1024,512]{2,1,0:T(8,128)(2,1)S(1)}, bf16[3,1024,512]{2,1,0:T(8,128)(2,1)}, u32[]{:S(2)}) copy-start(bf16[3,1024,512]{2,1,0:T(8,128)(2,1)} %refs_4_.8) | copy-start | bytes 9437188
  2.7 9.6 %copy-start.1 = (bf16[3,1024,512]{2,1,0:T(8,128)(2,1)S(1)}, bf16[3,1024,512]{2,1,0:T(8,128)(2,1)}, u32[]{:S(2)}) copy-start(bf16[3,1024,512]{2,1,0:T(8,128)(2,1)} %refs_4_.9) | copy-start | bytes 9437188
  2.7 9.6 %copy-start.3 = (bf16[512,1024]{1,0:T(8,128)(2,1)S(1)}, bf16[512,1024]{1,0:T(8,128)(2,1)}, u32[]{:S(2)}) copy-start(bf16[512,1024]{1,0:T(8,128)(2,1)} %refs_6_.7) | copy-start | bytes 3145732
  2.7 9.5 %copy-start.4 = (f32[1024]{0:T(1024)S(1)}, f32[1024]{0:T(1024)}, u32[]{:S(2)}) copy-start(f32[1024]{0:T(1024)} %param.13) | copy-start | bytes 12292
  2.7 9.5 %copy-start.6 = (f32[512]{0:T(512)S(1)}, f32[512]{0:T(512)}, u32[]{:S(2)}) copy-start(f32[512]{0:T(512)} %param.11) | copy-start | bytes 6148
  2.7 36.8 %collective-permute-start.1 = (bf16[512,512]{1,0:T(8,128)(2,1)S(1)}, bf16[512,512]{1,0:T(8,128)(2,1)S(1)}, u32[]{:S(2)}, u32[]{:S(2)}) collective-permute-start(bf16[512,512]{1,0:T(8,128)(2,1)S(1)} %get-tuple-element.43), channel_id=1, source_target_pairs={{0,31},{1,2},{2,1},{3,4},{4,3},{5,6},{6,5},{7,8},{8,7},{9,10},{10,... | collective-permute-start | bytes 1572872 | tf_op jit(solution)/shard_map/ppermute | solution.py:25
  12.1 20.5 %collective-permute-start = (bf16[512,512]{1,0:T(8,128)(2,1)S(1)}, bf16[512,512]{1,0:T(8,128)(2,1)S(1)}, u32[]{:S(2)}, u32[]{:S(2)}) collective-permute-start(bf16[512,512]{1,0:T(8,128)(2,1)S(1)} %get-tuple-element.41), channel_id=1, source_target_pairs={{0,1},{1,0},{2,3},{3,2},{4,5},{5,4},{6,7},{7,6},{8,9},{9,8},{10,11... | collective-permute-start | bytes 1572872 | tf_op jit(solution)/shard_map/ppermute | solution.py:25
  18.2 21.4 %collective-permute-start.8 = (bf16[512,512]{1,0:T(8,128)(2,1)S(1)}, bf16[512,512]{1,0:T(8,128)(2,1)S(1)}, u32[]{:S(2)}, u32[]{:S(2)}) collective-permute-start(bf16[512,512]{1,0:T(8,128)(2,1)S(1)} %get-tuple-element.58), channel_id=1, source_target_pairs={{0,2},{1,3},{2,0},{3,1},{4,6},{5,7},{6,4},{7,5},{8,10},{9,11},{10,... | collective-permute-start | bytes 1572872 | tf_op jit(solution)/shard_map/ppermute | solution.py:25
  18.3 27.6 %collective-permute-start.9 = (bf16[512,512]{1,0:T(8,128)(2,1)S(1)}, bf16[512,512]{1,0:T(8,128)(2,1)S(1)}, u32[]{:S(2)}, u32[]{:S(2)}) collective-permute-start(bf16[512,512]{1,0:T(8,128)(2,1)S(1)} %get-tuple-element.59), channel_id=1, source_target_pairs={{0,30},{1,31},{2,4},{3,5},{4,2},{5,3},{6,8},{7,9},{8,6},{9,7},{10,... | collective-permute-start | bytes 1572872 | tf_op jit(solution)/shard_map/ppermute | solution.py:25
  25.8 20.2 %collective-permute-start.6 = (bf16[512,512]{1,0:T(8,128)(2,1)S(1)}, bf16[512,512]{1,0:T(8,128)(2,1)S(1)}, u32[]{:S(2)}, u32[]{:S(2)}) collective-permute-start(bf16[512,512]{1,0:T(8,128)(2,1)S(1)} %get-tuple-element.54), channel_id=1, source_target_pairs={{0,2},{1,3},{2,0},{3,1},{4,6},{5,7},{6,4},{7,5},{8,10},{9,11},{10,... | collective-permute-start | bytes 1572872 | tf_op jit(solution)/shard_map/ppermute | solution.py:25
  32.6 20.7 %collective-permute-start.7 = (bf16[512,512]{1,0:T(8,128)(2,1)S(1)}, bf16[512,512]{1,0:T(8,128)(2,1)S(1)}, u32[]{:S(2)}, u32[]{:S(2)}) collective-permute-start(bf16[512,512]{1,0:T(8,128)(2,1)S(1)} %get-tuple-element.55), channel_id=1, source_target_pairs={{0,30},{1,31},{2,4},{3,5},{4,2},{5,3},{6,8},{7,9},{8,6},{9,7},{10,... | collective-permute-start | bytes 1572872 | tf_op jit(solution)/shard_map/ppermute | solution.py:25
  39.6 16.1 %collective-permute-start.4 = (bf16[512,512]{1,0:T(8,128)(2,1)S(1)}, bf16[512,512]{1,0:T(8,128)(2,1)S(1)}, u32[]{:S(2)}, u32[]{:S(2)}) collective-permute-start(bf16[512,512]{1,0:T(8,128)(2,1)S(1)} %get-tuple-element.50), channel_id=1, source_target_pairs={{0,2},{1,3},{2,0},{3,1},{4,6},{5,7},{6,4},{7,5},{8,10},{9,11},{10,... | collective-permute-start | bytes 1572872 | tf_op jit(solution)/shard_map/ppermute | solution.py:25
  39.7 9.4 %copy-start.7 = (f32[512]{0:T(512)S(1)}, f32[512]{0:T(512)}, u32[]{:S(2)}) copy-start(f32[512]{0:T(512)} %param.15) | copy-start | bytes 6148
  39.7 22.3 %collective-permute-start.5 = (bf16[512,512]{1,0:T(8,128)(2,1)S(1)}, bf16[512,512]{1,0:T(8,128)(2,1)S(1)}, u32[]{:S(2)}, u32[]{:S(2)}) collective-permute-start(bf16[512,512]{1,0:T(8,128)(2,1)S(1)} %get-tuple-element.51), channel_id=1, source_target_pairs={{0,30},{1,31},{2,4},{3,5},{4,2},{5,3},{6,8},{7,9},{8,6},{9,7},{10,... | collective-permute-start | bytes 1572872 | tf_op jit(solution)/shard_map/ppermute | solution.py:25
  45.9 5.6 %copy-start.2 = (bf16[512,1024]{1,0:T(8,128)(2,1)S(1)}, bf16[512,1024]{1,0:T(8,128)(2,1)}, u32[]{:S(2)}) copy-start(bf16[512,1024]{1,0:T(8,128)(2,1)} %point_ref.7) | copy-start | bytes 3145732
  45.9 5.6 %copy-start.5 = (f32[1024]{0:T(1024)S(1)}, f32[1024]{0:T(1024)}, u32[]{:S(2)}) copy-start(f32[1024]{0:T(1024)} %param.17) | copy-start | bytes 12292
  45.9 19.5 %collective-permute-start.2 = (bf16[512,512]{1,0:T(8,128)(2,1)S(1)}, bf16[512,512]{1,0:T(8,128)(2,1)S(1)}, u32[]{:S(2)}, u32[]{:S(2)}) collective-permute-start(bf16[512,512]{1,0:T(8,128)(2,1)S(1)} %get-tuple-element.46), channel_id=1, source_target_pairs={{0,2},{1,3},{2,0},{3,1},{4,6},{5,7},{6,4},{7,5},{8,10},{9,11},{10,... | collective-permute-start | bytes 1572872 | tf_op jit(solution)/shard_map/ppermute | solution.py:25
  46.0 26.2 %collective-permute-start.3 = (bf16[512,512]{1,0:T(8,128)(2,1)S(1)}, bf16[512,512]{1,0:T(8,128)(2,1)S(1)}, u32[]{:S(2)}, u32[]{:S(2)}) collective-permute-start(bf16[512,512]{1,0:T(8,128)(2,1)S(1)} %get-tuple-element.47), channel_id=1, source_target_pairs={{0,30},{1,31},{2,4},{3,5},{4,2},{5,3},{6,8},{7,9},{8,6},{9,7},{10,... | collective-permute-start | bytes 1572872 | tf_op jit(solution)/shard_map/ppermute | solution.py:25

commit v3 on v2

--- a/solution.py
+++ b/solution.py
@@ -68,24 +68,26 @@
 
     def body(x_hbm, taps_hbm, act_ref, product_ref, x_own, tap_own, sems):
         which = tap + odd_position() * (2 - 2 * tap)
-        half = size // 2
-        rows = quarter_rows(quarter, size)
-        copies = [
-            pltpu.make_async_copy(x_hbm.at[rows], x_own, sems.at[0]),
-            pltpu.make_async_copy(taps_hbm.at[which], tap_own, sems.at[1]),
-        ]
+        piece = size // 4
+        start = quarter_rows(quarter, size).start
+        copies = []
+        for k in range(4):
+            rows = pl.ds(pl.multiple_of(start + k * piece, piece), piece)
+            copies.append(pltpu.make_async_copy(x_hbm.at[rows], x_own.at[pl.ds(k * piece, piece)], sems.at[k]))
+        copies.insert(2, pltpu.make_async_copy(taps_hbm.at[which], tap_own, sems.at[4]))
         for copy in copies:
             copy.start()
-        copies[0].wait()
-        for k in range(2):
-            part = pl.ds(k * half, half)
+        tap_copy = copies.pop(2)
+        for k in range(4):
+            copies[k].wait()
+            part = pl.ds(k * piece, piece)
             act_ref[part, :] = gelu(x_own[part, :].astype(F32)).astype(BF16)
-        copies[1].wait()
+        tap_copy.wait()
         product_ref[...] = dot(act_ref[...], tap_own[...]).astype(BF16)
 
     return call(
         body, f"rim{quarter}", [shape(size, c), shape(size, m)], (x, taps), 2 * size * c * m,
-        [pltpu.VMEM((size, c), BF16), pltpu.VMEM((c, m), BF16), pltpu.SemaphoreType.DMA((2,))],
+        [pltpu.VMEM((size, c), BF16), pltpu.VMEM((c, m), BF16), pltpu.SemaphoreType.DMA((5,))],
         specs=[HBM, HBM],
     )
 
@@ -210,29 +212,31 @@
     tower_input = pltpu.with_memory_space_constraint(tower_input, pltpu.HBM)
     rim_taps = pltpu.with_memory_space_constraint(first_conv_taps, pltpu.HBM)
     act0, to_pair = rim(tower_input, rim_taps, 0)
-    later, to_pair = lax.optimization_barrier((tower_input, to_pair))
     from_pair = swap(to_pair, lambda i: i % 2 == 1, 1)
+
+    def send(products):
+        return (
+            swap(products[1], lambda i: i // 2 % 2 == 1, 2),
+            swap(products[0], lambda i: i // 2 % 2 == 0, 2),
+        )
+
+    act1, act2, one1, far1, *products1 = layer(tower_input, 1, (act0, None, None), None, near, fresh=True)
+    later, *products1 = lax.optimization_barrier((tower_input, *products1))
+    sides1 = send(products1)
     act3, to_partner = rim(later, rim_taps, 3)
     from_partner = swap(to_partner, lambda i: i % 2 == 0, 1)
-
-    def send(products):
-        return (
-            swap(products[0], lambda i: i // 2 % 2 == 0, 2),
-            swap(products[1], lambda i: i // 2 % 2 == 1, 2),
-        )
-
-    act1, act2, one1, far1, *products1 = layer(tower_input, 1, (act0, None, None), None, near, fresh=True)
-    sides1 = send(products1)
     one2, far2, *products2 = layer(tower_input, 2, (act1, act2, act3), None, near)
     sides2 = send(products2)
+    one0, far0, *products0 = layer(tower_input, 0, (None, act0, act1), from_pair, near)
+    sides0 = send(products0)
     one3, far3, *products3 = layer(tower_input, 3, (act2, act3, None), from_partner, near)
     sides3 = send(products3)
-    one0, far0, *products0 = layer(tower_input, 0, (None, act0, act1), from_pair, near)
-    sides0 = send(products0)
-
-    centres = centre((far1, far2, far3, far0), second_conv_taps, second_conv_bias[None, :])
+
+    centres = centre((far1, far2, far0, far3), second_conv_taps, second_conv_bias[None, :])
     out = None
-    for quarter, total, sides, one in zip((1, 2, 3, 0), centres, (sides1, sides2, sides3, sides0), (one1, one2, one3, one0)):
+    for quarter, total, sides, one in zip(
+        (1, 2, 0, 3), centres, (sides1, sides2, sides0, sides3), (one1, one2, one0, one3)
+    ):
         out = finish(quarter, total, *sides, one, second_point_weight, second_point_bias[None, :], out)
     return out
 

time: 74.6 us -> 68.3 us (0.916)
  waiting for transfers between devices: 22 us -> 16.1 us
    ppermute x10, waiting for transfers between devices: 22 us -> 16.1 us  [swap(): return lax.ppermute(value, 'seq', sorted(pairs))]
  transfers between devices with their start and end apart: 10 -> 10, of which waited for: 5 -> 4; matrix products, arithmetic and copies ran while one was open for 0% -> 0% of each run, Pallas kernels for 39% -> 43%
where the time goes in v3:
time: 68.3 us; the launch traced here: 67.9 us
  Pallas kernels  33.6 us (49%)
  starting transfers between devices  17.8 us (26%)
  waiting for transfers between devices  16.1 us (24%)
    pallas_call x11, Pallas kernels, call(): pl.pallas_call(body, in_specs=specs, out_specs=[VMEM] * len(out_shape) if...  33.6 us
    ppermute x10, starting transfers between devices, swap(): return lax.ppermute(value, 'seq', sorted(pairs))  17.8 us
    ppermute x10, waiting for transfers between devices, swap(): return lax.ppermute(value, 'seq', sorted(pairs))  16.1 us
  transfers between devices with their start and end apart: 10, of which 4 were waited for; matrix products, arithmetic and copies ran while one was open for 0% of the time, Pallas kernels for 43%

profile of v3, /device:TPU:0, one launch (start us, length us, event | category | flops | bytes accessed | tf_op | source)
XLA Modules:
  0.0 67.9 jit_solution(5510793747829808310)
XLA Ops:
  0.0 0.0 copy-start
  0.0 0.0 copy-start.2
  0.0 0.0 copy-start.4
  0.0 0.0 copy-start.5
  0.0 0.0 copy-start.7
  0.0 2.7 %rim0.1 = (bf16[512,1024]{1,0:T(8,128)(2,1)S(1)}, bf16[512,512]{1,0:T(8,128)(2,1)S(1)}) custom-call(bf16[2048,1024]{1,0:T(8,128)(2,1)} %refs_0_.7, bf16[3,1024,512]{2,1,0:T(8,128)(2,1)} %refs_4_.8), custom_call_target="tpu_custom_call" | custom-call | flops 536870912 | bytes 7340032 | tf_op jit(solution)/shard_map/rim0/pallas_call | solution.py:48
  2.7 6.7 %collective-permute-start = (bf16[512,512]{1,0:T(8,128)(2,1)S(1)}, bf16[512,512]{1,0:T(8,128)(2,1)S(1)}, u32[]{:S(2)}, u32[]{:S(2)}) collective-permute-start(bf16[512,512]{1,0:T(8,128)(2,1)S(1)} %get-tuple-element.43), channel_id=1, source_target_pairs={{0,31},{1,2},{2,1},{3,4},{4,3},{5,6},{6,5},{7,8},{8,7},{9,10},{10,... | collective-permute-start | bytes 1572872 | tf_op jit(solution)/shard_map/ppermute | solution.py:25
  9.5 0.0 copy-done
  9.5 0.0 copy-done.2
  9.5 0.0 copy-done.4
  9.5 0.0 copy-done.5
  9.5 0.0 copy-done.7
  9.5 6.0 %layer1.1 = (bf16[512,1024]{1,0:T(8,128)(2,1)S(1)}, bf16[512,1024]{1,0:T(8,128)(2,1)S(1)}, bf16[512,1024]{1,0:T(8,128)(2,1)S(1)}, bf16[512,1024]{1,0:T(8,128)(2,...) custom-call(bf16[2048,1024]{1,0:T(8,128)(2,1)} %refs_0_.7, ...), custom_call_target="tpu_custom_call" | custom-call | flops 3221225472 | bytes 12589056 | tf_op jit(solution)/shard_map/layer1/pallas_call | solution.py:48
  15.5 0.0 copy-start.1
  15.5 0.9 %collective-permute-start.8 = (bf16[512,512]{1,0:T(8,128)(2,1)S(1)}, bf16[512,512]{1,0:T(8,128)(2,1)S(1)}, u32[]{:S(2)}, u32[]{:S(2)}) collective-permute-start(bf16[512,512]{1,0:T(8,128)(2,1)S(1)} %get-tuple-element.60), channel_id=1, source_target_pairs={{0,30},{1,31},{2,4},{3,5},{4,2},{5,3},{6,8},{7,9},{8,6},{9,7},{10,... | collective-permute-start | bytes 1572872 | tf_op jit(solution)/shard_map/ppermute | solution.py:25
  16.4 0.0 collective-permute-start.9
  16.4 2.6 %rim3.1 = (bf16[512,1024]{1,0:T(8,128)(2,1)S(1)}, bf16[512,512]{1,0:T(8,128)(2,1)S(1)}) custom-call(bf16[2048,1024]{1,0:T(8,128)(2,1)} %refs_0_.7, bf16[3,1024,512]{2,1,0:T(8,128)(2,1)} %refs_4_.8), custom_call_target="tpu_custom_call" | custom-call | flops 536870912 | bytes 7340032 | tf_op jit(solution)/shard_map/rim3/pallas_call | solution.py:48
  19.0 0.6 collective-permute-start.1
  19.6 0.0 copy-done.1
  19.6 5.0 %layer2.1 = (bf16[512,1024]{1,0:T(8,128)(2,1)S(1)}, bf16[512,1024]{1,0:T(8,128)(2,1)S(1)}, bf16[512,512]{1,0:T(8,128)(2,1)S(1)}, bf16[512,512]{1,0:T(8,128)(2,1)S(1)}) custom-call(bf16[2048,1024]{1,0:T(8,128)(2,1)} %refs_0_.7, bf16[512,1024]{1,0:T(8,128)(2,1)S(1)} %get-tuple-element.36.refs_1_.refs_2_, ...), custom_call_target="tpu_custom_call" | custom-call | flops 3221225472 | bytes 14686208 | tf_op jit(solution)/shard_map/layer2/pallas_call | solution.py:48
  24.6 4.0 %collective-permute-start.6 = (bf16[512,512]{1,0:T(8,128)(2,1)S(1)}, bf16[512,512]{1,0:T(8,128)(2,1)S(1)}, u32[]{:S(2)}, u32[]{:S(2)}) collective-permute-start(bf16[512,512]{1,0:T(8,128)(2,1)S(1)} %get-tuple-element.56), channel_id=1, source_target_pairs={{0,30},{1,31},{2,4},{3,5},{4,2},{5,3},{6,8},{7,9},{8,6},{9,7},{10,... | collective-permute-start | bytes 1572872 | tf_op jit(solution)/shard_map/ppermute | solution.py:25
  28.6 0.0 collective-permute-done.refs_3_
  28.6 0.0 collective-permute-start.7
  28.6 3.8 %layer0.1 = (bf16[512,1024]{1,0:T(8,128)(2,1)S(1)}, bf16[512,1024]{1,0:T(8,128)(2,1)S(1)}, bf16[512,512]{1,0:T(8,128)(2,1)S(1)}, bf16[512,512]{1,0:T(8,128)(2,1)S(1)}) custom-call(bf16[2048,1024]{1,0:T(8,128)(2,1)} %refs_0_.7, bf16[512,1024]{1,0:T(8,128)(2,1)S(1)} %get-tuple-element.34.refs_1_, bf16[512,1024]{1,0:T(8,128)(2,1)S(1)} %get-tuple-element.36.refs_1_.refs_2_, ...), custom_call_target="tpu_custom_call" | custom-call | flops 3221225472 | bytes 14161920 | tf_op jit(solution)/shard_map/layer0/pallas_call | solution.py:48
  32.4 1.3 %collective-permute-done.8.one_side_ref = bf16[512,512]{1,0:T(8,128)(2,1)S(1)} collective-permute-done((bf16[512,512]{1,0:T(8,128)(2,1)S(1)}, bf16[512,512]{1,0:T(8,128)(2,1)S(1)}, u32[]{:S(2)}, u32[]{:S(2)}) %collective-permute-start.8) | collective-permute-done | bytes 524320 | tf_op jit(solution)/shard_map/ppermute | solution.py:25
  33.7 5.1 %collective-permute-start.4 = (bf16[512,512]{1,0:T(8,128)(2,1)S(1)}, bf16[512,512]{1,0:T(8,128)(2,1)S(1)}, u32[]{:S(2)}, u32[]{:S(2)}) collective-permute-start(bf16[512,512]{1,0:T(8,128)(2,1)S(1)} %get-tuple-element.52), channel_id=1, source_target_pairs={{0,30},{1,31},{2,4},{3,5},{4,2},{5,3},{6,8},{7,9},{8,6},{9,7},{10,... | collective-permute-start | bytes 1572872 | tf_op jit(solution)/shard_map/ppermute | solution.py:25
  38.8 0.0 collective-permute-done.1.refs_3_
  38.8 0.0 copy-start.8
  38.8 0.0 collective-permute-start.5
  38.8 4.0 %layer3.1 = (bf16[512,1024]{1,0:T(8,128)(2,1)S(1)}, bf16[512,1024]{1,0:T(8,128)(2,1)S(1)}, bf16[512,512]{1,0:T(8,128)(2,1)S(1)}, bf16[512,512]{1,0:T(8,128)(2,1)S(1)}) custom-call(bf16[2048,1024]{1,0:T(8,128)(2,1)} %refs_0_.7, bf16[512,1024]{1,0:T(8,128)(2,1)S(1)} %get-tuple-element.37.refs_2_.refs_1_, ...), custom_call_target="tpu_custom_call" | custom-call | flops 3221225472 | bytes 14161920 | tf_op jit(solution)/shard_map/layer3/pallas_call | solution.py:48
  42.8 0.0 copy-start.3
  42.8 0.0 copy-start.6
  42.8 0.0 collective-permute-done.9.other_side_ref
  42.8 0.3 collective-permute-start.2
  43.2 1.8 %collective-permute-done.6.one_side_ref = bf16[512,512]{1,0:T(8,128)(2,1)S(1)} collective-permute-done((bf16[512,512]{1,0:T(8,128)(2,1)S(1)}, bf16[512,512]{1,0:T(8,128)(2,1)S(1)}, u32[]{:S(2)}, u32[]{:S(2)}) %collective-permute-start.6) | collective-permute-done | bytes 524320 | tf_op jit(solution)/shard_map/ppermute | solution.py:25
  45.0 0.1 collective-permute-start.3
  45.0 0.0 copy-done.8
  45.0 2.3 %centre.1 = (f32[512,512]{1,0:T(8,128)S(1)}, f32[512,512]{1,0:T(8,128)S(1)}, f32[512,512]{1,0:T(8,128)S(1)}, f32[512,512]{1,0:T(8,128)S(1)}) custom-call(bf16[512,1024]{1,0:T(8,128)(2,1)S(1)} %get-tuple-element.35.refs_0_, bf16[512,1024]{1,0:T(8,128)(2,1)S(1)} %get-tuple-element.42.refs_1_, bf16[512,1024]{1,0:T(8,128)(2,1)S(1)} %get-tuple-element.44.refs_2_, ...), custom_call_target="tpu_custom_call" | custom-call | flops 2147483648 | bytes 7342080 | tf_op jit(solution)/shard_map/centre/pallas_call | solution.py:48
  47.4 0.0 copy-done.3
  47.4 0.0 copy-done.6
  47.4 1.8 %finish1.1.rest_0_ = bf16[2048,1024]{1,0:T(8,128)(2,1)} custom-call(f32[512,512]{1,0:T(8,128)S(1)} %get-tuple-element.59.centre_ref, bf16[512,512]{1,0:T(8,128)(2,1)S(1)} %collective-permute-done.8.one_side_ref, bf16[512,512]{1,0:T(8,128)(2,1)S(1)} %collective-permute-done.9.other_side_ref, bf16[512,1024]{1,0:T(8,128)(2,1)S(1)} %get-tuple-element.62.one_ref, ...), custom_call_target="tpu_custom_call" | custom-call | flops 536870912 | bytes 4198400 | tf_op jit(solution)/shard_map/finish1/pallas_call | solution.py:48
  49.2 0.0 collective-permute-done.7.other_side_ref
  49.3 1.8 %finish2.1.rest_0_ = bf16[2048,1024]{1,0:T(8,128)(2,1)} custom-call(f32[512,512]{1,0:T(8,128)S(1)} %get-tuple-element.55.centre_ref, bf16[512,512]{1,0:T(8,128)(2,1)S(1)} %collective-permute-done.6.one_side_ref, bf16[512,512]{1,0:T(8,128)(2,1)S(1)} %collective-permute-done.7.other_side_ref, ...), custom_call_target="tpu_custom_call", output_to_operand_aliasing={{}: (6, {})} | custom-call | flops 536870912 | bytes 8392704 | tf_op jit(solution)/shard_map/finish2/pallas_call | solution.py:48
  51.1 5.1 %collective-permute-done.4.one_side_ref = bf16[512,512]{1,0:T(8,128)(2,1)S(1)} collective-permute-done((bf16[512,512]{1,0:T(8,128)(2,1)S(1)}, bf16[512,512]{1,0:T(8,128)(2,1)S(1)}, u32[]{:S(2)}, u32[]{:S(2)}) %collective-permute-start.4) | collective-permute-done | bytes 524320 | tf_op jit(solution)/shard_map/ppermute | solution.py:25
  56.2 0.0 collective-permute-done.5.other_side_ref
  56.2 1.8 %finish0.1.rest_0_ = bf16[2048,1024]{1,0:T(8,128)(2,1)} custom-call(f32[512,512]{1,0:T(8,128)S(1)} %get-tuple-element.51.centre_ref, bf16[512,512]{1,0:T(8,128)(2,1)S(1)} %collective-permute-done.4.one_side_ref, bf16[512,512]{1,0:T(8,128)(2,1)S(1)} %collective-permute-done.5.other_side_ref, ...), custom_call_target="tpu_custom_call", output_to_operand_aliasing={{}: (6, {})} | custom-call | flops 536870912 | bytes 8392704 | tf_op jit(solution)/shard_map/finish0/pallas_call | solution.py:48
  58.0 7.9 %collective-permute-done.2.one_side_ref = bf16[512,512]{1,0:T(8,128)(2,1)S(1)} collective-permute-done((bf16[512,512]{1,0:T(8,128)(2,1)S(1)}, bf16[512,512]{1,0:T(8,128)(2,1)S(1)}, u32[]{:S(2)}, u32[]{:S(2)}) %collective-permute-start.2) | collective-permute-done | bytes 524320 | tf_op jit(solution)/shard_map/ppermute | solution.py:25
  66.0 0.0 collective-permute-done.3.other_side_ref
  66.0 1.8 %finish3.1 = bf16[2048,1024]{1,0:T(8,128)(2,1)} custom-call(f32[512,512]{1,0:T(8,128)S(1)} %get-tuple-element.47.centre_ref, bf16[512,512]{1,0:T(8,128)(2,1)S(1)} %collective-permute-done.2.one_side_ref, bf16[512,512]{1,0:T(8,128)(2,1)S(1)} %collective-permute-done.3.other_side_ref, ...), custom_call_target="tpu_custom_call", output_to_operand_aliasing={{}: (6, {})} | custom-call | flops 536870912 | bytes 8392704 | tf_op jit(solution)/shard_map/finish3/pallas_call | solution.py:48
Async XLA Ops:
  0.0 9.5 %copy-start = (bf16[3,1024,512]{2,1,0:T(8,128)(2,1)S(1)}, bf16[3,1024,512]{2,1,0:T(8,128)(2,1)}, u32[]{:S(2)}) copy-start(bf16[3,1024,512]{2,1,0:T(8,128)(2,1)} %refs_4_.8) | copy-start | bytes 9437188
  0.0 9.5 %copy-start.2 = (bf16[3,1024,512]{2,1,0:T(8,128)(2,1)S(1)}, bf16[3,1024,512]{2,1,0:T(8,128)(2,1)}, u32[]{:S(2)}) copy-start(bf16[3,1024,512]{2,1,0:T(8,128)(2,1)} %refs_4_.9) | copy-start | bytes 9437188
  0.0 9.5 %copy-start.4 = (bf16[512,1024]{1,0:T(8,128)(2,1)S(1)}, bf16[512,1024]{1,0:T(8,128)(2,1)}, u32[]{:S(2)}) copy-start(bf16[512,1024]{1,0:T(8,128)(2,1)} %refs_6_.7) | copy-start | bytes 3145732
  0.0 9.5 %copy-start.5 = (f32[1024]{0:T(1024)S(1)}, f32[1024]{0:T(1024)}, u32[]{:S(2)}) copy-start(f32[1024]{0:T(1024)} %param.13) | copy-start | bytes 12292
  0.0 9.5 %copy-start.7 = (f32[512]{0:T(512)S(1)}, f32[512]{0:T(512)}, u32[]{:S(2)}) copy-start(f32[512]{0:T(512)} %param.11) | copy-start | bytes 6148
  2.7 25.9 %collective-permute-start = (bf16[512,512]{1,0:T(8,128)(2,1)S(1)}, bf16[512,512]{1,0:T(8,128)(2,1)S(1)}, u32[]{:S(2)}, u32[]{:S(2)}) collective-permute-start(bf16[512,512]{1,0:T(8,128)(2,1)S(1)} %get-tuple-element.43), channel_id=1, source_target_pairs={{0,31},{1,2},{2,1},{3,4},{4,3},{5,6},{6,5},{7,8},{8,7},{9,10},{10,... | collective-permute-start | bytes 1572872 | tf_op jit(solution)/shard_map/ppermute | solution.py:25
  15.5 4.1 %copy-start.1 = (bf16[3,1024,512]{2,1,0:T(8,128)(2,1)S(1)}, bf16[3,1024,512]{2,1,0:T(8,128)(2,1)}, u32[]{:S(2)}) copy-start(bf16[3,1024,512]{2,1,0:T(8,128)(2,1)} %refs_4_.8) | copy-start | bytes 9437188
  15.5 18.2 %collective-permute-start.8 = (bf16[512,512]{1,0:T(8,128)(2,1)S(1)}, bf16[512,512]{1,0:T(8,128)(2,1)S(1)}, u32[]{:S(2)}, u32[]{:S(2)}) collective-permute-start(bf16[512,512]{1,0:T(8,128)(2,1)S(1)} %get-tuple-element.60), channel_id=1, source_target_pairs={{0,30},{1,31},{2,4},{3,5},{4,2},{5,3},{6,8},{7,9},{8,6},{9,7},{10,... | collective-permute-start | bytes 1572872 | tf_op jit(solution)/shard_map/ppermute | solution.py:25
  16.4 26.5 %collective-permute-start.9 = (bf16[512,512]{1,0:T(8,128)(2,1)S(1)}, bf16[512,512]{1,0:T(8,128)(2,1)S(1)}, u32[]{:S(2)}, u32[]{:S(2)}) collective-permute-start(bf16[512,512]{1,0:T(8,128)(2,1)S(1)} %get-tuple-element.61), channel_id=1, source_target_pairs={{0,2},{1,3},{2,0},{3,1},{4,6},{5,7},{6,4},{7,5},{8,10},{9,11},{10,... | collective-permute-start | bytes 1572872 | tf_op jit(solution)/shard_map/ppermute | solution.py:25
  19.0 19.9 %collective-permute-start.1 = (bf16[512,512]{1,0:T(8,128)(2,1)S(1)}, bf16[512,512]{1,0:T(8,128)(2,1)S(1)}, u32[]{:S(2)}, u32[]{:S(2)}) collective-permute-start(bf16[512,512]{1,0:T(8,128)(2,1)S(1)} %get-tuple-element.45), channel_id=1, source_target_pairs={{0,1},{1,0},{2,3},{3,2},{4,5},{5,4},{6,7},{7,6},{8,9},{9,8},{10,11... | collective-permute-start | bytes 1572872 | tf_op jit(solution)/shard_map/ppermute | solution.py:25
  24.6 20.4 %collective-permute-start.6 = (bf16[512,512]{1,0:T(8,128)(2,1)S(1)}, bf16[512,512]{1,0:T(8,128)(2,1)S(1)}, u32[]{:S(2)}, u32[]{:S(2)}) collective-permute-start(bf16[512,512]{1,0:T(8,128)(2,1)S(1)} %get-tuple-element.56), channel_id=1, source_target_pairs={{0,30},{1,31},{2,4},{3,5},{4,2},{5,3},{6,8},{7,9},{8,6},{9,7},{10,... | collective-permute-start | bytes 1572872 | tf_op jit(solution)/shard_map/ppermute | solution.py:25
  28.6 20.6 %collective-permute-start.7 = (bf16[512,512]{1,0:T(8,128)(2,1)S(1)}, bf16[512,512]{1,0:T(8,128)(2,1)S(1)}, u32[]{:S(2)}, u32[]{:S(2)}) collective-permute-start(bf16[512,512]{1,0:T(8,128)(2,1)S(1)} %get-tuple-element.57), channel_id=1, source_target_pairs={{0,2},{1,3},{2,0},{3,1},{4,6},{5,7},{6,4},{7,5},{8,10},{9,11},{10,... | collective-permute-start | bytes 1572872 | tf_op jit(solution)/shard_map/ppermute | solution.py:25
  33.7 22.5 %collective-permute-start.4 = (bf16[512,512]{1,0:T(8,128)(2,1)S(1)}, bf16[512,512]{1,0:T(8,128)(2,1)S(1)}, u32[]{:S(2)}, u32[]{:S(2)}) collective-permute-start(bf16[512,512]{1,0:T(8,128)(2,1)S(1)} %get-tuple-element.52), channel_id=1, source_target_pairs={{0,30},{1,31},{2,4},{3,5},{4,2},{5,3},{6,8},{7,9},{8,6},{9,7},{10,... | collective-permute-start | bytes 1572872 | tf_op jit(solution)/shard_map/ppermute | solution.py:25
  38.8 6.2 %copy-start.8 = (f32[512]{0:T(512)S(1)}, f32[512]{0:T(512)}, u32[]{:S(2)}) copy-start(f32[512]{0:T(512)} %param.15) | copy-start | bytes 6148
  38.8 17.4 %collective-permute-start.5 = (bf16[512,512]{1,0:T(8,128)(2,1)S(1)}, bf16[512,512]{1,0:T(8,128)(2,1)S(1)}, u32[]{:S(2)}, u32[]{:S(2)}) collective-permute-start(bf16[512,512]{1,0:T(8,128)(2,1)S(1)} %get-tuple-element.53), channel_id=1, source_target_pairs={{0,2},{1,3},{2,0},{3,1},{4,6},{5,7},{6,4},{7,5},{8,10},{9,11},{10,... | collective-permute-start | bytes 1572872 | tf_op jit(solution)/shard_map/ppermute | solution.py:25
  42.8 4.6 %copy-start.3 = (bf16[512,1024]{1,0:T(8,128)(2,1)S(1)}, bf16[512,1024]{1,0:T(8,128)(2,1)}, u32[]{:S(2)}) copy-start(bf16[512,1024]{1,0:T(8,128)(2,1)} %point_ref.7) | copy-start | bytes 3145732
  42.8 4.6 %copy-start.6 = (f32[1024]{0:T(1024)S(1)}, f32[1024]{0:T(1024)}, u32[]{:S(2)}) copy-start(f32[1024]{0:T(1024)} %param.17) | copy-start | bytes 12292
  42.8 23.1 %collective-permute-start.2 = (bf16[512,512]{1,0:T(8,128)(2,1)S(1)}, bf16[512,512]{1,0:T(8,128)(2,1)S(1)}, u32[]{:S(2)}, u32[]{:S(2)}) collective-permute-start(bf16[512,512]{1,0:T(8,128)(2,1)S(1)} %get-tuple-element.48), channel_id=1, source_target_pairs={{0,30},{1,31},{2,4},{3,5},{4,2},{5,3},{6,8},{7,9},{8,6},{9,7},{10,... | collective-permute-start | bytes 1572872 | tf_op jit(solution)/shard_map/ppermute | solution.py:25
  45.0 21.0 %collective-permute-start.3 = (bf16[512,512]{1,0:T(8,128)(2,1)S(1)}, bf16[512,512]{1,0:T(8,128)(2,1)S(1)}, u32[]{:S(2)}, u32[]{:S(2)}) collective-permute-start(bf16[512,512]{1,0:T(8,128)(2,1)S(1)} %get-tuple-element.49), channel_id=1, source_target_pairs={{0,2},{1,3},{2,0},{3,1},{4,6},{5,7},{6,4},{7,5},{8,10},{9,11},{10,... | collective-permute-start | bytes 1572872 | tf_op jit(solution)/shard_map/ppermute | solution.py:25

commit v4 on v3

v4 whole, which is shorter than its diff:
```python
import math

import jax
import jax.numpy as jnp
from jax import lax
from jax.experimental import pallas as pl
from jax.experimental.pallas import tpu as pltpu
from jax.sharding import PartitionSpec as P

LIMIT = 16 * 1024 * 1024
VMEM = pl.BlockSpec(memory_space=pltpu.VMEM)
ANY = pl.BlockSpec(memory_space=pl.ANY)
HBM = pl.BlockSpec(memory_space=pltpu.HBM)
SLOPE = math.sqrt(2.0 / math.pi)
LAST_PIECE = 128
BF16 = jnp.bfloat16
F32 = jnp.float32


def swap(value, first, step):
    size = lax.axis_size("seq")
    pairs = []
    for i in range(size):
        if first(i):
            j = (i + step) % size
            pairs += [(i, j), (j, i)]
    return lax.ppermute(value, "seq", sorted(pairs))


def gelu(v):
    half = 0.5 * v
    return half + half * jnp.tanh(v * (SLOPE + (SLOPE * 0.044715) * (v * v)))


def dot(a, b):
    return jnp.dot(a, b, preferred_element_type=F32)


def odd_position():
    return lax.rem(lax.axis_index("seq"), 2)


def quarter_rows(quarter, size):
    at = quarter + odd_position() * (3 - 2 * quarter)
    return pl.ds(pl.multiple_of(at * size, size), size)


def call(body, name, out_shape, args, flops, scratch, aliases=None, out_specs=None, specs=None):
    moved = sum(a.size * a.dtype.itemsize for a in args)
    return pl.pallas_call(
        body,
        in_specs=specs,
        out_specs=[VMEM] * len(out_shape) if out_specs is None else out_specs,
        out_shape=out_shape,
        scratch_shapes=scratch,
        input_output_aliases=aliases or {},
        compiler_params=pltpu.CompilerParams(vmem_limit_bytes=LIMIT),
        cost_estimate=pl.CostEstimate(flops=flops, bytes_accessed=moved, transcendentals=0),
        name=name,
    )(*args)


def shape(rows, columns, dtype=BF16):
    return jax.ShapeDtypeStruct((rows, columns), dtype)


def rim(x, taps, quarter):
    size, (c, m) = x.shape[0] // 4, taps.shape[1:]
    half = size // 2
    top, bottom = pl.ds(0, half), pl.ds(half, half)
    tap = 2 if quarter == 0 else 0

    def body(x_ref, taps_ref, act_ref, product_ref, x_own, tap_own, sems):
        which = tap + odd_position() * (2 - 2 * tap)
        start = quarter_rows(quarter, size).start

        def rows(k):
            return pl.ds(pl.multiple_of(start + k * half, half), half)

        first, tap_copy, second = (
            pltpu.make_async_copy(x_ref.at[rows(0)], x_own.at[top], sems.at[0]),
            pltpu.make_async_copy(taps_ref.at[which], tap_own, sems.at[1]),
            pltpu.make_async_copy(x_ref.at[rows(1)], x_own.at[bottom], sems.at[2]),
        )
        for copy in (first, tap_copy, second):
            copy.start()
        first.wait()
        act_ref[top, :] = gelu(x_own[top, :].astype(F32)).astype(BF16)
        tap_copy.wait()
        second.wait()
        product_ref[top, :] = dot(act_ref[top, :], tap_own[...]).astype(BF16)
        act_ref[bottom, :] = gelu(x_own[bottom, :].astype(F32)).astype(BF16)
        product_ref[bottom, :] = dot(act_ref[bottom, :], tap_own[...]).astype(BF16)

    return call(
        body, f"rim{quarter}", [shape(size, c), shape(size, m)], (x, taps), 2 * size * c * m,
        [pltpu.VMEM((size, c), BF16), pltpu.VMEM((c, m), BF16), pltpu.SemaphoreType.DMA((3,))],
        specs=[HBM] * 2,
    )


def after_total(total, x, point, bias_point, outer, one_ref, act_ref, product_refs):
    mid = gelu(total).astype(BF16)
    one = (x.astype(F32) + dot(mid, point[...]) + bias_point[...]).astype(BF16)
    one_ref[...] = one
    act = gelu(one.astype(F32)).astype(BF16)
    act_ref[...] = act
    odd_pair = lax.rem(lax.div(lax.axis_index("seq"), 2), 2)
    for tap, pieces in zip((2 * odd_pair, 2 - 2 * odd_pair), product_refs):
        product = dot(act, outer[tap]).astype(BF16)
        at = 0
        for ref in pieces:
            ref[...] = product[at : at + ref.shape[0], :]
            at += ref.shape[0]


def layer(x, quarter, acts, arrived, weights, pieces, fresh=False):
    taps, bias_conv, point, bias_point, outer = weights
    size, (c, m) = x.shape[0] // 4, taps.shape[1:]
    given = [a for a in acts if a is not None]
    known = [a is not None for a in acts]
    loads = (quarter, quarter + 1) if fresh else (quarter,)
    n = len(pieces)

    def body(*refs):
        refs = list(refs)
        x_ref = refs.pop(0)
        sources = [refs.pop(0) if k else None for k in known]
        arrived_ref = None if arrived is None else refs.pop(0)
        taps_ref, bias_conv_ref, point_ref, bias_point_ref, outer_ref = refs[:5]
        refs = refs[5:]
        made = [refs.pop(0), refs.pop(0)] if fresh else []
        one_ref, act_ref = refs[:2]
        product_refs = refs[2 : 2 + n], refs[2 + n : 2 + 2 * n]
        x_own, sems = refs[2 + 2 * n :]
        odd = odd_position()
        copies = [
            pltpu.make_async_copy(x_ref.at[quarter_rows(q, size)], x_own.at[k], sems.at[k]) for k, q in enumerate(loads)
        ]
        for copy in copies:
            copy.start()
        total = None if arrived is None else arrived_ref[...].astype(F32)
        for k, source in enumerate(sources):
            if fresh and k > 0:
                source = made[k - 1]
                copies[k - 1].wait()
                source[...] = gelu(x_own[k - 1].astype(F32)).astype(BF16)
            if source is not None:
                term = dot(source[...], taps_ref[k + odd * (2 - 2 * k)])
                total = term if total is None else total + term
        if not fresh:
            copies[0].wait()
        after_total(
            total + bias_conv_ref[...], x_own[0], point_ref, bias_point_ref, outer_ref, one_ref, act_ref, product_refs
        )

    args = [x] + given + ([] if arrived is None else [arrived]) + list(weights)
    outs = ([shape(size, c)] * 2 if fresh else []) + [shape(size, c)] * 2 + [shape(rows, m) for rows in pieces] * 2
    results = call(
        body, f"layer{quarter}", outs, args, 12 * size * c * m,
        [pltpu.VMEM((len(loads), size, c), BF16), pltpu.SemaphoreType.DMA((len(loads),))],
        specs=[HBM] + [VMEM] * (len(args) - 1),
    )
    return *results[: -2 * n], list(zip(results[-2 * n : -n], results[-n:]))


def centre(acts, outer, bias_conv):
    size, c = acts[0].shape
    m = outer.shape[2]
    n = len(acts)

    def body(*refs):
        outer_ref, bias_ref = refs[n : n + 2]
        for act_ref, out_ref in zip(refs[:n], refs[n + 2 :]):
            out_ref[...] = dot(act_ref[...], outer_ref[1]) + bias_ref[...]

    args = list(acts) + [outer, bias_conv]
    return call(body, "centre", [shape(size, m, F32)] * n, args, 2 * n * size * c * m, [], specs=[VMEM] * len(args))


def finish(quarter, at, centre_sum, one_side, other_side, one, point, bias_point, whole):
    size, c = one.shape
    rows, m = one_side.shape
    steps = 2 if rows % 256 == 0 else 1
    step = rows // steps

    def body(centre_ref, one_side_ref, other_side_ref, one_ref, point_ref, bias_ref, *rest):
        out_hbm, held, sems = rest[-3:]
        start = quarter_rows(quarter, size).start + at
        copies = []
        for k in range(steps):
            part, own = pl.ds(k * step, step), pl.ds(at + k * step, step)
            total = centre_ref[own, :] + one_side_ref[part, :].astype(F32) + other_side_ref[part, :].astype(F32)
            mid = gelu(total).astype(BF16)
            out = one_ref[own, :].astype(F32) + dot(mid, point_ref[...]) + bias_ref[...]
            held[k] = out.astype(BF16)
            to = pl.ds(pl.multiple_of(start + k * step, 128), step)
            copies.append(pltpu.make_async_copy(held.at[k], out_hbm.at[to], sems.at[k]))
            copies[k].start()
        for copy in copies:
            copy.wait()

    args = [centre_sum, one_side, other_side, one, point, bias_point] + ([] if whole is None else [whole])
    return call(
        body, f"finish{quarter}", [shape(4 * size, c)], args, 2 * rows * c * m,
        [pltpu.VMEM((steps, step, c), BF16), pltpu.SemaphoreType.DMA((steps,))],
        aliases={} if whole is None else {6: 0}, out_specs=[ANY], specs=[VMEM] * 6 + [ANY] * (len(args) - 6),
    )[0]


def per_device(
    tower_input,
    first_conv_taps,
    first_conv_bias,
    first_point_weight,
    first_point_bias,
    second_conv_taps,
    second_conv_bias,
    second_point_weight,
    second_point_bias,
):
    size = tower_input.shape[0] // 4
    whole = (size,)
    split = (size - LAST_PIECE, LAST_PIECE)

    near = (first_conv_taps, first_conv_bias[None, :], first_point_weight, first_point_bias[None, :], second_conv_taps)
    x = pltpu.with_memory_space_constraint(tower_input, pltpu.HBM)
    rim_taps = pltpu.with_memory_space_constraint(first_conv_taps, pltpu.HBM)
    act0, to_pair = rim(x, rim_taps, 0)
    from_pair = swap(to_pair, lambda i: i % 2 == 1, 1)

    def send(products):
        return [
            (swap(second, lambda i: i // 2 % 2 == 1, 2), swap(first, lambda i: i // 2 % 2 == 0, 2))
            for first, second in products
        ]

    act1, act2, one1, far1, products1 = layer(x, 1, (act0, None, None), None, near, whole, fresh=True)
    later, products1 = lax.optimization_barrier((x, products1))
    sides1 = send(products1)
    act3, to_partner = rim(later, rim_taps, 3)
    from_partner = swap(to_partner, lambda i: i % 2 == 0, 1)
    one2, far2, products2 = layer(x, 2, (act1, act2, act3), None, near, whole)
    sides2 = send(products2)
    one0, far0, products0 = layer(x, 0, (None, act0, act1), from_pair, near, whole)
    sides0 = send(products0)
    one3, far3, products3 = layer(x, 3, (act2, act3, None), from_partner, near, split)
    sides3 = send(products3)

    centres = centre((far1, far2, far0, far3), second_conv_taps, second_conv_bias[None, :])
    out = None
    for quarter, total, sides, one in zip(
        (1, 2, 0, 3), centres, (sides1, sides2, sides0, sides3), (one1, one2, one0, one3)
    ):
        at = 0
        for pair in sides:
            out = finish(quarter, at, total, *pair, one, second_point_weight, second_point_bias[None, :], out)
            at += pair[0].shape[0]
    return out


def solution(mesh):
    return jax.shard_map(
        per_device,
        mesh=mesh,
        in_specs=(P(("grp", "seq"), None), P(), P(), P(), P(), P(), P(), P(), P()),
        out_specs=P(("grp", "seq"), None),
        check_vma=False,
    )
```

time: 68.3 us -> 67.3 us (0.985)
  waiting for transfers between devices: 16.1 us -> 8.76 us
  starting transfers between devices: 17.8 us -> 23.5 us
    ppermute x10 -> x12, waiting for transfers between devices: 16.1 us -> 8.76 us  [swap(): return lax.ppermute(value, 'seq', sorted(pairs))]
    ppermute x10 -> x12, starting transfers between devices: 17.8 us -> 23.5 us  [swap(): return lax.ppermute(value, 'seq', sorted(pairs))]
    pallas_call x11 -> x12, Pallas kernels: 33.6 us -> 34.1 us  [call(): pl.pallas_call(body, in_specs=specs, out_specs=[VMEM] * len(out_shape) if...]
  transfers between devices with their start and end apart: 10 -> 12, of which waited for: 4 -> 4; matrix products, arithmetic and copies ran while one was open for 0% -> 0% of each run, Pallas kernels for 43% -> 46%
where the time goes in v4:
time: 67.3 us; the launch traced here: 66.8 us
  Pallas kernels  34.1 us (51%)
  starting transfers between devices  23.5 us (35%)
  waiting for transfers between devices  8.76 us (13%)
    pallas_call x12, Pallas kernels, call(): pl.pallas_call(body, in_specs=specs, out_specs=[VMEM] * len(out_shape) if...  34.1 us
    ppermute x12, starting transfers between devices, swap(): return lax.ppermute(value, 'seq', sorted(pairs))  23.5 us
    ppermute x12, waiting for transfers between devices, swap(): return lax.ppermute(value, 'seq', sorted(pairs))  8.76 us
  transfers between devices with their start and end apart: 12, of which 4 were waited for; matrix products, arithmetic and copies ran while one was open for 0% of the time, Pallas kernels for 46%

profile of v4, /device:TPU:0, one launch (start us, length us, event | category | flops | bytes accessed | tf_op | source)
XLA Modules:
  0.0 66.8 jit_solution(9214775160516704136)
XLA Ops:
  0.0 0.0 copy-start
  0.0 0.0 copy-start.2
  0.0 0.0 copy-start.4
  0.0 0.0 copy-start.6
  0.0 0.0 copy-start.7
  0.0 2.4 %rim0.1 = (bf16[512,1024]{1,0:T(8,128)(2,1)S(1)}, bf16[512,512]{1,0:T(8,128)(2,1)S(1)}) custom-call(bf16[2048,1024]{1,0:T(8,128)(2,1)} %refs_0_.7, bf16[3,1024,512]{2,1,0:T(8,128)(2,1)} %refs_4_.8), custom_call_target="tpu_custom_call" | custom-call | flops 536870912 | bytes 7340032 | tf_op jit(solution)/shard_map/rim0/pallas_call | solution.py:50
  2.4 6.7 %collective-permute-start = (bf16[512,512]{1,0:T(8,128)(2,1)S(1)}, bf16[512,512]{1,0:T(8,128)(2,1)S(1)}, u32[]{:S(2)}, u32[]{:S(2)}) collective-permute-start(bf16[512,512]{1,0:T(8,128)(2,1)S(1)} %get-tuple-element.45), channel_id=1, source_target_pairs={{0,31},{1,2},{2,1},{3,4},{4,3},{5,6},{6,5},{7,8},{8,7},{9,10},{10,... | collective-permute-start | bytes 1572872 | tf_op jit(solution)/shard_map/ppermute | solution.py:27
  9.2 0.0 copy-done
  9.2 0.0 copy-done.2
  9.2 0.0 copy-done.4
  9.2 0.0 copy-done.6
  9.2 0.0 copy-done.7
  9.2 5.6 %layer1.1 = (bf16[512,1024]{1,0:T(8,128)(2,1)S(1)}, bf16[512,1024]{1,0:T(8,128)(2,1)S(1)}, bf16[512,1024]{1,0:T(8,128)(2,1)S(1)}, bf16[512,1024]{1,0:T(8,128)(2,...) custom-call(bf16[2048,1024]{1,0:T(8,128)(2,1)} %refs_0_.7, ...), custom_call_target="tpu_custom_call" | custom-call | flops 3221225472 | bytes 12589056 | tf_op jit(solution)/shard_map/layer1/pallas_call | solution.py:50
  14.8 0.0 copy-start.1
  14.8 0.9 %collective-permute-start.10 = (bf16[512,512]{1,0:T(8,128)(2,1)S(1)}, bf16[512,512]{1,0:T(8,128)(2,1)S(1)}, u32[]{:S(2)}, u32[]{:S(2)}) collective-permute-start(bf16[512,512]{1,0:T(8,128)(2,1)S(1)} %get-tuple-element.64), channel_id=1, source_target_pairs={{0,30},{1,31},{2,4},{3,5},{4,2},{5,3},{6,8},{7,9},{8,6},{9,7},{10,... | collective-permute-start | bytes 1572872 | tf_op jit(solution)/shard_map/ppermute | solution.py:27
  15.7 0.0 collective-permute-start.11
  15.7 2.3 %rim3.1 = (bf16[512,1024]{1,0:T(8,128)(2,1)S(1)}, bf16[512,512]{1,0:T(8,128)(2,1)S(1)}) custom-call(bf16[2048,1024]{1,0:T(8,128)(2,1)} %refs_0_.7, bf16[3,1024,512]{2,1,0:T(8,128)(2,1)} %refs_4_.8), custom_call_target="tpu_custom_call" | custom-call | flops 536870912 | bytes 7340032 | tf_op jit(solution)/shard_map/rim3/pallas_call | solution.py:50
  18.0 0.9 %collective-permute-start.1 = (bf16[512,512]{1,0:T(8,128)(2,1)S(1)}, bf16[512,512]{1,0:T(8,128)(2,1)S(1)}, u32[]{:S(2)}, u32[]{:S(2)}) collective-permute-start(bf16[512,512]{1,0:T(8,128)(2,1)S(1)} %get-tuple-element.47), channel_id=1, source_target_pairs={{0,1},{1,0},{2,3},{3,2},{4,5},{5,4},{6,7},{7,6},{8,9},{9,8},{10,11... | collective-permute-start | bytes 1572872 | tf_op jit(solution)/shard_map/ppermute | solution.py:27
  18.9 0.0 copy-done.1
  18.9 5.0 %layer2.1 = (bf16[512,1024]{1,0:T(8,128)(2,1)S(1)}, bf16[512,1024]{1,0:T(8,128)(2,1)S(1)}, bf16[512,512]{1,0:T(8,128)(2,1)S(1)}, bf16[512,512]{1,0:T(8,128)(2,1)S(1)}) custom-call(bf16[2048,1024]{1,0:T(8,128)(2,1)} %refs_0_.7, bf16[512,1024]{1,0:T(8,128)(2,1)S(1)} %get-tuple-element.38.refs_1_.refs_2_, ...), custom_call_target="tpu_custom_call" | custom-call | flops 3221225472 | bytes 14686208 | tf_op jit(solution)/shard_map/layer2/pallas_call | solution.py:50
  23.9 3.8 %collective-permute-start.8 = (bf16[512,512]{1,0:T(8,128)(2,1)S(1)}, bf16[512,512]{1,0:T(8,128)(2,1)S(1)}, u32[]{:S(2)}, u32[]{:S(2)}) collective-permute-start(bf16[512,512]{1,0:T(8,128)(2,1)S(1)} %get-tuple-element.60), channel_id=1, source_target_pairs={{0,30},{1,31},{2,4},{3,5},{4,2},{5,3},{6,8},{7,9},{8,6},{9,7},{10,... | collective-permute-start | bytes 1572872 | tf_op jit(solution)/shard_map/ppermute | solution.py:27
  27.7 0.0 collective-permute-done.refs_3_
  27.7 0.0 collective-permute-start.9
  27.7 3.8 %layer0.1 = (bf16[512,1024]{1,0:T(8,128)(2,1)S(1)}, bf16[512,1024]{1,0:T(8,128)(2,1)S(1)}, bf16[512,512]{1,0:T(8,128)(2,1)S(1)}, bf16[512,512]{1,0:T(8,128)(2,1)S(1)}) custom-call(bf16[2048,1024]{1,0:T(8,128)(2,1)} %refs_0_.7, bf16[512,1024]{1,0:T(8,128)(2,1)S(1)} %get-tuple-element.36.refs_1_, bf16[512,1024]{1,0:T(8,128)(2,1)S(1)} %get-tuple-element.38.refs_1_.refs_2_, ...), custom_call_target="tpu_custom_call" | custom-call | flops 3221225472 | bytes 14161920 | tf_op jit(solution)/shard_map/layer0/pallas_call | solution.py:50
  31.5 1.6 %collective-permute-done.10.one_side_ref = bf16[512,512]{1,0:T(8,128)(2,1)S(1)} collective-permute-done((bf16[512,512]{1,0:T(8,128)(2,1)S(1)}, bf16[512,512]{1,0:T(8,128)(2,1)S(1)}, u32[]{:S(2)}, u32[]{:S(2)}) %collective-permute-start.10) | collective-permute-done | bytes 524320 | tf_op jit(solution)/shard_map/ppermute | solution.py:27
  33.1 5.5 %collective-permute-start.6 = (bf16[512,512]{1,0:T(8,128)(2,1)S(1)}, bf16[512,512]{1,0:T(8,128)(2,1)S(1)}, u32[]{:S(2)}, u32[]{:S(2)}) collective-permute-start(bf16[512,512]{1,0:T(8,128)(2,1)S(1)} %get-tuple-element.56), channel_id=1, source_target_pairs={{0,30},{1,31},{2,4},{3,5},{4,2},{5,3},{6,8},{7,9},{8,6},{9,7},{10,... | collective-permute-start | bytes 1572872 | tf_op jit(solution)/shard_map/ppermute | solution.py:27
  38.5 0.0 collective-permute-done.1.refs_3_
  38.6 0.0 copy-start.8
  38.6 0.0 collective-permute-start.7
  38.6 4.6 %layer3.1 = (bf16[512,1024]{1,0:T(8,128)(2,1)S(1)}, bf16[512,1024]{1,0:T(8,128)(2,1)S(1)}, bf16[384,512]{1,0:T(8,128)(2,1)S(1)}, bf16[128,512]{1,0:T(8,128)(2,1)...) custom-call(bf16[2048,1024]{1,0:T(8,128)(2,1)} %refs_0_.7, ...), custom_call_target="tpu_custom_call" | custom-call | flops 3221225472 | bytes 14161920 | tf_op jit(solution)/shard_map/layer3/pallas_call | solution.py:50
  43.1 0.0 copy-start.3
  43.1 0.0 copy-start.5
  43.1 0.0 collective-permute-done.11.other_side_ref
  43.2 0.2 collective-permute-start.4
  43.3 1.0 %collective-permute-done.8.one_side_ref = bf16[512,512]{1,0:T(8,128)(2,1)S(1)} collective-permute-done((bf16[512,512]{1,0:T(8,128)(2,1)S(1)}, bf16[512,512]{1,0:T(8,128)(2,1)S(1)}, u32[]{:S(2)}, u32[]{:S(2)}) %collective-permute-start.8) | collective-permute-done | bytes 524320 | tf_op jit(solution)/shard_map/ppermute | solution.py:27
  44.3 1.0 %collective-permute-start.5 = (bf16[384,512]{1,0:T(8,128)(2,1)S(1)}, bf16[384,512]{1,0:T(8,128)(2,1)S(1)}, u32[]{:S(2)}, u32[]{:S(2)}) collective-permute-start(bf16[384,512]{1,0:T(8,128)(2,1)S(1)} %get-tuple-element.54), channel_id=1, source_target_pairs={{0,2},{1,3},{2,0},{3,1},{4,6},{5,7},{6,4},{7,5},{8,10},{9,11},{10,... | collective-permute-start | bytes 1179656 | tf_op jit(solution)/shard_map/ppermute | solution.py:27
  45.4 0.0 copy-done.8
  45.4 2.3 %centre.1 = (f32[512,512]{1,0:T(8,128)S(1)}, f32[512,512]{1,0:T(8,128)S(1)}, f32[512,512]{1,0:T(8,128)S(1)}, f32[512,512]{1,0:T(8,128)S(1)}) custom-call(bf16[512,1024]{1,0:T(8,128)(2,1)S(1)} %get-tuple-element.37.refs_0_, bf16[512,1024]{1,0:T(8,128)(2,1)S(1)} %get-tuple-element.44.refs_1_, bf16[512,1024]{1,0:T(8,128)(2,1)S(1)} %get-tuple-element.46.refs_2_, ...), custom_call_target="tpu_custom_call" | custom-call | flops 2147483648 | bytes 7342080 | tf_op jit(solution)/shard_map/centre/pallas_call | solution.py:50
  47.7 0.0 copy-done.3
  47.7 0.0 copy-done.5
  47.7 1.8 %finish1.1.rest_0_ = bf16[2048,1024]{1,0:T(8,128)(2,1)} custom-call(f32[512,512]{1,0:T(8,128)S(1)} %get-tuple-element.63.centre_ref, bf16[512,512]{1,0:T(8,128)(2,1)S(1)} %collective-permute-done.10.one_side_ref, bf16[512,512]{1,0:T(8,128)(2,1)S(1)} %collective-permute-done.11.other_side_ref, bf16[512,1024]{1,0:T(8,128)(2,1)S(1)} %get-tuple-element.66.one_ref, ...), custom_call_target="tpu_custom_call" | custom-call | flops 536870912 | bytes 4198400 | tf_op jit(solution)/shard_map/finish1/pallas_call | solution.py:50
  49.5 0.0 collective-permute-done.9.other_side_ref
  49.5 4.5 %collective-permute-start.2 = (bf16[128,512]{1,0:T(8,128)(2,1)S(1)}, bf16[128,512]{1,0:T(8,128)(2,1)S(1)}, u32[]{:S(2)}, u32[]{:S(2)}) collective-permute-start(bf16[128,512]{1,0:T(8,128)(2,1)S(1)} %get-tuple-element.50), channel_id=1, source_target_pairs={{0,30},{1,31},{2,4},{3,5},{4,2},{5,3},{6,8},{7,9},{8,6},{9,7},{10,... | collective-permute-start | bytes 393224 | tf_op jit(solution)/shard_map/ppermute | solution.py:27
  54.1 1.5 %collective-permute-done.6.one_side_ref = bf16[512,512]{1,0:T(8,128)(2,1)S(1)} collective-permute-done((bf16[512,512]{1,0:T(8,128)(2,1)S(1)}, bf16[512,512]{1,0:T(8,128)(2,1)S(1)}, u32[]{:S(2)}, u32[]{:S(2)}) %collective-permute-start.6) | collective-permute-done | bytes 524320 | tf_op jit(solution)/shard_map/ppermute | solution.py:27
  55.5 0.0 collective-permute-start.3
  55.5 1.8 %finish2.1.rest_0_ = bf16[2048,1024]{1,0:T(8,128)(2,1)} custom-call(f32[512,512]{1,0:T(8,128)S(1)} %get-tuple-element.59.centre_ref, bf16[512,512]{1,0:T(8,128)(2,1)S(1)} %collective-permute-done.8.one_side_ref, bf16[512,512]{1,0:T(8,128)(2,1)S(1)} %collective-permute-done.9.other_side_ref, ...), custom_call_target="tpu_custom_call", output_to_operand_aliasing={{}: (6, {})} | custom-call | flops 536870912 | bytes 8392704 | tf_op jit(solution)/shard_map/finish2/pallas_call | solution.py:50
  57.4 0.0 collective-permute-done.7.other_side_ref
  57.4 1.8 %finish0.1.rest_0_ = bf16[2048,1024]{1,0:T(8,128)(2,1)} custom-call(f32[512,512]{1,0:T(8,128)S(1)} %get-tuple-element.55.centre_ref, bf16[512,512]{1,0:T(8,128)(2,1)S(1)} %collective-permute-done.6.one_side_ref, bf16[512,512]{1,0:T(8,128)(2,1)S(1)} %collective-permute-done.7.other_side_ref, ...), custom_call_target="tpu_custom_call", output_to_operand_aliasing={{}: (6, {})} | custom-call | flops 536870912 | bytes 8392704 | tf_op jit(solution)/shard_map/finish0/pallas_call | solution.py:50
  59.2 4.7 %collective-permute-done.4.one_side_ref = bf16[384,512]{1,0:T(8,128)(2,1)S(1)} collective-permute-done((bf16[384,512]{1,0:T(8,128)(2,1)S(1)}, bf16[384,512]{1,0:T(8,128)(2,1)S(1)}, u32[]{:S(2)}, u32[]{:S(2)}) %collective-permute-start.4) | collective-permute-done | bytes 393248 | tf_op jit(solution)/shard_map/ppermute | solution.py:27
  63.9 0.0 collective-permute-done.5.other_side_ref
  63.9 1.6 %finish3.2.rest_0_ = bf16[2048,1024]{1,0:T(8,128)(2,1)} custom-call(f32[512,512]{1,0:T(8,128)S(1)} %get-tuple-element.49.centre_ref, bf16[384,512]{1,0:T(8,128)(2,1)S(1)} %collective-permute-done.4.one_side_ref, bf16[384,512]{1,0:T(8,128)(2,1)S(1)} %collective-permute-done.5.other_side_ref, ...), custom_call_target="tpu_custom_call", output_to_operand_aliasing={{}: (6, {})} | custom-call | flops 402653184 | bytes 8130560 | tf_op jit(solution)/shard_map/finish3/pallas_call | solution.py:50
  65.5 0.0 collective-permute-done.2.one_side_ref
  65.6 0.0 collective-permute-done.3.other_side_ref
  65.6 1.1 %finish3.3 = bf16[2048,1024]{1,0:T(8,128)(2,1)} custom-call(f32[512,512]{1,0:T(8,128)S(1)} %get-tuple-element.49.centre_ref, bf16[128,512]{1,0:T(8,128)(2,1)S(1)} %collective-permute-done.2.one_side_ref, bf16[128,512]{1,0:T(8,128)(2,1)S(1)} %collective-permute-done.3.other_side_ref, ...), custom_call_target="tpu_custom_call", output_to_operand_aliasing={{}: (6, {})} | custom-call | flops 134217728 | bytes 7606272 | tf_op jit(solution)/shard_map/finish3/pallas_call | solution.py:50
Async XLA Ops:
  0.0 9.2 %copy-start = (bf16[3,1024,512]{2,1,0:T(8,128)(2,1)S(1)}, bf16[3,1024,512]{2,1,0:T(8,128)(2,1)}, u32[]{:S(2)}) copy-start(bf16[3,1024,512]{2,1,0:T(8,128)(2,1)} %refs_4_.8) | copy-start | bytes 9437188
  0.0 9.2 %copy-start.2 = (bf16[3,1024,512]{2,1,0:T(8,128)(2,1)S(1)}, bf16[3,1024,512]{2,1,0:T(8,128)(2,1)}, u32[]{:S(2)}) copy-start(bf16[3,1024,512]{2,1,0:T(8,128)(2,1)} %refs_4_.9) | copy-start | bytes 9437188
  0.0 9.2 %copy-start.4 = (bf16[512,1024]{1,0:T(8,128)(2,1)S(1)}, bf16[512,1024]{1,0:T(8,128)(2,1)}, u32[]{:S(2)}) copy-start(bf16[512,1024]{1,0:T(8,128)(2,1)} %refs_6_.7) | copy-start | bytes 3145732
  0.0 9.2 %copy-start.6 = (f32[1024]{0:T(1024)S(1)}, f32[1024]{0:T(1024)}, u32[]{:S(2)}) copy-start(f32[1024]{0:T(1024)} %param.13) | copy-start | bytes 12292
  0.0 9.2 %copy-start.7 = (f32[512]{0:T(512)S(1)}, f32[512]{0:T(512)}, u32[]{:S(2)}) copy-start(f32[512]{0:T(512)} %param.11) | copy-start | bytes 6148
  2.4 25.3 %collective-permute-start = (bf16[512,512]{1,0:T(8,128)(2,1)S(1)}, bf16[512,512]{1,0:T(8,128)(2,1)S(1)}, u32[]{:S(2)}, u32[]{:S(2)}) collective-permute-start(bf16[512,512]{1,0:T(8,128)(2,1)S(1)} %get-tuple-element.45), channel_id=1, source_target_pairs={{0,31},{1,2},{2,1},{3,4},{4,3},{5,6},{6,5},{7,8},{8,7},{9,10},{10,... | collective-permute-start | bytes 1572872 | tf_op jit(solution)/shard_map/ppermute | solution.py:27
  14.8 4.1 %copy-start.1 = (bf16[3,1024,512]{2,1,0:T(8,128)(2,1)S(1)}, bf16[3,1024,512]{2,1,0:T(8,128)(2,1)}, u32[]{:S(2)}) copy-start(bf16[3,1024,512]{2,1,0:T(8,128)(2,1)} %refs_4_.8) | copy-start | bytes 9437188
  14.8 18.2 %collective-permute-start.10 = (bf16[512,512]{1,0:T(8,128)(2,1)S(1)}, bf16[512,512]{1,0:T(8,128)(2,1)S(1)}, u32[]{:S(2)}, u32[]{:S(2)}) collective-permute-start(bf16[512,512]{1,0:T(8,128)(2,1)S(1)} %get-tuple-element.64), channel_id=1, source_target_pairs={{0,30},{1,31},{2,4},{3,5},{4,2},{5,3},{6,8},{7,9},{8,6},{9,7},{10,... | collective-permute-start | bytes 1572872 | tf_op jit(solution)/shard_map/ppermute | solution.py:27
  15.7 27.4 %collective-permute-start.11 = (bf16[512,512]{1,0:T(8,128)(2,1)S(1)}, bf16[512,512]{1,0:T(8,128)(2,1)S(1)}, u32[]{:S(2)}, u32[]{:S(2)}) collective-permute-start(bf16[512,512]{1,0:T(8,128)(2,1)S(1)} %get-tuple-element.65), channel_id=1, source_target_pairs={{0,2},{1,3},{2,0},{3,1},{4,6},{5,7},{6,4},{7,5},{8,10},{9,11},{10,... | collective-permute-start | bytes 1572872 | tf_op jit(solution)/shard_map/ppermute | solution.py:27
  18.0 20.5 %collective-permute-start.1 = (bf16[512,512]{1,0:T(8,128)(2,1)S(1)}, bf16[512,512]{1,0:T(8,128)(2,1)S(1)}, u32[]{:S(2)}, u32[]{:S(2)}) collective-permute-start(bf16[512,512]{1,0:T(8,128)(2,1)S(1)} %get-tuple-element.47), channel_id=1, source_target_pairs={{0,1},{1,0},{2,3},{3,2},{4,5},{5,4},{6,7},{7,6},{8,9},{9,8},{10,11... | collective-permute-start | bytes 1572872 | tf_op jit(solution)/shard_map/ppermute | solution.py:27
  23.9 20.4 %collective-permute-start.8 = (bf16[512,512]{1,0:T(8,128)(2,1)S(1)}, bf16[512,512]{1,0:T(8,128)(2,1)S(1)}, u32[]{:S(2)}, u32[]{:S(2)}) collective-permute-start(bf16[512,512]{1,0:T(8,128)(2,1)S(1)} %get-tuple-element.60), channel_id=1, source_target_pairs={{0,30},{1,31},{2,4},{3,5},{4,2},{5,3},{6,8},{7,9},{8,6},{9,7},{10,... | collective-permute-start | bytes 1572872 | tf_op jit(solution)/shard_map/ppermute | solution.py:27
  27.7 21.8 %collective-permute-start.9 = (bf16[512,512]{1,0:T(8,128)(2,1)S(1)}, bf16[512,512]{1,0:T(8,128)(2,1)S(1)}, u32[]{:S(2)}, u32[]{:S(2)}) collective-permute-start(bf16[512,512]{1,0:T(8,128)(2,1)S(1)} %get-tuple-element.61), channel_id=1, source_target_pairs={{0,2},{1,3},{2,0},{3,1},{4,6},{5,7},{6,4},{7,5},{8,10},{9,11},{10,... | collective-permute-start | bytes 1572872 | tf_op jit(solution)/shard_map/ppermute | solution.py:27
  33.1 22.5 %collective-permute-start.6 = (bf16[512,512]{1,0:T(8,128)(2,1)S(1)}, bf16[512,512]{1,0:T(8,128)(2,1)S(1)}, u32[]{:S(2)}, u32[]{:S(2)}) collective-permute-start(bf16[512,512]{1,0:T(8,128)(2,1)S(1)} %get-tuple-element.56), channel_id=1, source_target_pairs={{0,30},{1,31},{2,4},{3,5},{4,2},{5,3},{6,8},{7,9},{8,6},{9,7},{10,... | collective-permute-start | bytes 1572872 | tf_op jit(solution)/shard_map/ppermute | solution.py:27
  38.6 6.8 %copy-start.8 = (f32[512]{0:T(512)S(1)}, f32[512]{0:T(512)}, u32[]{:S(2)}) copy-start(f32[512]{0:T(512)} %param.15) | copy-start | bytes 6148
  38.6 18.8 %collective-permute-start.7 = (bf16[512,512]{1,0:T(8,128)(2,1)S(1)}, bf16[512,512]{1,0:T(8,128)(2,1)S(1)}, u32[]{:S(2)}, u32[]{:S(2)}) collective-permute-start(bf16[512,512]{1,0:T(8,128)(2,1)S(1)} %get-tuple-element.57), channel_id=1, source_target_pairs={{0,2},{1,3},{2,0},{3,1},{4,6},{5,7},{6,4},{7,5},{8,10},{9,11},{10,... | collective-permute-start | bytes 1572872 | tf_op jit(solution)/shard_map/ppermute | solution.py:27
  43.1 4.6 %copy-start.3 = (bf16[512,1024]{1,0:T(8,128)(2,1)S(1)}, bf16[512,1024]{1,0:T(8,128)(2,1)}, u32[]{:S(2)}) copy-start(bf16[512,1024]{1,0:T(8,128)(2,1)} %point_ref.9) | copy-start | bytes 3145732
  43.1 4.6 %copy-start.5 = (f32[1024]{0:T(1024)S(1)}, f32[1024]{0:T(1024)}, u32[]{:S(2)}) copy-start(f32[1024]{0:T(1024)} %param.17) | copy-start | bytes 12292
  43.2 20.7 %collective-permute-start.4 = (bf16[384,512]{1,0:T(8,128)(2,1)S(1)}, bf16[384,512]{1,0:T(8,128)(2,1)S(1)}, u32[]{:S(2)}, u32[]{:S(2)}) collective-permute-start(bf16[384,512]{1,0:T(8,128)(2,1)S(1)} %get-tuple-element.53), channel_id=1, source_target_pairs={{0,30},{1,31},{2,4},{3,5},{4,2},{5,3},{6,8},{7,9},{8,6},{9,7},{10,... | collective-permute-start | bytes 1179656 | tf_op jit(solution)/shard_map/ppermute | solution.py:27
  44.3 19.6 %collective-permute-start.5 = (bf16[384,512]{1,0:T(8,128)(2,1)S(1)}, bf16[384,512]{1,0:T(8,128)(2,1)S(1)}, u32[]{:S(2)}, u32[]{:S(2)}) collective-permute-start(bf16[384,512]{1,0:T(8,128)(2,1)S(1)} %get-tuple-element.54), channel_id=1, source_target_pairs={{0,2},{1,3},{2,0},{3,1},{4,6},{5,7},{6,4},{7,5},{8,10},{9,11},{10,... | collective-permute-start | bytes 1179656 | tf_op jit(solution)/shard_map/ppermute | solution.py:27
  49.5 16.0 %collective-permute-start.2 = (bf16[128,512]{1,0:T(8,128)(2,1)S(1)}, bf16[128,512]{1,0:T(8,128)(2,1)S(1)}, u32[]{:S(2)}, u32[]{:S(2)}) collective-permute-start(bf16[128,512]{1,0:T(8,128)(2,1)S(1)} %get-tuple-element.50), channel_id=1, source_target_pairs={{0,30},{1,31},{2,4},{3,5},{4,2},{5,3},{6,8},{7,9},{8,6},{9,7},{10,... | collective-permute-start | bytes 393224 | tf_op jit(solution)/shard_map/ppermute | solution.py:27
  55.5 10.0 %collective-permute-start.3 = (bf16[128,512]{1,0:T(8,128)(2,1)S(1)}, bf16[128,512]{1,0:T(8,128)(2,1)S(1)}, u32[]{:S(2)}, u32[]{:S(2)}) collective-permute-start(bf16[128,512]{1,0:T(8,128)(2,1)S(1)} %get-tuple-element.51), channel_id=1, source_target_pairs={{0,2},{1,3},{2,0},{3,1},{4,6},{5,7},{6,4},{7,5},{8,10},{9,11},{10,... | collective-permute-start | bytes 393224 | tf_op jit(solution)/shard_map/ppermute | solution.py:27

commit v5 on v4

--- a/solution.py
+++ b/solution.py
@@ -12,7 +12,7 @@
 ANY = pl.BlockSpec(memory_space=pl.ANY)
 HBM = pl.BlockSpec(memory_space=pltpu.HBM)
 SLOPE = math.sqrt(2.0 / math.pi)
-LAST_PIECE = 128
+LAST_PIECE = 256
 BF16 = jnp.bfloat16
 F32 = jnp.float32
 
@@ -181,7 +181,7 @@
 def finish(quarter, at, centre_sum, one_side, other_side, one, point, bias_point, whole):
     size, c = one.shape
     rows, m = one_side.shape
-    steps = 2 if rows % 256 == 0 else 1
+    steps = 2 if rows % 32 == 0 else 1
     step = rows // steps
 
     def body(centre_ref, one_side_ref, other_side_ref, one_ref, point_ref, bias_ref, *rest):
@@ -194,7 +194,7 @@
             mid = gelu(total).astype(BF16)
             out = one_ref[own, :].astype(F32) + dot(mid, point_ref[...]) + bias_ref[...]
             held[k] = out.astype(BF16)
-            to = pl.ds(pl.multiple_of(start + k * step, 128), step)
+            to = pl.ds(pl.multiple_of(start + k * step, 16), step)
             copies.append(pltpu.make_async_copy(held.at[k], out_hbm.at[to], sems.at[k]))
             copies[k].start()
         for copy in copies:
@@ -245,18 +245,21 @@
     one0, far0, products0 = layer(x, 0, (None, act0, act1), from_pair, near, whole)
     sides0 = send(products0)
     one3, far3, products3 = layer(x, 3, (act2, act3, None), from_partner, near, split)
-    sides3 = send(products3)
-
-    centres = centre((far1, far2, far0, far3), second_conv_taps, second_conv_bias[None, :])
-    out = None
-    for quarter, total, sides, one in zip(
-        (1, 2, 0, 3), centres, (sides1, sides2, sides0, sides3), (one1, one2, one0, one3)
-    ):
-        at = 0
+    sides3 = send(products3[:1])
+
+    def finished(quarter, at, total, sides, one, out):
         for pair in sides:
             out = finish(quarter, at, total, *pair, one, second_point_weight, second_point_bias[None, :], out)
             at += pair[0].shape[0]
-    return out
+        return out
+
+    total1, total2, total0, total3 = centre((far1, far2, far0, far3), second_conv_taps, second_conv_bias[None, :])
+    out = finished(1, 0, total1, sides1, one1, None)
+    out = finished(2, 0, total2, sides2, one2, out)
+    out, last = lax.optimization_barrier((out, products3[1]))
+    sides3 += send([last])
+    out = finished(0, 0, total0, sides0, one0, out)
+    return finished(3, 0, total3, sides3, one3, out)
 
 
 def solution(mesh):

time: 67.3 us -> 67.6 us (level)
  transfers between devices with their start and end apart: 12 -> 12, of which waited for: 4 -> 4; matrix products, arithmetic and copies ran while one was open for 0% -> 0% of each run, Pallas kernels for 46% -> 45%
where the time goes in v5:
time: 67.6 us; the launch traced here: 66.8 us
  Pallas kernels  34.1 us (50%)
  starting transfers between devices  23.4 us (35%)
  waiting for transfers between devices  8.96 us (13%)
    pallas_call x12, Pallas kernels, call(): pl.pallas_call(body, in_specs=specs, out_specs=[VMEM] * len(out_shape) if...  34.1 us
    ppermute x12, starting transfers between devices, swap(): return lax.ppermute(value, 'seq', sorted(pairs))  23.4 us
    ppermute x12, waiting for transfers between devices, swap(): return lax.ppermute(value, 'seq', sorted(pairs))  8.96 us
  transfers between devices with their start and end apart: 12, of which 4 were waited for; matrix products, arithmetic and copies ran while one was open for 0% of the time, Pallas kernels for 45%

profile of v5, /device:TPU:0, one launch (start us, length us, event | category | flops | bytes accessed | tf_op | source)
XLA Modules:
  0.0 66.8 jit_solution(16161164345418624585)
XLA Ops:
  0.0 0.0 copy-start
  0.0 0.0 copy-start.2
  0.0 0.0 copy-start.4
  0.0 0.0 copy-start.6
  0.0 0.0 copy-start.7
  0.0 2.4 %rim0.1 = (bf16[512,1024]{1,0:T(8,128)(2,1)S(1)}, bf16[512,512]{1,0:T(8,128)(2,1)S(1)}) custom-call(bf16[2048,1024]{1,0:T(8,128)(2,1)} %refs_0_.7, bf16[3,1024,512]{2,1,0:T(8,128)(2,1)} %refs_4_.8), custom_call_target="tpu_custom_call" | custom-call | flops 536870912 | bytes 7340032 | tf_op jit(solution)/shard_map/rim0/pallas_call | solution.py:50
  2.4 6.7 %collective-permute-start = (bf16[512,512]{1,0:T(8,128)(2,1)S(1)}, bf16[512,512]{1,0:T(8,128)(2,1)S(1)}, u32[]{:S(2)}, u32[]{:S(2)}) collective-permute-start(bf16[512,512]{1,0:T(8,128)(2,1)S(1)} %get-tuple-element.48), channel_id=1, source_target_pairs={{0,31},{1,2},{2,1},{3,4},{4,3},{5,6},{6,5},{7,8},{8,7},{9,10},{10,... | collective-permute-start | bytes 1572872 | tf_op jit(solution)/shard_map/ppermute | solution.py:27
  9.2 0.0 copy-done
  9.2 0.0 copy-done.2
  9.2 0.0 copy-done.4
  9.2 0.0 copy-done.6
  9.2 0.0 copy-done.7
  9.2 5.6 %layer1.1 = (bf16[512,1024]{1,0:T(8,128)(2,1)S(1)}, bf16[512,1024]{1,0:T(8,128)(2,1)S(1)}, bf16[512,1024]{1,0:T(8,128)(2,1)S(1)}, bf16[512,1024]{1,0:T(8,128)(2,...) custom-call(bf16[2048,1024]{1,0:T(8,128)(2,1)} %refs_0_.7, ...), custom_call_target="tpu_custom_call" | custom-call | flops 3221225472 | bytes 12589056 | tf_op jit(solution)/shard_map/layer1/pallas_call | solution.py:50
  14.8 0.0 copy-start.1
  14.8 0.9 %collective-permute-start.4 = (bf16[512,512]{1,0:T(8,128)(2,1)S(1)}, bf16[512,512]{1,0:T(8,128)(2,1)S(1)}, u32[]{:S(2)}, u32[]{:S(2)}) collective-permute-start(bf16[512,512]{1,0:T(8,128)(2,1)S(1)} %get-tuple-element.58), channel_id=1, source_target_pairs={{0,30},{1,31},{2,4},{3,5},{4,2},{5,3},{6,8},{7,9},{8,6},{9,7},{10,... | collective-permute-start | bytes 1572872 | tf_op jit(solution)/shard_map/ppermute | solution.py:27
  15.7 0.0 collective-permute-start.5
  15.7 2.3 %rim3.1 = (bf16[512,1024]{1,0:T(8,128)(2,1)S(1)}, bf16[512,512]{1,0:T(8,128)(2,1)S(1)}) custom-call(bf16[2048,1024]{1,0:T(8,128)(2,1)} %refs_0_.7, bf16[3,1024,512]{2,1,0:T(8,128)(2,1)} %refs_4_.8), custom_call_target="tpu_custom_call" | custom-call | flops 536870912 | bytes 7340032 | tf_op jit(solution)/shard_map/rim3/pallas_call | solution.py:50
  18.0 0.9 %collective-permute-start.1 = (bf16[512,512]{1,0:T(8,128)(2,1)S(1)}, bf16[512,512]{1,0:T(8,128)(2,1)S(1)}, u32[]{:S(2)}, u32[]{:S(2)}) collective-permute-start(bf16[512,512]{1,0:T(8,128)(2,1)S(1)} %get-tuple-element.50), channel_id=1, source_target_pairs={{0,1},{1,0},{2,3},{3,2},{4,5},{5,4},{6,7},{7,6},{8,9},{9,8},{10,11... | collective-permute-start | bytes 1572872 | tf_op jit(solution)/shard_map/ppermute | solution.py:27
  18.9 0.0 copy-done.1
  18.9 5.0 %layer2.1 = (bf16[512,1024]{1,0:T(8,128)(2,1)S(1)}, bf16[512,1024]{1,0:T(8,128)(2,1)S(1)}, bf16[512,512]{1,0:T(8,128)(2,1)S(1)}, bf16[512,512]{1,0:T(8,128)(2,1)S(1)}) custom-call(bf16[2048,1024]{1,0:T(8,128)(2,1)} %refs_0_.7, bf16[512,1024]{1,0:T(8,128)(2,1)S(1)} %get-tuple-element.41.refs_1_.refs_2_, ...), custom_call_target="tpu_custom_call" | custom-call | flops 3221225472 | bytes 14686208 | tf_op jit(solution)/shard_map/layer2/pallas_call | solution.py:50
  23.9 3.8 %collective-permute-start.2 = (bf16[512,512]{1,0:T(8,128)(2,1)S(1)}, bf16[512,512]{1,0:T(8,128)(2,1)S(1)}, u32[]{:S(2)}, u32[]{:S(2)}) collective-permute-start(bf16[512,512]{1,0:T(8,128)(2,1)S(1)} %get-tuple-element.54), channel_id=1, source_target_pairs={{0,30},{1,31},{2,4},{3,5},{4,2},{5,3},{6,8},{7,9},{8,6},{9,7},{10,... | collective-permute-start | bytes 1572872 | tf_op jit(solution)/shard_map/ppermute | solution.py:27
  27.7 0.0 collective-permute-done.refs_3_
  27.7 0.0 collective-permute-start.3
  27.7 3.8 %layer0.1 = (bf16[512,1024]{1,0:T(8,128)(2,1)S(1)}, bf16[512,1024]{1,0:T(8,128)(2,1)S(1)}, bf16[512,512]{1,0:T(8,128)(2,1)S(1)}, bf16[512,512]{1,0:T(8,128)(2,1)S(1)}) custom-call(bf16[2048,1024]{1,0:T(8,128)(2,1)} %refs_0_.7, bf16[512,1024]{1,0:T(8,128)(2,1)S(1)} %get-tuple-element.39.refs_1_, bf16[512,1024]{1,0:T(8,128)(2,1)S(1)} %get-tuple-element.41.refs_1_.refs_2_, ...), custom_call_target="tpu_custom_call" | custom-call | flops 3221225472 | bytes 14161920 | tf_op jit(solution)/shard_map/layer0/pallas_call | solution.py:50
  31.5 1.6 %collective-permute-done.4.one_side_ref = bf16[512,512]{1,0:T(8,128)(2,1)S(1)} collective-permute-done((bf16[512,512]{1,0:T(8,128)(2,1)S(1)}, bf16[512,512]{1,0:T(8,128)(2,1)S(1)}, u32[]{:S(2)}, u32[]{:S(2)}) %collective-permute-start.4) | collective-permute-done | bytes 524320 | tf_op jit(solution)/shard_map/ppermute | solution.py:27
  33.1 5.5 %collective-permute-start.10 = (bf16[512,512]{1,0:T(8,128)(2,1)S(1)}, bf16[512,512]{1,0:T(8,128)(2,1)S(1)}, u32[]{:S(2)}, u32[]{:S(2)}) collective-permute-start(bf16[512,512]{1,0:T(8,128)(2,1)S(1)} %get-tuple-element.69), channel_id=1, source_target_pairs={{0,30},{1,31},{2,4},{3,5},{4,2},{5,3},{6,8},{7,9},{8,6},{9,7},{10,... | collective-permute-start | bytes 1572872 | tf_op jit(solution)/shard_map/ppermute | solution.py:27
  38.5 0.0 collective-permute-done.1.refs_3_
  38.6 0.0 copy-start.8
  38.6 0.0 collective-permute-start.11
  38.6 4.6 %layer3.1 = (bf16[512,1024]{1,0:T(8,128)(2,1)S(1)}, bf16[512,1024]{1,0:T(8,128)(2,1)S(1)}, bf16[256,512]{1,0:T(8,128)(2,1)S(1)}, bf16[256,512]{1,0:T(8,128)(2,1)...) custom-call(bf16[2048,1024]{1,0:T(8,128)(2,1)} %refs_0_.7, ...), custom_call_target="tpu_custom_call" | custom-call | flops 3221225472 | bytes 14161920 | tf_op jit(solution)/shard_map/layer3/pallas_call | solution.py:50
  43.1 0.0 copy-start.3
  43.1 0.0 copy-start.5
  43.1 0.0 copy-done.8
  43.2 2.3 %centre.1 = (f32[512,512]{1,0:T(8,128)S(1)}, f32[512,512]{1,0:T(8,128)S(1)}, f32[512,512]{1,0:T(8,128)S(1)}, f32[512,512]{1,0:T(8,128)S(1)}) custom-call(bf16[512,1024]{1,0:T(8,128)(2,1)S(1)} %get-tuple-element.40.refs_0_, bf16[512,1024]{1,0:T(8,128)(2,1)S(1)} %get-tuple-element.47.refs_1_, bf16[512,1024]{1,0:T(8,128)(2,1)S(1)} %get-tuple-element.49.refs_2_, ...), custom_call_target="tpu_custom_call" | custom-call | flops 2147483648 | bytes 7342080 | tf_op jit(solution)/shard_map/centre/pallas_call | solution.py:50
  45.5 0.0 collective-permute-done.5.other_side_ref
  45.5 0.2 collective-permute-start.8
  45.7 0.0 copy-done.3
  45.7 0.0 copy-done.5
  45.7 1.8 %finish1.1.rest_0_ = bf16[2048,1024]{1,0:T(8,128)(2,1)} custom-call(f32[512,512]{1,0:T(8,128)S(1)} %get-tuple-element.57.centre_ref, bf16[512,512]{1,0:T(8,128)(2,1)S(1)} %collective-permute-done.4.one_side_ref, bf16[512,512]{1,0:T(8,128)(2,1)S(1)} %collective-permute-done.5.other_side_ref, bf16[512,1024]{1,0:T(8,128)(2,1)S(1)} %get-tuple-element.60.one_ref, ...), custom_call_target="tpu_custom_call" | custom-call | flops 536870912 | bytes 4198400 | tf_op jit(solution)/shard_map/finish1/pallas_call | solution.py:50
  47.5 0.0 collective-permute-done.2.one_side_ref
  47.5 2.0 %collective-permute-start.9 = (bf16[256,512]{1,0:T(8,128)(2,1)S(1)}, bf16[256,512]{1,0:T(8,128)(2,1)S(1)}, u32[]{:S(2)}, u32[]{:S(2)}) collective-permute-start(bf16[256,512]{1,0:T(8,128)(2,1)S(1)} %get-tuple-element.67), channel_id=1, source_target_pairs={{0,2},{1,3},{2,0},{3,1},{4,6},{5,7},{6,4},{7,5},{8,10},{9,11},{10,... | collective-permute-start | bytes 786440 | tf_op jit(solution)/shard_map/ppermute | solution.py:27
  49.5 0.0 collective-permute-done.3.other_side_ref
  49.5 1.8 %finish2.1.rest_0_ = bf16[2048,1024]{1,0:T(8,128)(2,1)} custom-call(f32[512,512]{1,0:T(8,128)S(1)} %get-tuple-element.53.centre_ref, bf16[512,512]{1,0:T(8,128)(2,1)S(1)} %collective-permute-done.2.one_side_ref, bf16[512,512]{1,0:T(8,128)(2,1)S(1)} %collective-permute-done.3.other_side_ref, ...), custom_call_target="tpu_custom_call", output_to_operand_aliasing={{}: (6, {})} | custom-call | flops 536870912 | bytes 8392704 | tf_op jit(solution)/shard_map/finish2/pallas_call | solution.py:50
  51.4 3.4 %collective-permute-start.6 = (bf16[256,512]{1,0:T(8,128)(2,1)S(1)}, bf16[256,512]{1,0:T(8,128)(2,1)S(1)}, u32[]{:S(2)}, u32[]{:S(2)}) collective-permute-start(bf16[256,512]{1,0:T(8,128)(2,1)S(1)} %get-tuple-element.63), channel_id=1, source_target_pairs={{0,30},{1,31},{2,4},{3,5},{4,2},{5,3},{6,8},{7,9},{8,6},{9,7},{10,... | collective-permute-start | bytes 786440 | tf_op jit(solution)/shard_map/ppermute | solution.py:27
  54.8 0.8 %collective-permute-done.10.one_side_ref = bf16[512,512]{1,0:T(8,128)(2,1)S(1)} collective-permute-done((bf16[512,512]{1,0:T(8,128)(2,1)S(1)}, bf16[512,512]{1,0:T(8,128)(2,1)S(1)}, u32[]{:S(2)}, u32[]{:S(2)}) %collective-permute-start.10) | collective-permute-done | bytes 524320 | tf_op jit(solution)/shard_map/ppermute | solution.py:27
  55.5 0.0 collective-permute-start.7
  55.5 0.0 collective-permute-done.11.other_side_ref
  55.5 1.8 %finish0.1.rest_0_ = bf16[2048,1024]{1,0:T(8,128)(2,1)} custom-call(f32[512,512]{1,0:T(8,128)S(1)} %get-tuple-element.68.centre_ref, bf16[512,512]{1,0:T(8,128)(2,1)S(1)} %collective-permute-done.10.one_side_ref, bf16[512,512]{1,0:T(8,128)(2,1)S(1)} %collective-permute-done.11.other_side_ref, ...), custom_call_target="tpu_custom_call", output_to_operand_aliasing={{}: (6, {})} | custom-call | flops 536870912 | bytes 8392704 | tf_op jit(solution)/shard_map/finish0/pallas_call | solution.py:50
  57.4 3.8 %collective-permute-done.8.one_side_ref = bf16[256,512]{1,0:T(8,128)(2,1)S(1)} collective-permute-done((bf16[256,512]{1,0:T(8,128)(2,1)S(1)}, bf16[256,512]{1,0:T(8,128)(2,1)S(1)}, u32[]{:S(2)}, u32[]{:S(2)}) %collective-permute-start.8) | collective-permute-done | bytes 262176 | tf_op jit(solution)/shard_map/ppermute | solution.py:27
  61.2 0.0 collective-permute-done.9.other_side_ref
  61.2 1.3 %finish3.2.rest_0_ = bf16[2048,1024]{1,0:T(8,128)(2,1)} custom-call(f32[512,512]{1,0:T(8,128)S(1)} %get-tuple-element.52.centre_ref, bf16[256,512]{1,0:T(8,128)(2,1)S(1)} %collective-permute-done.8.one_side_ref, bf16[256,512]{1,0:T(8,128)(2,1)S(1)} %collective-permute-done.9.other_side_ref, ...), custom_call_target="tpu_custom_call", output_to_operand_aliasing={{}: (6, {})} | custom-call | flops 268435456 | bytes 7868416 | tf_op jit(solution)/shard_map/finish3/pallas_call | solution.py:50
  62.5 2.8 %collective-permute-done.6.one_side_ref = bf16[256,512]{1,0:T(8,128)(2,1)S(1)} collective-permute-done((bf16[256,512]{1,0:T(8,128)(2,1)S(1)}, bf16[256,512]{1,0:T(8,128)(2,1)S(1)}, u32[]{:S(2)}, u32[]{:S(2)}) %collective-permute-start.6) | collective-permute-done | bytes 262176 | tf_op jit(solution)/shard_map/ppermute | solution.py:27
  65.3 0.0 collective-permute-done.7.other_side_ref
  65.3 1.3 %finish3.3 = bf16[2048,1024]{1,0:T(8,128)(2,1)} custom-call(f32[512,512]{1,0:T(8,128)S(1)} %get-tuple-element.52.centre_ref, bf16[256,512]{1,0:T(8,128)(2,1)S(1)} %collective-permute-done.6.one_side_ref, bf16[256,512]{1,0:T(8,128)(2,1)S(1)} %collective-permute-done.7.other_side_ref, ...), custom_call_target="tpu_custom_call", output_to_operand_aliasing={{}: (6, {})} | custom-call | flops 268435456 | bytes 7868416 | tf_op jit(solution)/shard_map/finish3/pallas_call | solution.py:50
Async XLA Ops:
  0.0 9.2 %copy-start = (bf16[3,1024,512]{2,1,0:T(8,128)(2,1)S(1)}, bf16[3,1024,512]{2,1,0:T(8,128)(2,1)}, u32[]{:S(2)}) copy-start(bf16[3,1024,512]{2,1,0:T(8,128)(2,1)} %refs_4_.8) | copy-start | bytes 9437188
  0.0 9.2 %copy-start.2 = (bf16[3,1024,512]{2,1,0:T(8,128)(2,1)S(1)}, bf16[3,1024,512]{2,1,0:T(8,128)(2,1)}, u32[]{:S(2)}) copy-start(bf16[3,1024,512]{2,1,0:T(8,128)(2,1)} %refs_4_.9) | copy-start | bytes 9437188
  0.0 9.2 %copy-start.4 = (bf16[512,1024]{1,0:T(8,128)(2,1)S(1)}, bf16[512,1024]{1,0:T(8,128)(2,1)}, u32[]{:S(2)}) copy-start(bf16[512,1024]{1,0:T(8,128)(2,1)} %refs_6_.7) | copy-start | bytes 3145732
  0.0 9.2 %copy-start.6 = (f32[1024]{0:T(1024)S(1)}, f32[1024]{0:T(1024)}, u32[]{:S(2)}) copy-start(f32[1024]{0:T(1024)} %param.13) | copy-start | bytes 12292
  0.0 9.2 %copy-start.7 = (f32[512]{0:T(512)S(1)}, f32[512]{0:T(512)}, u32[]{:S(2)}) copy-start(f32[512]{0:T(512)} %param.11) | copy-start | bytes 6148
  2.4 25.3 %collective-permute-start = (bf16[512,512]{1,0:T(8,128)(2,1)S(1)}, bf16[512,512]{1,0:T(8,128)(2,1)S(1)}, u32[]{:S(2)}, u32[]{:S(2)}) collective-permute-start(bf16[512,512]{1,0:T(8,128)(2,1)S(1)} %get-tuple-element.48), channel_id=1, source_target_pairs={{0,31},{1,2},{2,1},{3,4},{4,3},{5,6},{6,5},{7,8},{8,7},{9,10},{10,... | collective-permute-start | bytes 1572872 | tf_op jit(solution)/shard_map/ppermute | solution.py:27
  14.8 4.1 %copy-start.1 = (bf16[3,1024,512]{2,1,0:T(8,128)(2,1)S(1)}, bf16[3,1024,512]{2,1,0:T(8,128)(2,1)}, u32[]{:S(2)}) copy-start(bf16[3,1024,512]{2,1,0:T(8,128)(2,1)} %refs_4_.8) | copy-start | bytes 9437188
  14.8 18.2 %collective-permute-start.4 = (bf16[512,512]{1,0:T(8,128)(2,1)S(1)}, bf16[512,512]{1,0:T(8,128)(2,1)S(1)}, u32[]{:S(2)}, u32[]{:S(2)}) collective-permute-start(bf16[512,512]{1,0:T(8,128)(2,1)S(1)} %get-tuple-element.58), channel_id=1, source_target_pairs={{0,30},{1,31},{2,4},{3,5},{4,2},{5,3},{6,8},{7,9},{8,6},{9,7},{10,... | collective-permute-start | bytes 1572872 | tf_op jit(solution)/shard_map/ppermute | solution.py:27
  15.7 29.8 %collective-permute-start.5 = (bf16[512,512]{1,0:T(8,128)(2,1)S(1)}, bf16[512,512]{1,0:T(8,128)(2,1)S(1)}, u32[]{:S(2)}, u32[]{:S(2)}) collective-permute-start(bf16[512,512]{1,0:T(8,128)(2,1)S(1)} %get-tuple-element.59), channel_id=1, source_target_pairs={{0,2},{1,3},{2,0},{3,1},{4,6},{5,7},{6,4},{7,5},{8,10},{9,11},{10,... | collective-permute-start | bytes 1572872 | tf_op jit(solution)/shard_map/ppermute | solution.py:27
  18.0 20.5 %collective-permute-start.1 = (bf16[512,512]{1,0:T(8,128)(2,1)S(1)}, bf16[512,512]{1,0:T(8,128)(2,1)S(1)}, u32[]{:S(2)}, u32[]{:S(2)}) collective-permute-start(bf16[512,512]{1,0:T(8,128)(2,1)S(1)} %get-tuple-element.50), channel_id=1, source_target_pairs={{0,1},{1,0},{2,3},{3,2},{4,5},{5,4},{6,7},{7,6},{8,9},{9,8},{10,11... | collective-permute-start | bytes 1572872 | tf_op jit(solution)/shard_map/ppermute | solution.py:27
  23.9 23.6 %collective-permute-start.2 = (bf16[512,512]{1,0:T(8,128)(2,1)S(1)}, bf16[512,512]{1,0:T(8,128)(2,1)S(1)}, u32[]{:S(2)}, u32[]{:S(2)}) collective-permute-start(bf16[512,512]{1,0:T(8,128)(2,1)S(1)} %get-tuple-element.54), channel_id=1, source_target_pairs={{0,30},{1,31},{2,4},{3,5},{4,2},{5,3},{6,8},{7,9},{8,6},{9,7},{10,... | collective-permute-start | bytes 1572872 | tf_op jit(solution)/shard_map/ppermute | solution.py:27
  27.7 21.8 %collective-permute-start.3 = (bf16[512,512]{1,0:T(8,128)(2,1)S(1)}, bf16[512,512]{1,0:T(8,128)(2,1)S(1)}, u32[]{:S(2)}, u32[]{:S(2)}) collective-permute-start(bf16[512,512]{1,0:T(8,128)(2,1)S(1)} %get-tuple-element.55), channel_id=1, source_target_pairs={{0,2},{1,3},{2,0},{3,1},{4,6},{5,7},{6,4},{7,5},{8,10},{9,11},{10,... | collective-permute-start | bytes 1572872 | tf_op jit(solution)/shard_map/ppermute | solution.py:27
  33.1 22.5 %collective-permute-start.10 = (bf16[512,512]{1,0:T(8,128)(2,1)S(1)}, bf16[512,512]{1,0:T(8,128)(2,1)S(1)}, u32[]{:S(2)}, u32[]{:S(2)}) collective-permute-start(bf16[512,512]{1,0:T(8,128)(2,1)S(1)} %get-tuple-element.69), channel_id=1, source_target_pairs={{0,30},{1,31},{2,4},{3,5},{4,2},{5,3},{6,8},{7,9},{8,6},{9,7},{10,... | collective-permute-start | bytes 1572872 | tf_op jit(solution)/shard_map/ppermute | solution.py:27
  38.6 4.6 %copy-start.8 = (f32[512]{0:T(512)S(1)}, f32[512]{0:T(512)}, u32[]{:S(2)}) copy-start(f32[512]{0:T(512)} %param.15) | copy-start | bytes 6148
  38.6 17.0 %collective-permute-start.11 = (bf16[512,512]{1,0:T(8,128)(2,1)S(1)}, bf16[512,512]{1,0:T(8,128)(2,1)S(1)}, u32[]{:S(2)}, u32[]{:S(2)}) collective-permute-start(bf16[512,512]{1,0:T(8,128)(2,1)S(1)} %get-tuple-element.70), channel_id=1, source_target_pairs={{0,2},{1,3},{2,0},{3,1},{4,6},{5,7},{6,4},{7,5},{8,10},{9,11},{10,... | collective-permute-start | bytes 1572872 | tf_op jit(solution)/shard_map/ppermute | solution.py:27
  43.1 2.6 %copy-start.3 = (bf16[512,1024]{1,0:T(8,128)(2,1)S(1)}, bf16[512,1024]{1,0:T(8,128)(2,1)}, u32[]{:S(2)}) copy-start(bf16[512,1024]{1,0:T(8,128)(2,1)} %point_ref.9) | copy-start | bytes 3145732
  43.1 2.6 %copy-start.5 = (f32[1024]{0:T(1024)S(1)}, f32[1024]{0:T(1024)}, u32[]{:S(2)}) copy-start(f32[1024]{0:T(1024)} %param.17) | copy-start | bytes 12292
  45.5 15.6 %collective-permute-start.8 = (bf16[256,512]{1,0:T(8,128)(2,1)S(1)}, bf16[256,512]{1,0:T(8,128)(2,1)S(1)}, u32[]{:S(2)}, u32[]{:S(2)}) collective-permute-start(bf16[256,512]{1,0:T(8,128)(2,1)S(1)} %get-tuple-element.66), channel_id=1, source_target_pairs={{0,30},{1,31},{2,4},{3,5},{4,2},{5,3},{6,8},{7,9},{8,6},{9,7},{10,... | collective-permute-start | bytes 786440 | tf_op jit(solution)/shard_map/ppermute | solution.py:27
  47.5 13.6 %collective-permute-start.9 = (bf16[256,512]{1,0:T(8,128)(2,1)S(1)}, bf16[256,512]{1,0:T(8,128)(2,1)S(1)}, u32[]{:S(2)}, u32[]{:S(2)}) collective-permute-start(bf16[256,512]{1,0:T(8,128)(2,1)S(1)} %get-tuple-element.67), channel_id=1, source_target_pairs={{0,2},{1,3},{2,0},{3,1},{4,6},{5,7},{6,4},{7,5},{8,10},{9,11},{10,... | collective-permute-start | bytes 786440 | tf_op jit(solution)/shard_map/ppermute | solution.py:27
  51.4 13.9 %collective-permute-start.6 = (bf16[256,512]{1,0:T(8,128)(2,1)S(1)}, bf16[256,512]{1,0:T(8,128)(2,1)S(1)}, u32[]{:S(2)}, u32[]{:S(2)}) collective-permute-start(bf16[256,512]{1,0:T(8,128)(2,1)S(1)} %get-tuple-element.63), channel_id=1, source_target_pairs={{0,30},{1,31},{2,4},{3,5},{4,2},{5,3},{6,8},{7,9},{8,6},{9,7},{10,... | collective-permute-start | bytes 786440 | tf_op jit(solution)/shard_map/ppermute | solution.py:27
  55.5 9.8 %collective-permute-start.7 = (bf16[256,512]{1,0:T(8,128)(2,1)S(1)}, bf16[256,512]{1,0:T(8,128)(2,1)S(1)}, u32[]{:S(2)}, u32[]{:S(2)}) collective-permute-start(bf16[256,512]{1,0:T(8,128)(2,1)S(1)} %get-tuple-element.64), channel_id=1, source_target_pairs={{0,2},{1,3},{2,0},{3,1},{4,6},{5,7},{6,4},{7,5},{8,10},{9,11},{10,... | collective-permute-start | bytes 786440 | tf_op jit(solution)/shard_map/ppermute | solution.py:27

commit v6 on v4

--- a/solution.py
+++ b/solution.py
@@ -13,6 +13,7 @@
 HBM = pl.BlockSpec(memory_space=pltpu.HBM)
 SLOPE = math.sqrt(2.0 / math.pi)
 LAST_PIECE = 128
+RELAY = 128
 BF16 = jnp.bfloat16
 F32 = jnp.float32
 
@@ -64,38 +65,118 @@
     return jax.ShapeDtypeStruct((rows, columns), dtype)
 
 
-def rim(x, taps, quarter):
+def rim_activations(x_ref, taps_ref, tap, quarter, act_ref, x_own, tap_own, sems, put):
+    size = x_own.shape[0]
+    half = size // 2
+    top, bottom = pl.ds(0, half), pl.ds(half, half)
+    which = tap + odd_position() * (2 - 2 * tap)
+    start = quarter_rows(quarter, size).start
+    copies = []
+    for k in range(2):
+        rows = pl.ds(pl.multiple_of(start + k * half, half), half)
+        copies.append(pltpu.make_async_copy(x_ref.at[rows], x_own.at[pl.ds(k * half, half)], sems.at[k]))
+    copies.insert(1, pltpu.make_async_copy(taps_ref.at[which], tap_own, sems.at[2]))
+    for copy in copies:
+        copy.start()
+    copies[0].wait()
+    act_ref[top, :] = gelu(x_own[top, :].astype(F32)).astype(BF16)
+    copies[1].wait()
+    copies[2].wait()
+    put(0, dot(act_ref[top, :], tap_own[...]).astype(BF16))
+    act_ref[bottom, :] = gelu(x_own[bottom, :].astype(F32)).astype(BF16)
+    put(1, dot(act_ref[bottom, :], tap_own[...]).astype(BF16))
+
+
+def rim_scratch(size, c, m):
+    return [pltpu.VMEM((size, c), BF16), pltpu.VMEM((c, m), BF16), pltpu.SemaphoreType.DMA((3,))]
+
+
+def pair_rim(x, taps):
     size, (c, m) = x.shape[0] // 4, taps.shape[1:]
     half = size // 2
-    top, bottom = pl.ds(0, half), pl.ds(half, half)
-    tap = 2 if quarter == 0 else 0
-
-    def body(x_ref, taps_ref, act_ref, product_ref, x_own, tap_own, sems):
-        which = tap + odd_position() * (2 - 2 * tap)
-        start = quarter_rows(quarter, size).start
-
-        def rows(k):
-            return pl.ds(pl.multiple_of(start + k * half, half), half)
-
-        first, tap_copy, second = (
-            pltpu.make_async_copy(x_ref.at[rows(0)], x_own.at[top], sems.at[0]),
-            pltpu.make_async_copy(taps_ref.at[which], tap_own, sems.at[1]),
-            pltpu.make_async_copy(x_ref.at[rows(1)], x_own.at[bottom], sems.at[2]),
-        )
-        for copy in (first, tap_copy, second):
+
+    def body(x_ref, taps_ref, act_ref, direct_ref, relay_ref, *scratch):
+        def put(k, product):
+            if k == 0:
+                direct_ref[:half, :] = product
+            else:
+                direct_ref[half:, :] = product[: half - RELAY, :]
+                relay_ref[...] = product[half - RELAY :, :]
+
+        rim_activations(x_ref, taps_ref, 2, 0, act_ref, *scratch, put)
+
+    return call(
+        body, "rim0", [shape(size, c), shape(size - RELAY, m), shape(RELAY, m)], (x, taps), 2 * size * c * m,
+        rim_scratch(size, c, m), specs=[HBM] * 2,
+    )
+
+
+def partner_rim(x, taps):
+    size, (c, m) = x.shape[0] // 4, taps.shape[1:]
+    half = size // 2
+
+    def body(x_ref, taps_ref, act_ref, product_ref, *scratch):
+        def put(k, product):
+            product_ref[k * half : (k + 1) * half, :] = product
+
+        rim_activations(x_ref, taps_ref, 0, 3, act_ref, *scratch, put)
+
+    return call(
+        body, "rim3", [shape(size, c), shape(size, m)], (x, taps), 2 * size * c * m, rim_scratch(size, c, m),
+        specs=[HBM] * 2,
+    )
+
+
+def first_product(far, outer):
+    size, c = far.shape
+    m = outer.shape[2]
+
+    def body(far_ref, outer_ref, first_ref):
+        first_ref[...] = dot(far_ref[...], outer_ref[2 * odd_pair()]).astype(BF16)
+
+    return call(body, "first1", [shape(size, m)], (far, outer), 2 * size * c * m, [], specs=[VMEM] * 2)[0]
+
+
+def odd_pair():
+    return lax.rem(lax.div(lax.axis_index("seq"), 2), 2)
+
+
+def first_quarter(x, act, weights):
+    taps, bias_conv, point, bias_point, outer = weights
+    size, (c, m) = x.shape[0] // 4, taps.shape[1:]
+
+    def body(
+        x_ref, before_ref, taps_ref, bias_conv_ref, point_hbm, bias_point_ref, outer_hbm,
+        act1_ref, act2_ref, one_ref, far_ref, second_ref, point_own, outer_own, sems,
+    ):
+        copies = [
+            pltpu.make_async_copy(point_hbm, point_own, sems.at[0]),
+            pltpu.make_async_copy(outer_hbm.at[2 - 2 * odd_pair()], outer_own, sems.at[1]),
+        ]
+        for copy in copies:
             copy.start()
-        first.wait()
-        act_ref[top, :] = gelu(x_own[top, :].astype(F32)).astype(BF16)
-        tap_copy.wait()
-        second.wait()
-        product_ref[top, :] = dot(act_ref[top, :], tap_own[...]).astype(BF16)
-        act_ref[bottom, :] = gelu(x_own[bottom, :].astype(F32)).astype(BF16)
-        product_ref[bottom, :] = dot(act_ref[bottom, :], tap_own[...]).astype(BF16)
-
+        odd = odd_position()
+        total = dot(before_ref[...], taps_ref[2 * odd])
+        act1_ref[...] = gelu(x_ref[quarter_rows(1, size), :].astype(F32)).astype(BF16)
+        total = total + dot(act1_ref[...], taps_ref[1])
+        act2_ref[...] = gelu(x_ref[quarter_rows(2, size), :].astype(F32)).astype(BF16)
+        total = total + dot(act2_ref[...], taps_ref[2 - 2 * odd])
+        mid = gelu(total + bias_conv_ref[...]).astype(BF16)
+        copies[0].wait()
+        one = x_ref[quarter_rows(1, size), :].astype(F32) + dot(mid, point_own[...]) + bias_point_ref[...]
+        one = one.astype(BF16)
+        one_ref[...] = one
+        far = gelu(one.astype(F32)).astype(BF16)
+        far_ref[...] = far
+        copies[1].wait()
+        second_ref[...] = dot(far, outer_own[...]).astype(BF16)
+
+    point, outer = (pltpu.with_memory_space_constraint(w, pltpu.HBM) for w in (point, outer))
+    args = (x, act, taps, bias_conv, point, bias_point, outer)
     return call(
-        body, f"rim{quarter}", [shape(size, c), shape(size, m)], (x, taps), 2 * size * c * m,
-        [pltpu.VMEM((size, c), BF16), pltpu.VMEM((c, m), BF16), pltpu.SemaphoreType.DMA((3,))],
-        specs=[HBM] * 2,
+        body, "layer1", [shape(size, c)] * 4 + [shape(size, m)], args, 10 * size * c * m,
+        [pltpu.VMEM((m, c), BF16), pltpu.VMEM((c, m), BF16), pltpu.SemaphoreType.DMA((2,))],
+        specs=[VMEM] * 4 + [HBM, VMEM, HBM],
     )
 
 
@@ -105,8 +186,8 @@
     one_ref[...] = one
     act = gelu(one.astype(F32)).astype(BF16)
     act_ref[...] = act
-    odd_pair = lax.rem(lax.div(lax.axis_index("seq"), 2), 2)
-    for tap, pieces in zip((2 * odd_pair, 2 - 2 * odd_pair), product_refs):
+    odd = odd_pair()
+    for tap, pieces in zip((2 * odd, 2 - 2 * odd), product_refs):
         product = dot(act, outer[tap]).astype(BF16)
         at = 0
         for ref in pieces:
@@ -114,51 +195,48 @@
             at += ref.shape[0]
 
 
-def layer(x, quarter, acts, arrived, weights, pieces, fresh=False):
+def layer(x, quarter, acts, arrived, weights, pieces):
     taps, bias_conv, point, bias_point, outer = weights
     size, (c, m) = x.shape[0] // 4, taps.shape[1:]
     given = [a for a in acts if a is not None]
     known = [a is not None for a in acts]
-    loads = (quarter, quarter + 1) if fresh else (quarter,)
     n = len(pieces)
 
     def body(*refs):
         refs = list(refs)
         x_ref = refs.pop(0)
         sources = [refs.pop(0) if k else None for k in known]
-        arrived_ref = None if arrived is None else refs.pop(0)
+        arrived_refs = [refs.pop(0) for _ in arrived]
         taps_ref, bias_conv_ref, point_ref, bias_point_ref, outer_ref = refs[:5]
         refs = refs[5:]
-        made = [refs.pop(0), refs.pop(0)] if fresh else []
         one_ref, act_ref = refs[:2]
         product_refs = refs[2 : 2 + n], refs[2 + n : 2 + 2 * n]
-        x_own, sems = refs[2 + 2 * n :]
+        x_own, sem = refs[2 + 2 * n :]
         odd = odd_position()
-        copies = [
-            pltpu.make_async_copy(x_ref.at[quarter_rows(q, size)], x_own.at[k], sems.at[k]) for k, q in enumerate(loads)
-        ]
-        for copy in copies:
-            copy.start()
-        total = None if arrived is None else arrived_ref[...].astype(F32)
+        copy = pltpu.make_async_copy(x_ref.at[quarter_rows(quarter, size)], x_own, sem)
+        copy.start()
+        total = None
         for k, source in enumerate(sources):
-            if fresh and k > 0:
-                source = made[k - 1]
-                copies[k - 1].wait()
-                source[...] = gelu(x_own[k - 1].astype(F32)).astype(BF16)
             if source is not None:
                 term = dot(source[...], taps_ref[k + odd * (2 - 2 * k)])
                 total = term if total is None else total + term
-        if not fresh:
-            copies[0].wait()
+        if arrived:
+            parts, missing = [], size
+            for ref, (_, first) in zip(arrived_refs, arrived):
+                rows = min(ref.shape[0] - first, missing)
+                parts.append(ref[first : first + rows, :].astype(F32))
+                missing -= rows
+            total = total + (parts[0] if len(parts) == 1 else jnp.concatenate(parts, axis=0))
+        copy.wait()
         after_total(
-            total + bias_conv_ref[...], x_own[0], point_ref, bias_point_ref, outer_ref, one_ref, act_ref, product_refs
+            total + bias_conv_ref[...], x_own[...], point_ref, bias_point_ref, outer_ref, one_ref, act_ref, product_refs
         )
 
-    args = [x] + given + ([] if arrived is None else [arrived]) + list(weights)
-    outs = ([shape(size, c)] * 2 if fresh else []) + [shape(size, c)] * 2 + [shape(rows, m) for rows in pieces] * 2
+    args = [x] + given + [value for value, _ in arrived] + list(weights)
+    outs = [shape(size, c)] * 2 + [shape(rows, m) for rows in pieces] * 2
     results = call(
         body, f"layer{quarter}", outs, args, 12 * size * c * m,
-        [pltpu.VMEM((len(loads), size, c), BF16), pltpu.SemaphoreType.DMA((len(loads),))],
+        [pltpu.VMEM((size, c), BF16), pltpu.SemaphoreType.DMA],
         specs=[HBM] + [VMEM] * (len(args) - 1),
     )
     return *results[: -2 * n], list(zip(results[-2 * n : -n], results[-n:]))
@@ -226,25 +304,40 @@
     near = (first_conv_taps, first_conv_bias[None, :], first_point_weight, first_point_bias[None, :], second_conv_taps)
     x = pltpu.with_memory_space_constraint(tower_input, pltpu.HBM)
     rim_taps = pltpu.with_memory_space_constraint(first_conv_taps, pltpu.HBM)
-    act0, to_pair = rim(x, rim_taps, 0)
-    from_pair = swap(to_pair, lambda i: i % 2 == 1, 1)
+
+    def to_partner(value):
+        return swap(value, lambda i: i % 2 == 0, 1)
+
+    def second_matching(value):
+        return swap(value, lambda i: i // 2 % 2 == 1, 2)
+
+    def first_matching(value):
+        return swap(value, lambda i: i // 2 % 2 == 0, 2)
 
     def send(products):
-        return [
-            (swap(second, lambda i: i // 2 % 2 == 1, 2), swap(first, lambda i: i // 2 % 2 == 0, 2))
-            for first, second in products
-        ]
-
-    act1, act2, one1, far1, products1 = layer(x, 1, (act0, None, None), None, near, whole, fresh=True)
-    later, products1 = lax.optimization_barrier((x, products1))
-    sides1 = send(products1)
-    act3, to_partner = rim(later, rim_taps, 3)
-    from_partner = swap(to_partner, lambda i: i % 2 == 0, 1)
-    one2, far2, products2 = layer(x, 2, (act1, act2, act3), None, near, whole)
+        return [(second_matching(second), first_matching(first)) for first, second in products]
+
+    act0, direct, relay = pair_rim(x, rim_taps)
+    handed = to_partner(relay)
+    from_pair = swap(direct, lambda i: i % 2 == 1, 1)
+    near_input, handed = lax.optimization_barrier((tower_input, handed))
+    relayed = swap(handed, lambda i: i % 2 == 0, 3)
+
+    act1, act2, one1, far1, second1 = first_quarter(near_input, act0, near)
+    far1, second1 = lax.optimization_barrier((far1, second1))
+    side1 = second_matching(second1)
+    later, relayed, first1 = lax.optimization_barrier((x, relayed, first_product(far1, second_conv_taps)))
+    returned = to_partner(relayed)
+    sides1 = [(side1, first_matching(first1))]
+    act3, for_partner = partner_rim(later, rim_taps)
+    from_partner = to_partner(for_partner)
+    one2, far2, products2 = layer(x, 2, (act1, act2, act3), [], near, whole)
     sides2 = send(products2)
-    one0, far0, products0 = layer(x, 0, (None, act0, act1), from_pair, near, whole)
+    one0, far0, products0 = layer(
+        x, 0, (None, act0, act1), [(from_pair, 0), (returned, 0)], near, whole
+    )
     sides0 = send(products0)
-    one3, far3, products3 = layer(x, 3, (act2, act3, None), from_partner, near, split)
+    one3, far3, products3 = layer(x, 3, (act2, act3, None), [(from_partner, 0)], near, split)
     sides3 = send(products3)
 
     centres = centre((far1, far2, far0, far3), second_conv_taps, second_conv_bias[None, :])

time: 67.3 us -> 78 us (1.16)
  starting transfers between devices: 23.5 us -> 29.3 us
  waiting for transfers between devices: 8.76 us -> 13.2 us
    ppermute x12 -> x15, starting transfers between devices: 23.5 us -> 29.3 us  [swap(): return lax.ppermute(value, 'seq', sorted(pairs))]
    ppermute x12 -> x15, waiting for transfers between devices: 8.76 us -> 13.2 us  [swap(): return lax.ppermute(value, 'seq', sorted(pairs))]
    pallas_call x12 -> x13, Pallas kernels: 34.1 us -> 34.8 us  [call(): pl.pallas_call(body, in_specs=specs, out_specs=[VMEM] * len(out_shape) if...]
  transfers between devices with their start and end apart: 12 -> 15, of which waited for: 4 -> 4; matrix products, arithmetic and copies ran while one was open for 0% -> 0% of each run, Pallas kernels for 46% -> 40%
where the time goes in v6:
time: 78 us; the launch traced here: 77.7 us
  Pallas kernels  34.8 us (45%)
  starting transfers between devices  29.3 us (38%)
  waiting for transfers between devices  13.2 us (17%)
    pallas_call x13, Pallas kernels, call(): pl.pallas_call(body, in_specs=specs, out_specs=[VMEM] * len(out_shape) if...  34.8 us
    ppermute x15, starting transfers between devices, swap(): return lax.ppermute(value, 'seq', sorted(pairs))  29.3 us
    ppermute x15, waiting for transfers between devices, swap(): return lax.ppermute(value, 'seq', sorted(pairs))  13.2 us
  transfers between devices with their start and end apart: 15, of which 4 were waited for; matrix products, arithmetic and copies ran while one was open for 0% of the time, Pallas kernels for 40%

profile of v6, /device:TPU:0, one launch (start us, length us, event | category | flops | bytes accessed | tf_op | source)
XLA Modules:
  0.0 77.7 jit_solution(15610272953719752869)
XLA Ops:
  0.0 0.0 copy-start.1
  0.0 0.0 copy-start
  0.0 0.0 copy-start.7
  0.0 0.0 copy-start.8
  0.0 2.4 %rim0.1 = (bf16[512,1024]{1,0:T(8,128)(2,1)S(1)}, bf16[384,512]{1,0:T(8,128)(2,1)S(1)}, bf16[128,512]{1,0:T(8,128)(2,1)S(1)}) custom-call(bf16[2048,1024]{1,0:T(8,128)(2,1)} %refs_0_.5, bf16[3,1024,512]{2,1,0:T(8,128)(2,1)} %refs_4_.4), custom_call_target="tpu_custom_call" | custom-call | flops 536870912 | bytes 7340032 | tf_op jit(solution)/shard_map/rim0/pallas_call | solution.py:51
  2.4 2.1 %collective-permute-start = (bf16[128,512]{1,0:T(8,128)(2,1)S(1)}, bf16[128,512]{1,0:T(8,128)(2,1)S(1)}, u32[]{:S(2)}, u32[]{:S(2)}) collective-permute-start(bf16[128,512]{1,0:T(8,128)(2,1)S(1)} %get-tuple-element.40), channel_id=1, source_target_pairs={{0,1},{1,0},{2,3},{3,2},{4,5},{5,4},{6,7},{7,6},{8,9},{9,8},{10,11... | collective-permute-start | bytes 393224 | tf_op jit(solution)/shard_map/ppermute | solution.py:28
  4.5 4.8 %collective-permute-start.2 = (bf16[384,512]{1,0:T(8,128)(2,1)S(1)}, bf16[384,512]{1,0:T(8,128)(2,1)S(1)}, u32[]{:S(2)}, u32[]{:S(2)}) collective-permute-start(bf16[384,512]{1,0:T(8,128)(2,1)S(1)} %get-tuple-element.52), channel_id=1, source_target_pairs={{0,31},{1,2},{2,1},{3,4},{4,3},{5,6},{6,5},{7,8},{8,7},{9,10},{10,... | collective-permute-start | bytes 1179656 | tf_op jit(solution)/shard_map/ppermute | solution.py:28
  9.3 6.4 %collective-permute-done = bf16[128,512]{1,0:T(8,128)(2,1)S(1)} collective-permute-done((bf16[128,512]{1,0:T(8,128)(2,1)S(1)}, bf16[128,512]{1,0:T(8,128)(2,1)S(1)}, u32[]{:S(2)}, u32[]{:S(2)}) %collective-permute-start) | collective-permute-done | bytes 131104 | tf_op jit(solution)/shard_map/ppermute | solution.py:28
  15.7 3.4 %collective-permute-start.1 = (bf16[128,512]{1,0:T(8,128)(2,1)S(1)}, bf16[128,512]{1,0:T(8,128)(2,1)S(1)}, u32[]{:S(2)}, u32[]{:S(2)}) collective-permute-start(bf16[128,512]{1,0:T(8,128)(2,1)S(1)} %collective-permute-done), channel_id=1, source_target_pairs={{0,3},{1,30},{2,5},{3,0},{4,7},{5,2},{6,9},{7,4},{8,11},{9,6},{10,... | collective-permute-start | bytes 393224 | tf_op jit(solution)/shard_map/ppermute | solution.py:28
  19.1 0.0 copy-done.1
  19.1 0.0 copy-done
  19.1 0.0 copy-done.7
  19.1 0.0 copy-done.8
  19.1 0.0 copy-start.3
  19.1 5.3 %layer1.1 = (bf16[512,1024]{1,0:T(8,128)(2,1)S(1)}, bf16[512,1024]{1,0:T(8,128)(2,1)S(1)}, bf16[512,1024]{1,0:T(8,128)(2,1)S(1)}, bf16[512,1024]{1,0:T(8,128)(2,1)S(1)}, bf16[512,512]{1,0:T(8,128)(2,1)S(1)}) custom-call(bf16[2048,1024]{1,0:T(8,128)(2,1)S(1)} %copy-done, bf16[512,1024]{1,0:T(8,128)(2,1)S(1)} %get-tuple-element.42.before_ref.refs_1_, ...), custom_call_target="tpu_custom_call" | custom-call | flops 2684354560 | bytes 12589056 | tf_op jit(solution)/shard_map/layer1/pallas_call | solution.py:51
  24.5 3.9 %collective-permute-start.13 = (bf16[512,512]{1,0:T(8,128)(2,1)S(1)}, bf16[512,512]{1,0:T(8,128)(2,1)S(1)}, u32[]{:S(2)}, u32[]{:S(2)}) collective-permute-start(bf16[512,512]{1,0:T(8,128)(2,1)S(1)} %get-tuple-element.72), channel_id=1, source_target_pairs={{0,30},{1,31},{2,4},{3,5},{4,2},{5,3},{6,8},{7,9},{8,6},{9,7},{10,... | collective-permute-start | bytes 1572872 | tf_op jit(solution)/shard_map/ppermute | solution.py:28
  28.4 0.0 copy-done.3
  28.4 0.7 first1.1
  29.1 0.0 copy-start.2
  29.1 0.0 copy-start.5
  29.2 0.0 collective-permute-done.1
  29.2 1.1 %collective-permute-start.3 = (bf16[128,512]{1,0:T(8,128)(2,1)S(1)}, bf16[128,512]{1,0:T(8,128)(2,1)S(1)}, u32[]{:S(2)}, u32[]{:S(2)}) collective-permute-start(bf16[128,512]{1,0:T(8,128)(2,1)S(1)} %collective-permute-done.1), channel_id=1, source_target_pairs={{0,1},{1,0},{2,3},{3,2},{4,5},{5,4},{6,7},{7,6},{8,9},{9,8},{10,11... | collective-permute-start | bytes 393224 | tf_op jit(solution)/shard_map/ppermute | solution.py:28
  30.2 0.0 collective-permute-start.14
  30.2 2.4 %rim3.1 = (bf16[512,1024]{1,0:T(8,128)(2,1)S(1)}, bf16[512,512]{1,0:T(8,128)(2,1)S(1)}) custom-call(bf16[2048,1024]{1,0:T(8,128)(2,1)} %refs_0_.5, bf16[3,1024,512]{2,1,0:T(8,128)(2,1)} %refs_4_.4), custom_call_target="tpu_custom_call" | custom-call | flops 536870912 | bytes 7340032 | tf_op jit(solution)/shard_map/rim3/pallas_call | solution.py:51
  32.7 1.1 %collective-permute-start.4 = (bf16[512,512]{1,0:T(8,128)(2,1)S(1)}, bf16[512,512]{1,0:T(8,128)(2,1)S(1)}, u32[]{:S(2)}, u32[]{:S(2)}) collective-permute-start(bf16[512,512]{1,0:T(8,128)(2,1)S(1)} %get-tuple-element.55), channel_id=1, source_target_pairs={{0,1},{1,0},{2,3},{3,2},{4,5},{5,4},{6,7},{7,6},{8,9},{9,8},{10,11... | collective-permute-start | bytes 1572872 | tf_op jit(solution)/shard_map/ppermute | solution.py:28
  33.7 0.0 copy-done.2
  33.7 0.0 copy-done.5
  33.7 5.0 %layer2.1 = (bf16[512,1024]{1,0:T(8,128)(2,1)S(1)}, bf16[512,1024]{1,0:T(8,128)(2,1)S(1)}, bf16[512,512]{1,0:T(8,128)(2,1)S(1)}, bf16[512,512]{1,0:T(8,128)(2,1)S(1)}) custom-call(bf16[2048,1024]{1,0:T(8,128)(2,1)} %refs_0_.5, bf16[512,1024]{1,0:T(8,128)(2,1)S(1)} %get-tuple-element.46.refs_1_.refs_2_, ...), custom_call_target="tpu_custom_call" | custom-call | flops 3221225472 | bytes 14686208 | tf_op jit(solution)/shard_map/layer2/pallas_call | solution.py:51
  38.7 0.0 collective-permute-done.3.refs_4_
  38.7 3.7 %collective-permute-start.11 = (bf16[512,512]{1,0:T(8,128)(2,1)S(1)}, bf16[512,512]{1,0:T(8,128)(2,1)S(1)}, u32[]{:S(2)}, u32[]{:S(2)}) collective-permute-start(bf16[512,512]{1,0:T(8,128)(2,1)S(1)} %get-tuple-element.68), channel_id=1, source_target_pairs={{0,30},{1,31},{2,4},{3,5},{4,2},{5,3},{6,8},{7,9},{8,6},{9,7},{10,... | collective-permute-start | bytes 1572872 | tf_op jit(solution)/shard_map/ppermute | solution.py:28
  42.4 0.0 collective-permute-done.2.refs_3_
  42.4 0.0 collective-permute-start.12
  42.5 3.9 %layer0.1 = (bf16[512,1024]{1,0:T(8,128)(2,1)S(1)}, bf16[512,1024]{1,0:T(8,128)(2,1)S(1)}, bf16[512,512]{1,0:T(8,128)(2,1)S(1)}, bf16[512,512]{1,0:T(8,128)(2,1)S(1)}) custom-call(bf16[2048,1024]{1,0:T(8,128)(2,1)} %refs_0_.5, bf16[512,1024]{1,0:T(8,128)(2,1)S(1)} %get-tuple-element.42.before_ref.refs_1_, ...), custom_call_target="tpu_custom_call" | custom-call | flops 3221225472 | bytes 14161920 | tf_op jit(solution)/shard_map/layer0/pallas_call | solution.py:51
  46.4 0.0 collective-permute-done.13.one_side_ref
  46.4 2.2 %collective-permute-start.9 = (bf16[512,512]{1,0:T(8,128)(2,1)S(1)}, bf16[512,512]{1,0:T(8,128)(2,1)S(1)}, u32[]{:S(2)}, u32[]{:S(2)}) collective-permute-start(bf16[512,512]{1,0:T(8,128)(2,1)S(1)} %get-tuple-element.64), channel_id=1, source_target_pairs={{0,30},{1,31},{2,4},{3,5},{4,2},{5,3},{6,8},{7,9},{8,6},{9,7},{10,... | collective-permute-start | bytes 1572872 | tf_op jit(solution)/shard_map/ppermute | solution.py:28
  48.7 0.0 collective-permute-done.4.refs_3_
  48.7 0.0 copy-start.9
  48.7 0.0 collective-permute-start.10
  48.7 4.5 %layer3.1 = (bf16[512,1024]{1,0:T(8,128)(2,1)S(1)}, bf16[512,1024]{1,0:T(8,128)(2,1)S(1)}, bf16[384,512]{1,0:T(8,128)(2,1)S(1)}, bf16[128,512]{1,0:T(8,128)(2,1)...) custom-call(bf16[2048,1024]{1,0:T(8,128)(2,1)} %refs_0_.5, ...), custom_call_target="tpu_custom_call" | custom-call | flops 3221225472 | bytes 14161920 | tf_op jit(solution)/shard_map/layer3/pallas_call | solution.py:51
  53.2 0.0 copy-start.4
  53.2 0.0 copy-start.6
  53.2 0.0 collective-permute-done.14.other_side_ref
  53.3 3.3 %collective-permute-start.7 = (bf16[384,512]{1,0:T(8,128)(2,1)S(1)}, bf16[384,512]{1,0:T(8,128)(2,1)S(1)}, u32[]{:S(2)}, u32[]{:S(2)}) collective-permute-start(bf16[384,512]{1,0:T(8,128)(2,1)S(1)} %get-tuple-element.61), channel_id=1, source_target_pairs={{0,30},{1,31},{2,4},{3,5},{4,2},{5,3},{6,8},{7,9},{8,6},{9,7},{10,... | collective-permute-start | bytes 1179656 | tf_op jit(solution)/shard_map/ppermute | solution.py:28
  56.5 0.5 collective-permute-done.11.one_side_ref
  57.0 0.0 collective-permute-start.8
  57.0 0.0 copy-done.9
  57.0 2.3 %centre.1 = (f32[512,512]{1,0:T(8,128)S(1)}, f32[512,512]{1,0:T(8,128)S(1)}, f32[512,512]{1,0:T(8,128)S(1)}, f32[512,512]{1,0:T(8,128)S(1)}) custom-call(bf16[512,1024]{1,0:T(8,128)(2,1)S(1)} %get-tuple-element.45.far_ref.refs_0_, bf16[512,1024]{1,0:T(8,128)(2,1)S(1)} %get-tuple-element.51.refs_1_, bf16[512,1024]{1,0:T(8,128)(2,1)S(1)} %get-tuple-element.54.refs_2_, ...), custom_call_target="tpu_custom_call" | custom-call | flops 2147483648 | bytes 7342080 | tf_op jit(solution)/shard_map/centre/pallas_call | solution.py:51
  59.3 0.0 copy-done.4
  59.3 0.0 copy-done.6
  59.4 1.8 %finish1.1.rest_0_ = bf16[2048,1024]{1,0:T(8,128)(2,1)} custom-call(f32[512,512]{1,0:T(8,128)S(1)} %get-tuple-element.71.centre_ref, bf16[512,512]{1,0:T(8,128)(2,1)S(1)} %collective-permute-done.13.one_side_ref, bf16[512,512]{1,0:T(8,128)(2,1)S(1)} %collective-permute-done.14.other_side_ref, bf16[512,1024]{1,0:T(8,128)(2,1)S(1)} %get-tuple-element.74.one_ref, ...), custom_call_target="tpu_custom_call" | custom-call | flops 536870912 | bytes 4198400 | tf_op jit(solution)/shard_map/finish1/pallas_call | solution.py:51
  61.2 0.0 collective-permute-done.12.other_side_ref
  61.2 3.7 %collective-permute-start.5 = (bf16[128,512]{1,0:T(8,128)(2,1)S(1)}, bf16[128,512]{1,0:T(8,128)(2,1)S(1)}, u32[]{:S(2)}, u32[]{:S(2)}) collective-permute-start(bf16[128,512]{1,0:T(8,128)(2,1)S(1)} %get-tuple-element.58), channel_id=1, source_target_pairs={{0,30},{1,31},{2,4},{3,5},{4,2},{5,3},{6,8},{7,9},{8,6},{9,7},{10,... | collective-permute-start | bytes 393224 | tf_op jit(solution)/shard_map/ppermute | solution.py:28
  64.9 3.3 %collective-permute-done.9.one_side_ref = bf16[512,512]{1,0:T(8,128)(2,1)S(1)} collective-permute-done((bf16[512,512]{1,0:T(8,128)(2,1)S(1)}, bf16[512,512]{1,0:T(8,128)(2,1)S(1)}, u32[]{:S(2)}, u32[]{:S(2)}) %collective-permute-start.9) | collective-permute-done | bytes 524320 | tf_op jit(solution)/shard_map/ppermute | solution.py:28
  68.2 0.0 collective-permute-start.6
  68.2 1.8 %finish2.1.rest_0_ = bf16[2048,1024]{1,0:T(8,128)(2,1)} custom-call(f32[512,512]{1,0:T(8,128)S(1)} %get-tuple-element.67.centre_ref, bf16[512,512]{1,0:T(8,128)(2,1)S(1)} %collective-permute-done.11.one_side_ref, bf16[512,512]{1,0:T(8,128)(2,1)S(1)} %collective-permute-done.12.other_side_ref, ...), custom_call_target="tpu_custom_call", output_to_operand_aliasing={{}: (6, {})} | custom-call | flops 536870912 | bytes 8392704 | tf_op jit(solution)/shard_map/finish2/pallas_call | solution.py:51
  70.0 0.0 collective-permute-done.10.other_side_ref
  70.1 1.8 %finish0.1.rest_0_ = bf16[2048,1024]{1,0:T(8,128)(2,1)} custom-call(f32[512,512]{1,0:T(8,128)S(1)} %get-tuple-element.63.centre_ref, bf16[512,512]{1,0:T(8,128)(2,1)S(1)} %collective-permute-done.9.one_side_ref, bf16[512,512]{1,0:T(8,128)(2,1)S(1)} %collective-permute-done.10.other_side_ref, ...), custom_call_target="tpu_custom_call", output_to_operand_aliasing={{}: (6, {})} | custom-call | flops 536870912 | bytes 8392704 | tf_op jit(solution)/shard_map/finish0/pallas_call | solution.py:51
  71.9 2.9 %collective-permute-done.7.one_side_ref = bf16[384,512]{1,0:T(8,128)(2,1)S(1)} collective-permute-done((bf16[384,512]{1,0:T(8,128)(2,1)S(1)}, bf16[384,512]{1,0:T(8,128)(2,1)S(1)}, u32[]{:S(2)}, u32[]{:S(2)}) %collective-permute-start.7) | collective-permute-done | bytes 393248 | tf_op jit(solution)/shard_map/ppermute | solution.py:28
  74.8 0.0 collective-permute-done.8.other_side_ref
  74.8 1.6 %finish3.2.rest_0_ = bf16[2048,1024]{1,0:T(8,128)(2,1)} custom-call(f32[512,512]{1,0:T(8,128)S(1)} %get-tuple-element.57.centre_ref, bf16[384,512]{1,0:T(8,128)(2,1)S(1)} %collective-permute-done.7.one_side_ref, bf16[384,512]{1,0:T(8,128)(2,1)S(1)} %collective-permute-done.8.other_side_ref, ...), custom_call_target="tpu_custom_call", output_to_operand_aliasing={{}: (6, {})} | custom-call | flops 402653184 | bytes 8130560 | tf_op jit(solution)/shard_map/finish3/pallas_call | solution.py:51
  76.4 0.0 collective-permute-done.5.one_side_ref
  76.5 0.0 collective-permute-done.6.other_side_ref
  76.5 1.1 %finish3.3 = bf16[2048,1024]{1,0:T(8,128)(2,1)} custom-call(f32[512,512]{1,0:T(8,128)S(1)} %get-tuple-element.57.centre_ref, bf16[128,512]{1,0:T(8,128)(2,1)S(1)} %collective-permute-done.5.one_side_ref, bf16[128,512]{1,0:T(8,128)(2,1)S(1)} %collective-permute-done.6.other_side_ref, ...), custom_call_target="tpu_custom_call", output_to_operand_aliasing={{}: (6, {})} | custom-call | flops 134217728 | bytes 7606272 | tf_op jit(solution)/shard_map/finish3/pallas_call | solution.py:51
Async XLA Ops:
  0.0 19.1 %copy-start.1 = (bf16[3,1024,512]{2,1,0:T(8,128)(2,1)S(1)}, bf16[3,1024,512]{2,1,0:T(8,128)(2,1)}, u32[]{:S(2)}) copy-start(bf16[3,1024,512]{2,1,0:T(8,128)(2,1)} %refs_4_.4) | copy-start | bytes 9437188
  0.0 19.1 %copy-start = (bf16[2048,1024]{1,0:T(8,128)(2,1)S(1)}, bf16[2048,1024]{1,0:T(8,128)(2,1)}, u32[]{:S(2)}) copy-start(bf16[2048,1024]{1,0:T(8,128)(2,1)} %refs_0_.5) | copy-start | bytes 12582916
  0.0 19.1 %copy-start.7 = (f32[1024]{0:T(1024)S(1)}, f32[1024]{0:T(1024)}, u32[]{:S(2)}) copy-start(f32[1024]{0:T(1024)} %param.13) | copy-start | bytes 12292
  0.0 19.1 %copy-start.8 = (f32[512]{0:T(512)S(1)}, f32[512]{0:T(512)}, u32[]{:S(2)}) copy-start(f32[512]{0:T(512)} %param.11) | copy-start | bytes 6148
  2.4 13.3 %collective-permute-start = (bf16[128,512]{1,0:T(8,128)(2,1)S(1)}, bf16[128,512]{1,0:T(8,128)(2,1)S(1)}, u32[]{:S(2)}, u32[]{:S(2)}) collective-permute-start(bf16[128,512]{1,0:T(8,128)(2,1)S(1)} %get-tuple-element.40), channel_id=1, source_target_pairs={{0,1},{1,0},{2,3},{3,2},{4,5},{5,4},{6,7},{7,6},{8,9},{9,8},{10,11... | collective-permute-start | bytes 393224 | tf_op jit(solution)/shard_map/ppermute | solution.py:28
  4.5 37.9 %collective-permute-start.2 = (bf16[384,512]{1,0:T(8,128)(2,1)S(1)}, bf16[384,512]{1,0:T(8,128)(2,1)S(1)}, u32[]{:S(2)}, u32[]{:S(2)}) collective-permute-start(bf16[384,512]{1,0:T(8,128)(2,1)S(1)} %get-tuple-element.52), channel_id=1, source_target_pairs={{0,31},{1,2},{2,1},{3,4},{4,3},{5,6},{6,5},{7,8},{8,7},{9,10},{10,... | collective-permute-start | bytes 1179656 | tf_op jit(solution)/shard_map/ppermute | solution.py:28
  15.7 13.5 %collective-permute-start.1 = (bf16[128,512]{1,0:T(8,128)(2,1)S(1)}, bf16[128,512]{1,0:T(8,128)(2,1)S(1)}, u32[]{:S(2)}, u32[]{:S(2)}) collective-permute-start(bf16[128,512]{1,0:T(8,128)(2,1)S(1)} %collective-permute-done), channel_id=1, source_target_pairs={{0,3},{1,30},{2,5},{3,0},{4,7},{5,2},{6,9},{7,4},{8,11},{9,6},{10,... | collective-permute-start | bytes 393224 | tf_op jit(solution)/shard_map/ppermute | solution.py:28
  19.1 9.3 %copy-start.3 = (bf16[3,1024,512]{2,1,0:T(8,128)(2,1)S(1)}, bf16[3,1024,512]{2,1,0:T(8,128)(2,1)}, u32[]{:S(2)}) copy-start(bf16[3,1024,512]{2,1,0:T(8,128)(2,1)} %refs_4_.5) | copy-start | bytes 9437188
  24.5 21.9 %collective-permute-start.13 = (bf16[512,512]{1,0:T(8,128)(2,1)S(1)}, bf16[512,512]{1,0:T(8,128)(2,1)S(1)}, u32[]{:S(2)}, u32[]{:S(2)}) collective-permute-start(bf16[512,512]{1,0:T(8,128)(2,1)S(1)} %get-tuple-element.72), channel_id=1, source_target_pairs={{0,30},{1,31},{2,4},{3,5},{4,2},{5,3},{6,8},{7,9},{8,6},{9,7},{10,... | collective-permute-start | bytes 1572872 | tf_op jit(solution)/shard_map/ppermute | solution.py:28
  29.1 4.6 %copy-start.2 = (bf16[3,1024,512]{2,1,0:T(8,128)(2,1)S(1)}, bf16[3,1024,512]{2,1,0:T(8,128)(2,1)}, u32[]{:S(2)}) copy-start(bf16[3,1024,512]{2,1,0:T(8,128)(2,1)} %refs_4_.4) | copy-start | bytes 9437188
  29.1 4.6 %copy-start.5 = (bf16[512,1024]{1,0:T(8,128)(2,1)S(1)}, bf16[512,1024]{1,0:T(8,128)(2,1)}, u32[]{:S(2)}) copy-start(bf16[512,1024]{1,0:T(8,128)(2,1)} %refs_6_.3) | copy-start | bytes 3145732
  29.2 9.6 %collective-permute-start.3 = (bf16[128,512]{1,0:T(8,128)(2,1)S(1)}, bf16[128,512]{1,0:T(8,128)(2,1)S(1)}, u32[]{:S(2)}, u32[]{:S(2)}) collective-permute-start(bf16[128,512]{1,0:T(8,128)(2,1)S(1)} %collective-permute-done.1), channel_id=1, source_target_pairs={{0,1},{1,0},{2,3},{3,2},{4,5},{5,4},{6,7},{7,6},{8,9},{9,8},{10,11... | collective-permute-start | bytes 393224 | tf_op jit(solution)/shard_map/ppermute | solution.py:28
  30.2 23.0 %collective-permute-start.14 = (bf16[512,512]{1,0:T(8,128)(2,1)S(1)}, bf16[512,512]{1,0:T(8,128)(2,1)S(1)}, u32[]{:S(2)}, u32[]{:S(2)}) collective-permute-start(bf16[512,512]{1,0:T(8,128)(2,1)S(1)} %first1.1), channel_id=1, source_target_pairs={{0,2},{1,3},{2,0},{3,1},{4,6},{5,7},{6,4},{7,5},{8,10},{9,11},{10,... | collective-permute-start | bytes 1572872 | tf_op jit(solution)/shard_map/ppermute | solution.py:28
  32.7 16.0 %collective-permute-start.4 = (bf16[512,512]{1,0:T(8,128)(2,1)S(1)}, bf16[512,512]{1,0:T(8,128)(2,1)S(1)}, u32[]{:S(2)}, u32[]{:S(2)}) collective-permute-start(bf16[512,512]{1,0:T(8,128)(2,1)S(1)} %get-tuple-element.55), channel_id=1, source_target_pairs={{0,1},{1,0},{2,3},{3,2},{4,5},{5,4},{6,7},{7,6},{8,9},{9,8},{10,11... | collective-permute-start | bytes 1572872 | tf_op jit(solution)/shard_map/ppermute | solution.py:28
  38.7 18.3 %collective-permute-start.11 = (bf16[512,512]{1,0:T(8,128)(2,1)S(1)}, bf16[512,512]{1,0:T(8,128)(2,1)S(1)}, u32[]{:S(2)}, u32[]{:S(2)}) collective-permute-start(bf16[512,512]{1,0:T(8,128)(2,1)S(1)} %get-tuple-element.68), channel_id=1, source_target_pairs={{0,30},{1,31},{2,4},{3,5},{4,2},{5,3},{6,8},{7,9},{8,6},{9,7},{10,... | collective-permute-start | bytes 1572872 | tf_op jit(solution)/shard_map/ppermute | solution.py:28
  42.4 18.7 %collective-permute-start.12 = (bf16[512,512]{1,0:T(8,128)(2,1)S(1)}, bf16[512,512]{1,0:T(8,128)(2,1)S(1)}, u32[]{:S(2)}, u32[]{:S(2)}) collective-permute-start(bf16[512,512]{1,0:T(8,128)(2,1)S(1)} %get-tuple-element.69), channel_id=1, source_target_pairs={{0,2},{1,3},{2,0},{3,1},{4,6},{5,7},{6,4},{7,5},{8,10},{9,11},{10,... | collective-permute-start | bytes 1572872 | tf_op jit(solution)/shard_map/ppermute | solution.py:28
  46.4 21.8 %collective-permute-start.9 = (bf16[512,512]{1,0:T(8,128)(2,1)S(1)}, bf16[512,512]{1,0:T(8,128)(2,1)S(1)}, u32[]{:S(2)}, u32[]{:S(2)}) collective-permute-start(bf16[512,512]{1,0:T(8,128)(2,1)S(1)} %get-tuple-element.64), channel_id=1, source_target_pairs={{0,30},{1,31},{2,4},{3,5},{4,2},{5,3},{6,8},{7,9},{8,6},{9,7},{10,... | collective-permute-start | bytes 1572872 | tf_op jit(solution)/shard_map/ppermute | solution.py:28
  48.7 8.3 %copy-start.9 = (f32[512]{0:T(512)S(1)}, f32[512]{0:T(512)}, u32[]{:S(2)}) copy-start(f32[512]{0:T(512)} %param.15) | copy-start | bytes 6148
  48.7 21.4 %collective-permute-start.10 = (bf16[512,512]{1,0:T(8,128)(2,1)S(1)}, bf16[512,512]{1,0:T(8,128)(2,1)S(1)}, u32[]{:S(2)}, u32[]{:S(2)}) collective-permute-start(bf16[512,512]{1,0:T(8,128)(2,1)S(1)} %get-tuple-element.65), channel_id=1, source_target_pairs={{0,2},{1,3},{2,0},{3,1},{4,6},{5,7},{6,4},{7,5},{8,10},{9,11},{10,... | collective-permute-start | bytes 1572872 | tf_op jit(solution)/shard_map/ppermute | solution.py:28
  53.2 6.1 %copy-start.4 = (bf16[512,1024]{1,0:T(8,128)(2,1)S(1)}, bf16[512,1024]{1,0:T(8,128)(2,1)}, u32[]{:S(2)}) copy-start(bf16[512,1024]{1,0:T(8,128)(2,1)} %point_ref.9) | copy-start | bytes 3145732
  53.2 6.1 %copy-start.6 = (f32[1024]{0:T(1024)S(1)}, f32[1024]{0:T(1024)}, u32[]{:S(2)}) copy-start(f32[1024]{0:T(1024)} %param.17) | copy-start | bytes 12292
  53.3 21.5 %collective-permute-start.7 = (bf16[384,512]{1,0:T(8,128)(2,1)S(1)}, bf16[384,512]{1,0:T(8,128)(2,1)S(1)}, u32[]{:S(2)}, u32[]{:S(2)}) collective-permute-start(bf16[384,512]{1,0:T(8,128)(2,1)S(1)} %get-tuple-element.61), channel_id=1, source_target_pairs={{0,30},{1,31},{2,4},{3,5},{4,2},{5,3},{6,8},{7,9},{8,6},{9,7},{10,... | collective-permute-start | bytes 1179656 | tf_op jit(solution)/shard_map/ppermute | solution.py:28
  57.0 17.8 %collective-permute-start.8 = (bf16[384,512]{1,0:T(8,128)(2,1)S(1)}, bf16[384,512]{1,0:T(8,128)(2,1)S(1)}, u32[]{:S(2)}, u32[]{:S(2)}) collective-permute-start(bf16[384,512]{1,0:T(8,128)(2,1)S(1)} %get-tuple-element.62), channel_id=1, source_target_pairs={{0,2},{1,3},{2,0},{3,1},{4,6},{5,7},{6,4},{7,5},{8,10},{9,11},{10,... | collective-permute-start | bytes 1179656 | tf_op jit(solution)/shard_map/ppermute | solution.py:28
  61.2 15.3 %collective-permute-start.5 = (bf16[128,512]{1,0:T(8,128)(2,1)S(1)}, bf16[128,512]{1,0:T(8,128)(2,1)S(1)}, u32[]{:S(2)}, u32[]{:S(2)}) collective-permute-start(bf16[128,512]{1,0:T(8,128)(2,1)S(1)} %get-tuple-element.58), channel_id=1, source_target_pairs={{0,30},{1,31},{2,4},{3,5},{4,2},{5,3},{6,8},{7,9},{8,6},{9,7},{10,... | collective-permute-start | bytes 393224 | tf_op jit(solution)/shard_map/ppermute | solution.py:28
  68.2 8.2 %collective-permute-start.6 = (bf16[128,512]{1,0:T(8,128)(2,1)S(1)}, bf16[128,512]{1,0:T(8,128)(2,1)S(1)}, u32[]{:S(2)}, u32[]{:S(2)}) collective-permute-start(bf16[128,512]{1,0:T(8,128)(2,1)S(1)} %get-tuple-element.59), channel_id=1, source_target_pairs={{0,2},{1,3},{2,0},{3,1},{4,6},{5,7},{6,4},{7,5},{8,10},{9,11},{10,... | collective-permute-start | bytes 393224 | tf_op jit(solution)/shard_map/ppermute | solution.py:28

commit v7 on v6

--- a/solution.py
+++ b/solution.py
@@ -13,7 +13,7 @@
 HBM = pl.BlockSpec(memory_space=pltpu.HBM)
 SLOPE = math.sqrt(2.0 / math.pi)
 LAST_PIECE = 128
-RELAY = 128
+LATE = 128
 BF16 = jnp.bfloat16
 F32 = jnp.float32
 
@@ -65,76 +65,58 @@
     return jax.ShapeDtypeStruct((rows, columns), dtype)
 
 
-def rim_activations(x_ref, taps_ref, tap, quarter, act_ref, x_own, tap_own, sems, put):
-    size = x_own.shape[0]
+def rim_activations(x_ref, taps_ref, tap, quarter, size, act_ref, product_ref, x_own, tap_own, sems):
+    rows = x_own.shape[0]
     half = size // 2
-    top, bottom = pl.ds(0, half), pl.ds(half, half)
+    top, bottom = pl.ds(0, half), pl.ds(half, rows - half)
     which = tap + odd_position() * (2 - 2 * tap)
     start = quarter_rows(quarter, size).start
-    copies = []
-    for k in range(2):
-        rows = pl.ds(pl.multiple_of(start + k * half, half), half)
-        copies.append(pltpu.make_async_copy(x_ref.at[rows], x_own.at[pl.ds(k * half, half)], sems.at[k]))
-    copies.insert(1, pltpu.make_async_copy(taps_ref.at[which], tap_own, sems.at[2]))
+    copies = [
+        pltpu.make_async_copy(x_ref.at[pl.ds(pl.multiple_of(start, half), half)], x_own.at[top], sems.at[0]),
+        pltpu.make_async_copy(taps_ref.at[which], tap_own, sems.at[1]),
+        pltpu.make_async_copy(
+            x_ref.at[pl.ds(pl.multiple_of(start + half, half), rows - half)], x_own.at[bottom], sems.at[2]
+        ),
+    ]
     for copy in copies:
         copy.start()
     copies[0].wait()
     act_ref[top, :] = gelu(x_own[top, :].astype(F32)).astype(BF16)
     copies[1].wait()
     copies[2].wait()
-    put(0, dot(act_ref[top, :], tap_own[...]).astype(BF16))
+    product_ref[top, :] = dot(act_ref[top, :], tap_own[...]).astype(BF16)
     act_ref[bottom, :] = gelu(x_own[bottom, :].astype(F32)).astype(BF16)
-    put(1, dot(act_ref[bottom, :], tap_own[...]).astype(BF16))
-
-
-def rim_scratch(size, c, m):
-    return [pltpu.VMEM((size, c), BF16), pltpu.VMEM((c, m), BF16), pltpu.SemaphoreType.DMA((3,))]
-
-
-def pair_rim(x, taps):
+    product_ref[bottom, :] = dot(act_ref[bottom, :], tap_own[...]).astype(BF16)
+
+
+def rim(x, taps, quarter, rows):
     size, (c, m) = x.shape[0] // 4, taps.shape[1:]
-    half = size // 2
-
-    def body(x_ref, taps_ref, act_ref, direct_ref, relay_ref, *scratch):
-        def put(k, product):
-            if k == 0:
-                direct_ref[:half, :] = product
-            else:
-                direct_ref[half:, :] = product[: half - RELAY, :]
-                relay_ref[...] = product[half - RELAY :, :]
-
-        rim_activations(x_ref, taps_ref, 2, 0, act_ref, *scratch, put)
+
+    def body(x_ref, taps_ref, act_ref, product_ref, *scratch):
+        tap = 2 if quarter == 0 else 0
+        rim_activations(x_ref, taps_ref, tap, quarter, size, act_ref, product_ref, *scratch)
 
     return call(
-        body, "rim0", [shape(size, c), shape(size - RELAY, m), shape(RELAY, m)], (x, taps), 2 * size * c * m,
-        rim_scratch(size, c, m), specs=[HBM] * 2,
-    )
-
-
-def partner_rim(x, taps):
-    size, (c, m) = x.shape[0] // 4, taps.shape[1:]
-    half = size // 2
-
-    def body(x_ref, taps_ref, act_ref, product_ref, *scratch):
-        def put(k, product):
-            product_ref[k * half : (k + 1) * half, :] = product
-
-        rim_activations(x_ref, taps_ref, 0, 3, act_ref, *scratch, put)
-
-    return call(
-        body, "rim3", [shape(size, c), shape(size, m)], (x, taps), 2 * size * c * m, rim_scratch(size, c, m),
-        specs=[HBM] * 2,
-    )
-
-
-def first_product(far, outer):
+        body, f"rim{quarter}", [shape(rows, c), shape(rows, m)], (x, taps), 2 * rows * c * m,
+        [pltpu.VMEM((rows, c), BF16), pltpu.VMEM((c, m), BF16), pltpu.SemaphoreType.DMA((3,))], specs=[HBM] * 2,
+    )
+
+
+def behind_first(far, outer, act_top, act_bottom, taps):
     size, c = far.shape
     m = outer.shape[2]
-
-    def body(far_ref, outer_ref, first_ref):
+    late = act_bottom.shape[0]
+
+    def body(far_ref, outer_ref, top_ref, bottom_ref, taps_ref, first_ref, late_ref, act_ref):
         first_ref[...] = dot(far_ref[...], outer_ref[2 * odd_pair()]).astype(BF16)
-
-    return call(body, "first1", [shape(size, m)], (far, outer), 2 * size * c * m, [], specs=[VMEM] * 2)[0]
+        late_ref[...] = dot(bottom_ref[...], taps_ref[2 - 2 * odd_position()]).astype(BF16)
+        act_ref[: size - late, :] = top_ref[...]
+        act_ref[size - late :, :] = bottom_ref[...]
+
+    return call(
+        body, "behind1", [shape(size, m), shape(late, m), shape(size, c)], (far, outer, act_top, act_bottom, taps),
+        2 * size * c * m, [], specs=[VMEM] * 5,
+    )
 
 
 def odd_pair():
@@ -147,7 +129,7 @@
 
     def body(
         x_ref, before_ref, taps_ref, bias_conv_ref, point_hbm, bias_point_ref, outer_hbm,
-        act1_ref, act2_ref, one_ref, far_ref, second_ref, point_own, outer_own, sems,
+        bottom_ref, act1_ref, act2_ref, one_ref, far_ref, second_ref, point_own, outer_own, sems,
     ):
         copies = [
             pltpu.make_async_copy(point_hbm, point_own, sems.at[0]),
@@ -156,7 +138,9 @@
         for copy in copies:
             copy.start()
         odd = odd_position()
-        total = dot(before_ref[...], taps_ref[2 * odd])
+        at = quarter_rows(0, size).start + size - LATE
+        bottom_ref[...] = gelu(x_ref[pl.ds(pl.multiple_of(at, LATE), LATE), :].astype(F32)).astype(BF16)
+        total = jnp.concatenate([dot(before_ref[...], taps_ref[2 * odd]), dot(bottom_ref[...], taps_ref[2 * odd])], axis=0)
         act1_ref[...] = gelu(x_ref[quarter_rows(1, size), :].astype(F32)).astype(BF16)
         total = total + dot(act1_ref[...], taps_ref[1])
         act2_ref[...] = gelu(x_ref[quarter_rows(2, size), :].astype(F32)).astype(BF16)
@@ -174,7 +158,7 @@
     point, outer = (pltpu.with_memory_space_constraint(w, pltpu.HBM) for w in (point, outer))
     args = (x, act, taps, bias_conv, point, bias_point, outer)
     return call(
-        body, "layer1", [shape(size, c)] * 4 + [shape(size, m)], args, 10 * size * c * m,
+        body, "layer1", [shape(LATE, c)] + [shape(size, c)] * 4 + [shape(size, m)], args, 10 * size * c * m,
         [pltpu.VMEM((m, c), BF16), pltpu.VMEM((c, m), BF16), pltpu.SemaphoreType.DMA((2,))],
         specs=[VMEM] * 4 + [HBM, VMEM, HBM],
     )
@@ -317,24 +301,21 @@
     def send(products):
         return [(second_matching(second), first_matching(first)) for first, second in products]
 
-    act0, direct, relay = pair_rim(x, rim_taps)
-    handed = to_partner(relay)
+    act_top, direct = rim(x, rim_taps, 0, size - LATE)
     from_pair = swap(direct, lambda i: i % 2 == 1, 1)
-    near_input, handed = lax.optimization_barrier((tower_input, handed))
-    relayed = swap(handed, lambda i: i % 2 == 0, 3)
-
-    act1, act2, one1, far1, second1 = first_quarter(near_input, act0, near)
+    act_bottom, act1, act2, one1, far1, second1 = first_quarter(tower_input, act_top, near)
     far1, second1 = lax.optimization_barrier((far1, second1))
     side1 = second_matching(second1)
-    later, relayed, first1 = lax.optimization_barrier((x, relayed, first_product(far1, second_conv_taps)))
-    returned = to_partner(relayed)
+    first1, late, act0 = behind_first(far1, second_conv_taps, act_top, act_bottom, first_conv_taps)
+    later, first1, late = lax.optimization_barrier((x, first1, late))
+    from_pair_late = swap(late, lambda i: i % 2 == 1, 1)
     sides1 = [(side1, first_matching(first1))]
-    act3, for_partner = partner_rim(later, rim_taps)
+    act3, for_partner = rim(later, rim_taps, 3, size)
     from_partner = to_partner(for_partner)
     one2, far2, products2 = layer(x, 2, (act1, act2, act3), [], near, whole)
     sides2 = send(products2)
     one0, far0, products0 = layer(
-        x, 0, (None, act0, act1), [(from_pair, 0), (returned, 0)], near, whole
+        x, 0, (None, act0, act1), [(from_pair, 0), (from_pair_late, 0)], near, whole
     )
     sides0 = send(products0)
     one3, far3, products3 = layer(x, 3, (act2, act3, None), [(from_partner, 0)], near, split)

time: 78 us -> 73.4 us (0.941)
  starting transfers between devices: 29.3 us -> 19.4 us
  waiting for transfers between devices: 13.2 us -> 18.3 us
    ppermute x15 -> x13, starting transfers between devices: 29.3 us -> 19.4 us  [swap(): return lax.ppermute(value, 'seq', sorted(pairs))]
    ppermute x15 -> x13, waiting for transfers between devices: 13.2 us -> 18.3 us  [swap(): return lax.ppermute(value, 'seq', sorted(pairs))]
  transfers between devices with their start and end apart: 15 -> 13, of which waited for: 4 -> 4; matrix products, arithmetic and copies ran while one was open for 0% -> 0% of each run, Pallas kernels for 40% -> 43%
where the time goes in v7:
time: 73.4 us; the launch traced here: 72.5 us
  Pallas kernels  34.3 us (47%)
  starting transfers between devices  19.4 us (26%)
  waiting for transfers between devices  18.3 us (25%)
    pallas_call x13, Pallas kernels, call(): pl.pallas_call(body, in_specs=specs, out_specs=[VMEM] * len(out_shape) if...  34.3 us
    ppermute x13, starting transfers between devices, swap(): return lax.ppermute(value, 'seq', sorted(pairs))  19.4 us
    ppermute x13, waiting for transfers between devices, swap(): return lax.ppermute(value, 'seq', sorted(pairs))  18.3 us
  transfers between devices with their start and end apart: 13, of which 4 were waited for; matrix products, arithmetic and copies ran while one was open for 0% of the time, Pallas kernels for 43%

profile of v7, /device:TPU:0, one launch (start us, length us, event | category | flops | bytes accessed | tf_op | source)
XLA Modules:
  0.0 72.5 jit_solution(14062187158934701415)
XLA Ops:
  0.0 0.0 copy-start
  0.0 0.0 copy-start.2
  0.0 0.0 copy-start.7
  0.0 0.0 copy-start.8
  0.0 2.2 %rim0.1 = (bf16[384,1024]{1,0:T(8,128)(2,1)S(1)}, bf16[384,512]{1,0:T(8,128)(2,1)S(1)}) custom-call(bf16[2048,1024]{1,0:T(8,128)(2,1)} %refs_0_.5, bf16[3,1024,512]{2,1,0:T(8,128)(2,1)} %refs_4_.4), custom_call_target="tpu_custom_call" | custom-call | flops 402653184 | bytes 7340032 | tf_op jit(solution)/shard_map/rim0/pallas_call | solution.py:51
  2.2 6.7 %collective-permute-start = (bf16[384,512]{1,0:T(8,128)(2,1)S(1)}, bf16[384,512]{1,0:T(8,128)(2,1)S(1)}, u32[]{:S(2)}, u32[]{:S(2)}) collective-permute-start(bf16[384,512]{1,0:T(8,128)(2,1)S(1)} %get-tuple-element.54), channel_id=1, source_target_pairs={{0,31},{1,2},{2,1},{3,4},{4,3},{5,6},{6,5},{7,8},{8,7},{9,10},{10,... | collective-permute-start | bytes 1179656 | tf_op jit(solution)/shard_map/ppermute | solution.py:28
  8.9 0.0 copy-done
  8.9 0.0 copy-done.2
  8.9 0.0 copy-done.7
  8.9 0.0 copy-done.8
  9.0 0.0 copy-start.3
  9.0 5.1 %layer1.1 = (bf16[128,1024]{1,0:T(8,128)(2,1)S(1)}, bf16[512,1024]{1,0:T(8,128)(2,1)S(1)}, bf16[512,1024]{1,0:T(8,128)(2,1)S(1)}, bf16[512,1024]{1,0:T(8,128)(2,...) custom-call(bf16[2048,1024]{1,0:T(8,128)(2,1)S(1)} %copy-done.2, ...), custom_call_target="tpu_custom_call" | custom-call | flops 2684354560 | bytes 12326912 | tf_op jit(solution)/shard_map/layer1/pallas_call | solution.py:51
  14.1 0.9 %collective-permute-start.11 = (bf16[512,512]{1,0:T(8,128)(2,1)S(1)}, bf16[512,512]{1,0:T(8,128)(2,1)S(1)}, u32[]{:S(2)}, u32[]{:S(2)}) collective-permute-start(bf16[512,512]{1,0:T(8,128)(2,1)S(1)} %get-tuple-element.74), channel_id=1, source_target_pairs={{0,30},{1,31},{2,4},{3,5},{4,2},{5,3},{6,8},{7,9},{8,6},{9,7},{10,... | collective-permute-start | bytes 1572872 | tf_op jit(solution)/shard_map/ppermute | solution.py:28
  15.0 0.0 copy-done.3
  15.0 0.8 %behind1.1 = (bf16[512,512]{1,0:T(8,128)(2,1)S(1)}, bf16[128,512]{1,0:T(8,128)(2,1)S(1)}, bf16[512,1024]{1,0:T(8,128)(2,1)S(1)}) custom-call(bf16[512,1024]{1,0:T(8,128)(2,1)S(1)} %get-tuple-element.44.far_ref.refs_0_, bf16[3,1024,512]{2,1,0:T(8,128)(2,1)S(1)} %copy-done.3, bf16[384,1024]{1,0:T(8,128)(2,1)S(1)} %get-tuple-element.41.before_ref.top_ref, ...), custom_call_target="tpu_custom_call" | custom-call | flops 536870912 | bytes 8388608 | tf_op jit(solution)/shard_map/behind1/pallas_call | solution.py:51
  15.8 0.0 copy-start.1
  15.8 0.0 copy-start.5
  15.8 0.8 %collective-permute-start.1 = (bf16[128,512]{1,0:T(8,128)(2,1)S(1)}, bf16[128,512]{1,0:T(8,128)(2,1)S(1)}, u32[]{:S(2)}, u32[]{:S(2)}) collective-permute-start(bf16[128,512]{1,0:T(8,128)(2,1)S(1)} %get-tuple-element.55), channel_id=1, source_target_pairs={{0,31},{1,2},{2,1},{3,4},{4,3},{5,6},{6,5},{7,8},{8,7},{9,10},{10,... | collective-permute-start | bytes 393224 | tf_op jit(solution)/shard_map/ppermute | solution.py:28
  16.6 1.9 %collective-permute-start.12 = (bf16[512,512]{1,0:T(8,128)(2,1)S(1)}, bf16[512,512]{1,0:T(8,128)(2,1)S(1)}, u32[]{:S(2)}, u32[]{:S(2)}) collective-permute-start(bf16[512,512]{1,0:T(8,128)(2,1)S(1)} %get-tuple-element.75), channel_id=1, source_target_pairs={{0,2},{1,3},{2,0},{3,1},{4,6},{5,7},{6,4},{7,5},{8,10},{9,11},{10,... | collective-permute-start | bytes 1572872 | tf_op jit(solution)/shard_map/ppermute | solution.py:28
  18.5 2.3 %rim3.1 = (bf16[512,1024]{1,0:T(8,128)(2,1)S(1)}, bf16[512,512]{1,0:T(8,128)(2,1)S(1)}) custom-call(bf16[2048,1024]{1,0:T(8,128)(2,1)} %refs_0_.5, bf16[3,1024,512]{2,1,0:T(8,128)(2,1)} %refs_4_.4), custom_call_target="tpu_custom_call" | custom-call | flops 536870912 | bytes 7340032 | tf_op jit(solution)/shard_map/rim3/pallas_call | solution.py:51
  20.8 0.1 collective-permute-start.2
  20.9 0.0 copy-done.1
  20.9 0.0 copy-done.5
  20.9 5.0 %layer2.1 = (bf16[512,1024]{1,0:T(8,128)(2,1)S(1)}, bf16[512,1024]{1,0:T(8,128)(2,1)S(1)}, bf16[512,512]{1,0:T(8,128)(2,1)S(1)}, bf16[512,512]{1,0:T(8,128)(2,1)S(1)}) custom-call(bf16[2048,1024]{1,0:T(8,128)(2,1)} %refs_0_.5, bf16[512,1024]{1,0:T(8,128)(2,1)S(1)} %get-tuple-element.45.refs_1_.refs_2_, ...), custom_call_target="tpu_custom_call" | custom-call | flops 3221225472 | bytes 14686208 | tf_op jit(solution)/shard_map/layer2/pallas_call | solution.py:51
  25.9 6.3 %collective-permute-done.1.refs_4_ = bf16[128,512]{1,0:T(8,128)(2,1)S(1)} collective-permute-done((bf16[128,512]{1,0:T(8,128)(2,1)S(1)}, bf16[128,512]{1,0:T(8,128)(2,1)S(1)}, u32[]{:S(2)}, u32[]{:S(2)}) %collective-permute-start.1) | collective-permute-done | bytes 131104 | tf_op jit(solution)/shard_map/ppermute | solution.py:28
  32.2 0.0 collective-permute-start.9
  32.2 0.0 collective-permute-done.refs_3_
  32.2 0.0 collective-permute-start.10
  32.2 4.0 %layer0.1 = (bf16[512,1024]{1,0:T(8,128)(2,1)S(1)}, bf16[512,1024]{1,0:T(8,128)(2,1)S(1)}, bf16[512,512]{1,0:T(8,128)(2,1)S(1)}, bf16[512,512]{1,0:T(8,128)(2,1)S(1)}) custom-call(bf16[2048,1024]{1,0:T(8,128)(2,1)} %refs_0_.5, bf16[512,1024]{1,0:T(8,128)(2,1)S(1)} %get-tuple-element.53.refs_1_, bf16[512,1024]{1,0:T(8,128)(2,1)S(1)} %get-tuple-element.45.refs_1_.refs_2_, ...), custom_call_target="tpu_custom_call" | custom-call | flops 3221225472 | bytes 14161920 | tf_op jit(solution)/shard_map/layer0/pallas_call | solution.py:51
  36.2 0.0 collective-permute-done.11.one_side_ref
  36.2 5.4 %collective-permute-start.7 = (bf16[512,512]{1,0:T(8,128)(2,1)S(1)}, bf16[512,512]{1,0:T(8,128)(2,1)S(1)}, u32[]{:S(2)}, u32[]{:S(2)}) collective-permute-start(bf16[512,512]{1,0:T(8,128)(2,1)S(1)} %get-tuple-element.66), channel_id=1, source_target_pairs={{0,30},{1,31},{2,4},{3,5},{4,2},{5,3},{6,8},{7,9},{8,6},{9,7},{10,... | collective-permute-start | bytes 1572872 | tf_op jit(solution)/shard_map/ppermute | solution.py:28
  41.6 0.0 collective-permute-done.2.refs_3_
  41.6 0.0 copy-start.9
  41.6 0.0 collective-permute-start.8
  41.6 4.6 %layer3.1 = (bf16[512,1024]{1,0:T(8,128)(2,1)S(1)}, bf16[512,1024]{1,0:T(8,128)(2,1)S(1)}, bf16[384,512]{1,0:T(8,128)(2,1)S(1)}, bf16[128,512]{1,0:T(8,128)(2,1)...) custom-call(bf16[2048,1024]{1,0:T(8,128)(2,1)} %refs_0_.5, ...), custom_call_target="tpu_custom_call" | custom-call | flops 3221225472 | bytes 14161920 | tf_op jit(solution)/shard_map/layer3/pallas_call | solution.py:51
  46.2 0.0 copy-start.4
  46.2 0.0 copy-start.6
  46.2 0.0 collective-permute-done.12.other_side_ref
  46.2 2.2 %collective-permute-start.5 = (bf16[384,512]{1,0:T(8,128)(2,1)S(1)}, bf16[384,512]{1,0:T(8,128)(2,1)S(1)}, u32[]{:S(2)}, u32[]{:S(2)}) collective-permute-start(bf16[384,512]{1,0:T(8,128)(2,1)S(1)} %get-tuple-element.63), channel_id=1, source_target_pairs={{0,30},{1,31},{2,4},{3,5},{4,2},{5,3},{6,8},{7,9},{8,6},{9,7},{10,... | collective-permute-start | bytes 1179656 | tf_op jit(solution)/shard_map/ppermute | solution.py:28
  48.4 1.9 %collective-permute-done.9.one_side_ref = bf16[512,512]{1,0:T(8,128)(2,1)S(1)} collective-permute-done((bf16[512,512]{1,0:T(8,128)(2,1)S(1)}, bf16[512,512]{1,0:T(8,128)(2,1)S(1)}, u32[]{:S(2)}, u32[]{:S(2)}) %collective-permute-start.9) | collective-permute-done | bytes 524320 | tf_op jit(solution)/shard_map/ppermute | solution.py:28
  50.4 0.0 collective-permute-start.6
  50.4 0.0 copy-done.9
  50.4 2.3 %centre.1 = (f32[512,512]{1,0:T(8,128)S(1)}, f32[512,512]{1,0:T(8,128)S(1)}, f32[512,512]{1,0:T(8,128)S(1)}, f32[512,512]{1,0:T(8,128)S(1)}) custom-call(bf16[512,1024]{1,0:T(8,128)(2,1)S(1)} %get-tuple-element.44.far_ref.refs_0_, bf16[512,1024]{1,0:T(8,128)(2,1)S(1)} %get-tuple-element.52.refs_1_, bf16[512,1024]{1,0:T(8,128)(2,1)S(1)} %get-tuple-element.56.refs_2_, ...), custom_call_target="tpu_custom_call" | custom-call | flops 2147483648 | bytes 7342080 | tf_op jit(solution)/shard_map/centre/pallas_call | solution.py:51
  52.7 0.0 copy-done.4
  52.7 0.0 copy-done.6
  52.7 1.8 %finish1.1.rest_0_ = bf16[2048,1024]{1,0:T(8,128)(2,1)} custom-call(f32[512,512]{1,0:T(8,128)S(1)} %get-tuple-element.73.centre_ref, bf16[512,512]{1,0:T(8,128)(2,1)S(1)} %collective-permute-done.11.one_side_ref, bf16[512,512]{1,0:T(8,128)(2,1)S(1)} %collective-permute-done.12.other_side_ref, bf16[512,1024]{1,0:T(8,128)(2,1)S(1)} %get-tuple-element.76.one_ref, ...), custom_call_target="tpu_custom_call" | custom-call | flops 536870912 | bytes 4198400 | tf_op jit(solution)/shard_map/finish1/pallas_call | solution.py:51
  54.6 0.0 collective-permute-done.10.other_side_ref
  54.6 1.4 %collective-permute-start.3 = (bf16[128,512]{1,0:T(8,128)(2,1)S(1)}, bf16[128,512]{1,0:T(8,128)(2,1)S(1)}, u32[]{:S(2)}, u32[]{:S(2)}) collective-permute-start(bf16[128,512]{1,0:T(8,128)(2,1)S(1)} %get-tuple-element.60), channel_id=1, source_target_pairs={{0,30},{1,31},{2,4},{3,5},{4,2},{5,3},{6,8},{7,9},{8,6},{9,7},{10,... | collective-permute-start | bytes 393224 | tf_op jit(solution)/shard_map/ppermute | solution.py:28
  55.9 5.7 %collective-permute-done.7.one_side_ref = bf16[512,512]{1,0:T(8,128)(2,1)S(1)} collective-permute-done((bf16[512,512]{1,0:T(8,128)(2,1)S(1)}, bf16[512,512]{1,0:T(8,128)(2,1)S(1)}, u32[]{:S(2)}, u32[]{:S(2)}) %collective-permute-start.7) | collective-permute-done | bytes 524320 | tf_op jit(solution)/shard_map/ppermute | solution.py:28
  61.6 0.0 collective-permute-start.4
  61.6 1.8 %finish2.1.rest_0_ = bf16[2048,1024]{1,0:T(8,128)(2,1)} custom-call(f32[512,512]{1,0:T(8,128)S(1)} %get-tuple-element.69.centre_ref, bf16[512,512]{1,0:T(8,128)(2,1)S(1)} %collective-permute-done.9.one_side_ref, bf16[512,512]{1,0:T(8,128)(2,1)S(1)} %collective-permute-done.10.other_side_ref, ...), custom_call_target="tpu_custom_call", output_to_operand_aliasing={{}: (6, {})} | custom-call | flops 536870912 | bytes 8392704 | tf_op jit(solution)/shard_map/finish2/pallas_call | solution.py:51
  63.4 0.0 collective-permute-done.8.other_side_ref
  63.4 1.8 %finish0.1.rest_0_ = bf16[2048,1024]{1,0:T(8,128)(2,1)} custom-call(f32[512,512]{1,0:T(8,128)S(1)} %get-tuple-element.65.centre_ref, bf16[512,512]{1,0:T(8,128)(2,1)S(1)} %collective-permute-done.7.one_side_ref, bf16[512,512]{1,0:T(8,128)(2,1)S(1)} %collective-permute-done.8.other_side_ref, ...), custom_call_target="tpu_custom_call", output_to_operand_aliasing={{}: (6, {})} | custom-call | flops 536870912 | bytes 8392704 | tf_op jit(solution)/shard_map/finish0/pallas_call | solution.py:51
  65.2 4.3 %collective-permute-done.5.one_side_ref = bf16[384,512]{1,0:T(8,128)(2,1)S(1)} collective-permute-done((bf16[384,512]{1,0:T(8,128)(2,1)S(1)}, bf16[384,512]{1,0:T(8,128)(2,1)S(1)}, u32[]{:S(2)}, u32[]{:S(2)}) %collective-permute-start.5) | collective-permute-done | bytes 393248 | tf_op jit(solution)/shard_map/ppermute | solution.py:28
  69.6 0.0 collective-permute-done.6.other_side_ref
  69.6 1.6 %finish3.2.rest_0_ = bf16[2048,1024]{1,0:T(8,128)(2,1)} custom-call(f32[512,512]{1,0:T(8,128)S(1)} %get-tuple-element.59.centre_ref, bf16[384,512]{1,0:T(8,128)(2,1)S(1)} %collective-permute-done.5.one_side_ref, bf16[384,512]{1,0:T(8,128)(2,1)S(1)} %collective-permute-done.6.other_side_ref, ...), custom_call_target="tpu_custom_call", output_to_operand_aliasing={{}: (6, {})} | custom-call | flops 402653184 | bytes 8130560 | tf_op jit(solution)/shard_map/finish3/pallas_call | solution.py:51
  71.2 0.0 collective-permute-done.3.one_side_ref
  71.2 0.0 collective-permute-done.4.other_side_ref
  71.3 1.1 %finish3.3 = bf16[2048,1024]{1,0:T(8,128)(2,1)} custom-call(f32[512,512]{1,0:T(8,128)S(1)} %get-tuple-element.59.centre_ref, bf16[128,512]{1,0:T(8,128)(2,1)S(1)} %collective-permute-done.3.one_side_ref, bf16[128,512]{1,0:T(8,128)(2,1)S(1)} %collective-permute-done.4.other_side_ref, ...), custom_call_target="tpu_custom_call", output_to_operand_aliasing={{}: (6, {})} | custom-call | flops 134217728 | bytes 7606272 | tf_op jit(solution)/shard_map/finish3/pallas_call | solution.py:51
Async XLA Ops:
  0.0 8.9 %copy-start = (bf16[3,1024,512]{2,1,0:T(8,128)(2,1)S(1)}, bf16[3,1024,512]{2,1,0:T(8,128)(2,1)}, u32[]{:S(2)}) copy-start(bf16[3,1024,512]{2,1,0:T(8,128)(2,1)} %refs_4_.4) | copy-start | bytes 9437188
  0.0 8.9 %copy-start.2 = (bf16[2048,1024]{1,0:T(8,128)(2,1)S(1)}, bf16[2048,1024]{1,0:T(8,128)(2,1)}, u32[]{:S(2)}) copy-start(bf16[2048,1024]{1,0:T(8,128)(2,1)} %refs_0_.5) | copy-start | bytes 12582916
  0.0 8.9 %copy-start.7 = (f32[1024]{0:T(1024)S(1)}, f32[1024]{0:T(1024)}, u32[]{:S(2)}) copy-start(f32[1024]{0:T(1024)} %param.13) | copy-start | bytes 12292
  0.0 8.9 %copy-start.8 = (f32[512]{0:T(512)S(1)}, f32[512]{0:T(512)}, u32[]{:S(2)}) copy-start(f32[512]{0:T(512)} %param.11) | copy-start | bytes 6148
  2.2 30.0 %collective-permute-start = (bf16[384,512]{1,0:T(8,128)(2,1)S(1)}, bf16[384,512]{1,0:T(8,128)(2,1)S(1)}, u32[]{:S(2)}, u32[]{:S(2)}) collective-permute-start(bf16[384,512]{1,0:T(8,128)(2,1)S(1)} %get-tuple-element.54), channel_id=1, source_target_pairs={{0,31},{1,2},{2,1},{3,4},{4,3},{5,6},{6,5},{7,8},{8,7},{9,10},{10,... | collective-permute-start | bytes 1179656 | tf_op jit(solution)/shard_map/ppermute | solution.py:28
  9.0 6.0 %copy-start.3 = (bf16[3,1024,512]{2,1,0:T(8,128)(2,1)S(1)}, bf16[3,1024,512]{2,1,0:T(8,128)(2,1)}, u32[]{:S(2)}) copy-start(bf16[3,1024,512]{2,1,0:T(8,128)(2,1)} %refs_4_.5) | copy-start | bytes 9437188
  14.1 22.2 %collective-permute-start.11 = (bf16[512,512]{1,0:T(8,128)(2,1)S(1)}, bf16[512,512]{1,0:T(8,128)(2,1)S(1)}, u32[]{:S(2)}, u32[]{:S(2)}) collective-permute-start(bf16[512,512]{1,0:T(8,128)(2,1)S(1)} %get-tuple-element.74), channel_id=1, source_target_pairs={{0,30},{1,31},{2,4},{3,5},{4,2},{5,3},{6,8},{7,9},{8,6},{9,7},{10,... | collective-permute-start | bytes 1572872 | tf_op jit(solution)/shard_map/ppermute | solution.py:28
  15.8 5.0 %copy-start.1 = (bf16[3,1024,512]{2,1,0:T(8,128)(2,1)S(1)}, bf16[3,1024,512]{2,1,0:T(8,128)(2,1)}, u32[]{:S(2)}) copy-start(bf16[3,1024,512]{2,1,0:T(8,128)(2,1)} %refs_4_.4) | copy-start | bytes 9437188
  15.8 5.0 %copy-start.5 = (bf16[512,1024]{1,0:T(8,128)(2,1)S(1)}, bf16[512,1024]{1,0:T(8,128)(2,1)}, u32[]{:S(2)}) copy-start(bf16[512,1024]{1,0:T(8,128)(2,1)} %refs_6_.3) | copy-start | bytes 3145732
  15.8 16.4 %collective-permute-start.1 = (bf16[128,512]{1,0:T(8,128)(2,1)S(1)}, bf16[128,512]{1,0:T(8,128)(2,1)S(1)}, u32[]{:S(2)}, u32[]{:S(2)}) collective-permute-start(bf16[128,512]{1,0:T(8,128)(2,1)S(1)} %get-tuple-element.55), channel_id=1, source_target_pairs={{0,31},{1,2},{2,1},{3,4},{4,3},{5,6},{6,5},{7,8},{8,7},{9,10},{10,... | collective-permute-start | bytes 393224 | tf_op jit(solution)/shard_map/ppermute | solution.py:28
  16.6 29.6 %collective-permute-start.12 = (bf16[512,512]{1,0:T(8,128)(2,1)S(1)}, bf16[512,512]{1,0:T(8,128)(2,1)S(1)}, u32[]{:S(2)}, u32[]{:S(2)}) collective-permute-start(bf16[512,512]{1,0:T(8,128)(2,1)S(1)} %get-tuple-element.75), channel_id=1, source_target_pairs={{0,2},{1,3},{2,0},{3,1},{4,6},{5,7},{6,4},{7,5},{8,10},{9,11},{10,... | collective-permute-start | bytes 1572872 | tf_op jit(solution)/shard_map/ppermute | solution.py:28
  20.8 20.9 %collective-permute-start.2 = (bf16[512,512]{1,0:T(8,128)(2,1)S(1)}, bf16[512,512]{1,0:T(8,128)(2,1)S(1)}, u32[]{:S(2)}, u32[]{:S(2)}) collective-permute-start(bf16[512,512]{1,0:T(8,128)(2,1)S(1)} %get-tuple-element.57), channel_id=1, source_target_pairs={{0,1},{1,0},{2,3},{3,2},{4,5},{5,4},{6,7},{7,6},{8,9},{9,8},{10,11... | collective-permute-start | bytes 1572872 | tf_op jit(solution)/shard_map/ppermute | solution.py:28
  32.2 18.2 %collective-permute-start.9 = (bf16[512,512]{1,0:T(8,128)(2,1)S(1)}, bf16[512,512]{1,0:T(8,128)(2,1)S(1)}, u32[]{:S(2)}, u32[]{:S(2)}) collective-permute-start(bf16[512,512]{1,0:T(8,128)(2,1)S(1)} %get-tuple-element.70), channel_id=1, source_target_pairs={{0,30},{1,31},{2,4},{3,5},{4,2},{5,3},{6,8},{7,9},{8,6},{9,7},{10,... | collective-permute-start | bytes 1572872 | tf_op jit(solution)/shard_map/ppermute | solution.py:28
  32.2 22.4 %collective-permute-start.10 = (bf16[512,512]{1,0:T(8,128)(2,1)S(1)}, bf16[512,512]{1,0:T(8,128)(2,1)S(1)}, u32[]{:S(2)}, u32[]{:S(2)}) collective-permute-start(bf16[512,512]{1,0:T(8,128)(2,1)S(1)} %get-tuple-element.71), channel_id=1, source_target_pairs={{0,2},{1,3},{2,0},{3,1},{4,6},{5,7},{6,4},{7,5},{8,10},{9,11},{10,... | collective-permute-start | bytes 1572872 | tf_op jit(solution)/shard_map/ppermute | solution.py:28
  36.2 25.4 %collective-permute-start.7 = (bf16[512,512]{1,0:T(8,128)(2,1)S(1)}, bf16[512,512]{1,0:T(8,128)(2,1)S(1)}, u32[]{:S(2)}, u32[]{:S(2)}) collective-permute-start(bf16[512,512]{1,0:T(8,128)(2,1)S(1)} %get-tuple-element.66), channel_id=1, source_target_pairs={{0,30},{1,31},{2,4},{3,5},{4,2},{5,3},{6,8},{7,9},{8,6},{9,7},{10,... | collective-permute-start | bytes 1572872 | tf_op jit(solution)/shard_map/ppermute | solution.py:28
  41.6 8.8 %copy-start.9 = (f32[512]{0:T(512)S(1)}, f32[512]{0:T(512)}, u32[]{:S(2)}) copy-start(f32[512]{0:T(512)} %param.15) | copy-start | bytes 6148
  41.6 21.8 %collective-permute-start.8 = (bf16[512,512]{1,0:T(8,128)(2,1)S(1)}, bf16[512,512]{1,0:T(8,128)(2,1)S(1)}, u32[]{:S(2)}, u32[]{:S(2)}) collective-permute-start(bf16[512,512]{1,0:T(8,128)(2,1)S(1)} %get-tuple-element.67), channel_id=1, source_target_pairs={{0,2},{1,3},{2,0},{3,1},{4,6},{5,7},{6,4},{7,5},{8,10},{9,11},{10,... | collective-permute-start | bytes 1572872 | tf_op jit(solution)/shard_map/ppermute | solution.py:28
  46.2 6.5 %copy-start.4 = (bf16[512,1024]{1,0:T(8,128)(2,1)S(1)}, bf16[512,1024]{1,0:T(8,128)(2,1)}, u32[]{:S(2)}) copy-start(bf16[512,1024]{1,0:T(8,128)(2,1)} %point_ref.9) | copy-start | bytes 3145732
  46.2 6.5 %copy-start.6 = (f32[1024]{0:T(1024)S(1)}, f32[1024]{0:T(1024)}, u32[]{:S(2)}) copy-start(f32[1024]{0:T(1024)} %param.17) | copy-start | bytes 12292
  46.2 23.4 %collective-permute-start.5 = (bf16[384,512]{1,0:T(8,128)(2,1)S(1)}, bf16[384,512]{1,0:T(8,128)(2,1)S(1)}, u32[]{:S(2)}, u32[]{:S(2)}) collective-permute-start(bf16[384,512]{1,0:T(8,128)(2,1)S(1)} %get-tuple-element.63), channel_id=1, source_target_pairs={{0,30},{1,31},{2,4},{3,5},{4,2},{5,3},{6,8},{7,9},{8,6},{9,7},{10,... | collective-permute-start | bytes 1179656 | tf_op jit(solution)/shard_map/ppermute | solution.py:28
  50.4 19.2 %collective-permute-start.6 = (bf16[384,512]{1,0:T(8,128)(2,1)S(1)}, bf16[384,512]{1,0:T(8,128)(2,1)S(1)}, u32[]{:S(2)}, u32[]{:S(2)}) collective-permute-start(bf16[384,512]{1,0:T(8,128)(2,1)S(1)} %get-tuple-element.64), channel_id=1, source_target_pairs={{0,2},{1,3},{2,0},{3,1},{4,6},{5,7},{6,4},{7,5},{8,10},{9,11},{10,... | collective-permute-start | bytes 1179656 | tf_op jit(solution)/shard_map/ppermute | solution.py:28
  54.6 16.7 %collective-permute-start.3 = (bf16[128,512]{1,0:T(8,128)(2,1)S(1)}, bf16[128,512]{1,0:T(8,128)(2,1)S(1)}, u32[]{:S(2)}, u32[]{:S(2)}) collective-permute-start(bf16[128,512]{1,0:T(8,128)(2,1)S(1)} %get-tuple-element.60), channel_id=1, source_target_pairs={{0,30},{1,31},{2,4},{3,5},{4,2},{5,3},{6,8},{7,9},{8,6},{9,7},{10,... | collective-permute-start | bytes 393224 | tf_op jit(solution)/shard_map/ppermute | solution.py:28
  61.6 9.6 %collective-permute-start.4 = (bf16[128,512]{1,0:T(8,128)(2,1)S(1)}, bf16[128,512]{1,0:T(8,128)(2,1)S(1)}, u32[]{:S(2)}, u32[]{:S(2)}) collective-permute-start(bf16[128,512]{1,0:T(8,128)(2,1)S(1)} %get-tuple-element.61), channel_id=1, source_target_pairs={{0,2},{1,3},{2,0},{3,1},{4,6},{5,7},{6,4},{7,5},{8,10},{9,11},{10,... | collective-permute-start | bytes 393224 | tf_op jit(solution)/shard_map/ppermute | solution.py:28

commit v8 on v7

--- a/solution.py
+++ b/solution.py
@@ -12,8 +12,7 @@
 ANY = pl.BlockSpec(memory_space=pl.ANY)
 HBM = pl.BlockSpec(memory_space=pltpu.HBM)
 SLOPE = math.sqrt(2.0 / math.pi)
-LAST_PIECE = 128
-LATE = 128
+LAST_PIECE = 160
 BF16 = jnp.bfloat16
 F32 = jnp.float32
 
@@ -102,23 +101,6 @@
     )
 
 
-def behind_first(far, outer, act_top, act_bottom, taps):
-    size, c = far.shape
-    m = outer.shape[2]
-    late = act_bottom.shape[0]
-
-    def body(far_ref, outer_ref, top_ref, bottom_ref, taps_ref, first_ref, late_ref, act_ref):
-        first_ref[...] = dot(far_ref[...], outer_ref[2 * odd_pair()]).astype(BF16)
-        late_ref[...] = dot(bottom_ref[...], taps_ref[2 - 2 * odd_position()]).astype(BF16)
-        act_ref[: size - late, :] = top_ref[...]
-        act_ref[size - late :, :] = bottom_ref[...]
-
-    return call(
-        body, "behind1", [shape(size, m), shape(late, m), shape(size, c)], (far, outer, act_top, act_bottom, taps),
-        2 * size * c * m, [], specs=[VMEM] * 5,
-    )
-
-
 def odd_pair():
     return lax.rem(lax.div(lax.axis_index("seq"), 2), 2)
 
@@ -129,18 +111,17 @@
 
     def body(
         x_ref, before_ref, taps_ref, bias_conv_ref, point_hbm, bias_point_ref, outer_hbm,
-        bottom_ref, act1_ref, act2_ref, one_ref, far_ref, second_ref, point_own, outer_own, sems,
+        act1_ref, act2_ref, one_ref, far_ref, first_ref, second_ref, point_own, outer_own, sems,
     ):
         copies = [
             pltpu.make_async_copy(point_hbm, point_own, sems.at[0]),
-            pltpu.make_async_copy(outer_hbm.at[2 - 2 * odd_pair()], outer_own, sems.at[1]),
+            pltpu.make_async_copy(outer_hbm.at[2 - 2 * odd_pair()], outer_own.at[1], sems.at[1]),
+            pltpu.make_async_copy(outer_hbm.at[2 * odd_pair()], outer_own.at[0], sems.at[2]),
         ]
         for copy in copies:
             copy.start()
         odd = odd_position()
-        at = quarter_rows(0, size).start + size - LATE
-        bottom_ref[...] = gelu(x_ref[pl.ds(pl.multiple_of(at, LATE), LATE), :].astype(F32)).astype(BF16)
-        total = jnp.concatenate([dot(before_ref[...], taps_ref[2 * odd]), dot(bottom_ref[...], taps_ref[2 * odd])], axis=0)
+        total = dot(before_ref[...], taps_ref[2 * odd])
         act1_ref[...] = gelu(x_ref[quarter_rows(1, size), :].astype(F32)).astype(BF16)
         total = total + dot(act1_ref[...], taps_ref[1])
         act2_ref[...] = gelu(x_ref[quarter_rows(2, size), :].astype(F32)).astype(BF16)
@@ -153,13 +134,15 @@
         far = gelu(one.astype(F32)).astype(BF16)
         far_ref[...] = far
         copies[1].wait()
-        second_ref[...] = dot(far, outer_own[...]).astype(BF16)
+        second_ref[...] = dot(far, outer_own[1]).astype(BF16)
+        copies[2].wait()
+        first_ref[...] = dot(far, outer_own[0]).astype(BF16)
 
     point, outer = (pltpu.with_memory_space_constraint(w, pltpu.HBM) for w in (point, outer))
     args = (x, act, taps, bias_conv, point, bias_point, outer)
     return call(
-        body, "layer1", [shape(LATE, c)] + [shape(size, c)] * 4 + [shape(size, m)], args, 10 * size * c * m,
-        [pltpu.VMEM((m, c), BF16), pltpu.VMEM((c, m), BF16), pltpu.SemaphoreType.DMA((2,))],
+        body, "layer1", [shape(size, c)] * 4 + [shape(size, m)] * 2, args, 12 * size * c * m,
+        [pltpu.VMEM((m, c), BF16), pltpu.VMEM((2, c, m), BF16), pltpu.SemaphoreType.DMA((3,))],
         specs=[VMEM] * 4 + [HBM, VMEM, HBM],
     )
 
@@ -256,7 +239,7 @@
             mid = gelu(total).astype(BF16)
             out = one_ref[own, :].astype(F32) + dot(mid, point_ref[...]) + bias_ref[...]
             held[k] = out.astype(BF16)
-            to = pl.ds(pl.multiple_of(start + k * step, 128), step)
+            to = pl.ds(pl.multiple_of(start + k * step, 32), step)
             copies.append(pltpu.make_async_copy(held.at[k], out_hbm.at[to], sems.at[k]))
             copies[k].start()
         for copy in copies:
@@ -301,21 +284,17 @@
     def send(products):
         return [(second_matching(second), first_matching(first)) for first, second in products]
 
-    act_top, direct = rim(x, rim_taps, 0, size - LATE)
-    from_pair = swap(direct, lambda i: i % 2 == 1, 1)
-    act_bottom, act1, act2, one1, far1, second1 = first_quarter(tower_input, act_top, near)
-    far1, second1 = lax.optimization_barrier((far1, second1))
-    side1 = second_matching(second1)
-    first1, late, act0 = behind_first(far1, second_conv_taps, act_top, act_bottom, first_conv_taps)
-    later, first1, late = lax.optimization_barrier((x, first1, late))
-    from_pair_late = swap(late, lambda i: i % 2 == 1, 1)
-    sides1 = [(side1, first_matching(first1))]
+    act0, to_pair = rim(x, rim_taps, 0, size)
+    from_pair = swap(to_pair, lambda i: i % 2 == 1, 1)
+    act1, act2, one1, far1, *products1 = first_quarter(tower_input, act0, near)
+    later, products1 = lax.optimization_barrier((x, products1))
+    sides1 = send([products1])
     act3, for_partner = rim(later, rim_taps, 3, size)
     from_partner = to_partner(for_partner)
     one2, far2, products2 = layer(x, 2, (act1, act2, act3), [], near, whole)
     sides2 = send(products2)
     one0, far0, products0 = layer(
-        x, 0, (None, act0, act1), [(from_pair, 0), (from_pair_late, 0)], near, whole
+        x, 0, (None, act0, act1), [(from_pair, 0)], near, whole
     )
     sides0 = send(products0)
     one3, far3, products3 = layer(x, 3, (act2, act3, None), [(from_partner, 0)], near, split)

time: 73.4 us -> 67.4 us (0.918)
  waiting for transfers between devices: 18.3 us -> 8.17 us
  starting transfers between devices: 19.4 us -> 23.8 us
    ppermute x13 -> x12, waiting for transfers between devices: 18.3 us -> 8.17 us  [swap(): return lax.ppermute(value, 'seq', sorted(pairs))]
    ppermute x13 -> x12, starting transfers between devices: 19.4 us -> 23.8 us  [swap(): return lax.ppermute(value, 'seq', sorted(pairs))]
    pallas_call x13 -> x12, Pallas kernels: 34.3 us -> 34.3 us  [call(): pl.pallas_call(body, in_specs=specs, out_specs=[VMEM] * len(out_shape) if...]
  transfers between devices with their start and end apart: 13 -> 12, of which waited for: 4 -> 5; matrix products, arithmetic and copies ran while one was open for 0% -> 0% of each run, Pallas kernels for 43% -> 46%
where the time goes in v8:
time: 67.4 us; the launch traced here: 66.6 us
  Pallas kernels  34.3 us (51%)
  starting transfers between devices  23.8 us (35%)
  waiting for transfers between devices  8.17 us (12%)
    pallas_call x12, Pallas kernels, call(): pl.pallas_call(body, in_specs=specs, out_specs=[VMEM] * len(out_shape) if...  34.3 us
    ppermute x12, starting transfers between devices, swap(): return lax.ppermute(value, 'seq', sorted(pairs))  23.8 us
    ppermute x12, waiting for transfers between devices, swap(): return lax.ppermute(value, 'seq', sorted(pairs))  8.17 us
  transfers between devices with their start and end apart: 12, of which 5 were waited for; matrix products, arithmetic and copies ran while one was open for 0% of the time, Pallas kernels for 46%

profile of v8, /device:TPU:0, one launch (start us, length us, event | category | flops | bytes accessed | tf_op | source)
XLA Modules:
  0.0 66.6 jit_solution(7311338927115452637)
XLA Ops:
  0.0 0.0 copy-start.1
  0.0 0.0 copy-start
  0.0 0.0 copy-start.7
  0.0 0.0 copy-start.8
  0.0 2.4 %rim0.1 = (bf16[512,1024]{1,0:T(8,128)(2,1)S(1)}, bf16[512,512]{1,0:T(8,128)(2,1)S(1)}) custom-call(bf16[2048,1024]{1,0:T(8,128)(2,1)} %refs_0_.5, bf16[3,1024,512]{2,1,0:T(8,128)(2,1)} %refs_4_.6), custom_call_target="tpu_custom_call" | custom-call | flops 536870912 | bytes 7340032 | tf_op jit(solution)/shard_map/rim0/pallas_call | solution.py:50
  2.4 6.7 %collective-permute-start = (bf16[512,512]{1,0:T(8,128)(2,1)S(1)}, bf16[512,512]{1,0:T(8,128)(2,1)S(1)}, u32[]{:S(2)}, u32[]{:S(2)}) collective-permute-start(bf16[512,512]{1,0:T(8,128)(2,1)S(1)} %get-tuple-element.45), channel_id=1, source_target_pairs={{0,31},{1,2},{2,1},{3,4},{4,3},{5,6},{6,5},{7,8},{8,7},{9,10},{10,... | collective-permute-start | bytes 1572872 | tf_op jit(solution)/shard_map/ppermute | solution.py:27
  9.2 0.0 copy-done.1
  9.2 0.0 copy-done
  9.2 0.0 copy-done.7
  9.2 0.0 copy-done.8
  9.2 5.1 %layer1.1 = (bf16[512,1024]{1,0:T(8,128)(2,1)S(1)}, bf16[512,1024]{1,0:T(8,128)(2,1)S(1)}, bf16[512,1024]{1,0:T(8,128)(2,1)S(1)}, bf16[512,1024]{1,0:T(8,128)(2,...) custom-call(bf16[2048,1024]{1,0:T(8,128)(2,1)S(1)} %copy-done, ...), custom_call_target="tpu_custom_call" | custom-call | flops 3221225472 | bytes 12589056 | tf_op jit(solution)/shard_map/layer1/pallas_call | solution.py:50
  14.3 0.0 copy-start.2
  14.4 0.0 copy-start.3
  14.4 0.0 copy-start.5
  14.4 0.9 %collective-permute-start.10 = (bf16[512,512]{1,0:T(8,128)(2,1)S(1)}, bf16[512,512]{1,0:T(8,128)(2,1)S(1)}, u32[]{:S(2)}, u32[]{:S(2)}) collective-permute-start(bf16[512,512]{1,0:T(8,128)(2,1)S(1)} %get-tuple-element.64), channel_id=1, source_target_pairs={{0,30},{1,31},{2,4},{3,5},{4,2},{5,3},{6,8},{7,9},{8,6},{9,7},{10,... | collective-permute-start | bytes 1572872 | tf_op jit(solution)/shard_map/ppermute | solution.py:27
  15.3 0.0 collective-permute-start.11
  15.3 2.7 %rim3.1 = (bf16[512,1024]{1,0:T(8,128)(2,1)S(1)}, bf16[512,512]{1,0:T(8,128)(2,1)S(1)}) custom-call(bf16[2048,1024]{1,0:T(8,128)(2,1)} %refs_0_.5, bf16[3,1024,512]{2,1,0:T(8,128)(2,1)} %refs_4_.6), custom_call_target="tpu_custom_call" | custom-call | flops 536870912 | bytes 7340032 | tf_op jit(solution)/shard_map/rim3/pallas_call | solution.py:50
  18.0 0.6 collective-permute-start.1
  18.6 0.0 copy-done.2
  18.6 0.0 copy-done.3
  18.6 0.0 copy-done.5
  18.6 5.0 %layer2.1 = (bf16[512,1024]{1,0:T(8,128)(2,1)S(1)}, bf16[512,1024]{1,0:T(8,128)(2,1)S(1)}, bf16[512,512]{1,0:T(8,128)(2,1)S(1)}, bf16[512,512]{1,0:T(8,128)(2,1)S(1)}) custom-call(bf16[2048,1024]{1,0:T(8,128)(2,1)} %refs_0_.5, bf16[512,1024]{1,0:T(8,128)(2,1)S(1)} %get-tuple-element.38.refs_1_.refs_2_, ...), custom_call_target="tpu_custom_call" | custom-call | flops 3221225472 | bytes 14686208 | tf_op jit(solution)/shard_map/layer2/pallas_call | solution.py:50
  23.6 3.7 %collective-permute-start.8 = (bf16[512,512]{1,0:T(8,128)(2,1)S(1)}, bf16[512,512]{1,0:T(8,128)(2,1)S(1)}, u32[]{:S(2)}, u32[]{:S(2)}) collective-permute-start(bf16[512,512]{1,0:T(8,128)(2,1)S(1)} %get-tuple-element.60), channel_id=1, source_target_pairs={{0,30},{1,31},{2,4},{3,5},{4,2},{5,3},{6,8},{7,9},{8,6},{9,7},{10,... | collective-permute-start | bytes 1572872 | tf_op jit(solution)/shard_map/ppermute | solution.py:27
  27.3 0.0 collective-permute-done.refs_3_
  27.3 0.0 collective-permute-start.9
  27.3 4.0 %layer0.1 = (bf16[512,1024]{1,0:T(8,128)(2,1)S(1)}, bf16[512,1024]{1,0:T(8,128)(2,1)S(1)}, bf16[512,512]{1,0:T(8,128)(2,1)S(1)}, bf16[512,512]{1,0:T(8,128)(2,1)S(1)}) custom-call(bf16[2048,1024]{1,0:T(8,128)(2,1)} %refs_0_.5, bf16[512,1024]{1,0:T(8,128)(2,1)S(1)} %get-tuple-element.36.before_ref.refs_1_, ...), custom_call_target="tpu_custom_call" | custom-call | flops 3221225472 | bytes 14161920 | tf_op jit(solution)/shard_map/layer0/pallas_call | solution.py:50
  31.3 1.5 %collective-permute-done.10.one_side_ref = bf16[512,512]{1,0:T(8,128)(2,1)S(1)} collective-permute-done((bf16[512,512]{1,0:T(8,128)(2,1)S(1)}, bf16[512,512]{1,0:T(8,128)(2,1)S(1)}, u32[]{:S(2)}, u32[]{:S(2)}) %collective-permute-start.10) | collective-permute-done | bytes 524320 | tf_op jit(solution)/shard_map/ppermute | solution.py:27
  32.7 5.8 %collective-permute-start.6 = (bf16[512,512]{1,0:T(8,128)(2,1)S(1)}, bf16[512,512]{1,0:T(8,128)(2,1)S(1)}, u32[]{:S(2)}, u32[]{:S(2)}) collective-permute-start(bf16[512,512]{1,0:T(8,128)(2,1)S(1)} %get-tuple-element.56), channel_id=1, source_target_pairs={{0,30},{1,31},{2,4},{3,5},{4,2},{5,3},{6,8},{7,9},{8,6},{9,7},{10,... | collective-permute-start | bytes 1572872 | tf_op jit(solution)/shard_map/ppermute | solution.py:27
  38.5 0.0 collective-permute-done.1.refs_3_
  38.5 0.0 copy-start.9
  38.5 0.0 collective-permute-start.7
  38.6 4.6 %layer3.1 = (bf16[512,1024]{1,0:T(8,128)(2,1)S(1)}, bf16[512,1024]{1,0:T(8,128)(2,1)S(1)}, bf16[352,512]{1,0:T(8,128)(2,1)S(1)}, bf16[160,512]{1,0:T(8,128)(2,1)...) custom-call(bf16[2048,1024]{1,0:T(8,128)(2,1)} %refs_0_.5, ...), custom_call_target="tpu_custom_call" | custom-call | flops 3221225472 | bytes 14161920 | tf_op jit(solution)/shard_map/layer3/pallas_call | solution.py:50
  43.1 0.0 copy-start.4
  43.1 0.0 copy-start.6
  43.1 0.0 collective-permute-done.11.other_side_ref
  43.2 0.2 collective-permute-start.4
  43.3 0.6 collective-permute-done.8.one_side_ref
  44.0 1.4 %collective-permute-start.5 = (bf16[352,512]{1,0:T(8,128)(2,1)S(1)}, bf16[352,512]{1,0:T(8,128)(2,1)S(1)}, u32[]{:S(2)}, u32[]{:S(2)}) collective-permute-start(bf16[352,512]{1,0:T(8,128)(2,1)S(1)} %get-tuple-element.54), channel_id=1, source_target_pairs={{0,2},{1,3},{2,0},{3,1},{4,6},{5,7},{6,4},{7,5},{8,10},{9,11},{10,... | collective-permute-start | bytes 1081352 | tf_op jit(solution)/shard_map/ppermute | solution.py:27
  45.4 0.0 copy-done.9
  45.4 2.3 %centre.1 = (f32[512,512]{1,0:T(8,128)S(1)}, f32[512,512]{1,0:T(8,128)S(1)}, f32[512,512]{1,0:T(8,128)S(1)}, f32[512,512]{1,0:T(8,128)S(1)}) custom-call(bf16[512,1024]{1,0:T(8,128)(2,1)S(1)} %get-tuple-element.37.refs_0_, bf16[512,1024]{1,0:T(8,128)(2,1)S(1)} %get-tuple-element.44.refs_1_, bf16[512,1024]{1,0:T(8,128)(2,1)S(1)} %get-tuple-element.46.refs_2_, ...), custom_call_target="tpu_custom_call" | custom-call | flops 2147483648 | bytes 7342080 | tf_op jit(solution)/shard_map/centre/pallas_call | solution.py:50
  47.7 0.0 collective-permute-done.9.other_side_ref
  47.7 4.5 %collective-permute-start.2 = (bf16[160,512]{1,0:T(8,128)(2,1)S(1)}, bf16[160,512]{1,0:T(8,128)(2,1)S(1)}, u32[]{:S(2)}, u32[]{:S(2)}) collective-permute-start(bf16[160,512]{1,0:T(8,128)(2,1)S(1)} %get-tuple-element.50), channel_id=1, source_target_pairs={{0,30},{1,31},{2,4},{3,5},{4,2},{5,3},{6,8},{7,9},{8,6},{9,7},{10,... | collective-permute-start | bytes 491528 | tf_op jit(solution)/shard_map/ppermute | solution.py:27
  52.2 3.0 %collective-permute-done.6.one_side_ref = bf16[512,512]{1,0:T(8,128)(2,1)S(1)} collective-permute-done((bf16[512,512]{1,0:T(8,128)(2,1)S(1)}, bf16[512,512]{1,0:T(8,128)(2,1)S(1)}, u32[]{:S(2)}, u32[]{:S(2)}) %collective-permute-start.6) | collective-permute-done | bytes 524320 | tf_op jit(solution)/shard_map/ppermute | solution.py:27
  55.2 0.0 collective-permute-start.3
  55.2 0.0 copy-done.4
  55.2 0.0 copy-done.6
  55.2 1.8 %finish1.1.rest_0_ = bf16[2048,1024]{1,0:T(8,128)(2,1)} custom-call(f32[512,512]{1,0:T(8,128)S(1)} %get-tuple-element.63.centre_ref, bf16[512,512]{1,0:T(8,128)(2,1)S(1)} %collective-permute-done.10.one_side_ref, bf16[512,512]{1,0:T(8,128)(2,1)S(1)} %collective-permute-done.11.other_side_ref, bf16[512,1024]{1,0:T(8,128)(2,1)S(1)} %get-tuple-element.66.one_ref, ...), custom_call_target="tpu_custom_call" | custom-call | flops 536870912 | bytes 4198400 | tf_op jit(solution)/shard_map/finish1/pallas_call | solution.py:50
  57.0 1.8 %finish2.1.rest_0_ = bf16[2048,1024]{1,0:T(8,128)(2,1)} custom-call(f32[512,512]{1,0:T(8,128)S(1)} %get-tuple-element.59.centre_ref, bf16[512,512]{1,0:T(8,128)(2,1)S(1)} %collective-permute-done.8.one_side_ref, bf16[512,512]{1,0:T(8,128)(2,1)S(1)} %collective-permute-done.9.other_side_ref, ...), custom_call_target="tpu_custom_call", output_to_operand_aliasing={{}: (6, {})} | custom-call | flops 536870912 | bytes 8392704 | tf_op jit(solution)/shard_map/finish2/pallas_call | solution.py:50
  58.9 0.0 collective-permute-done.7.other_side_ref
  58.9 1.8 %finish0.1.rest_0_ = bf16[2048,1024]{1,0:T(8,128)(2,1)} custom-call(f32[512,512]{1,0:T(8,128)S(1)} %get-tuple-element.55.centre_ref, bf16[512,512]{1,0:T(8,128)(2,1)S(1)} %collective-permute-done.6.one_side_ref, bf16[512,512]{1,0:T(8,128)(2,1)S(1)} %collective-permute-done.7.other_side_ref, ...), custom_call_target="tpu_custom_call", output_to_operand_aliasing={{}: (6, {})} | custom-call | flops 536870912 | bytes 8392704 | tf_op jit(solution)/shard_map/finish0/pallas_call | solution.py:50
  60.7 2.3 %collective-permute-done.4.one_side_ref = bf16[352,512]{1,0:T(8,128)(2,1)S(1)} collective-permute-done((bf16[352,512]{1,0:T(8,128)(2,1)S(1)}, bf16[352,512]{1,0:T(8,128)(2,1)S(1)}, u32[]{:S(2)}, u32[]{:S(2)}) %collective-permute-start.4) | collective-permute-done | bytes 360480 | tf_op jit(solution)/shard_map/ppermute | solution.py:27
  62.9 0.0 collective-permute-done.5.other_side_ref
  62.9 1.6 %finish3.2.rest_0_ = bf16[2048,1024]{1,0:T(8,128)(2,1)} custom-call(f32[512,512]{1,0:T(8,128)S(1)} %get-tuple-element.49.centre_ref, bf16[352,512]{1,0:T(8,128)(2,1)S(1)} %collective-permute-done.4.one_side_ref, bf16[352,512]{1,0:T(8,128)(2,1)S(1)} %collective-permute-done.5.other_side_ref, ...), custom_call_target="tpu_custom_call", output_to_operand_aliasing={{}: (6, {})} | custom-call | flops 369098752 | bytes 8065024 | tf_op jit(solution)/shard_map/finish3/pallas_call | solution.py:50
  64.5 0.8 %collective-permute-done.2.one_side_ref = bf16[160,512]{1,0:T(8,128)(2,1)S(1)} collective-permute-done((bf16[160,512]{1,0:T(8,128)(2,1)S(1)}, bf16[160,512]{1,0:T(8,128)(2,1)S(1)}, u32[]{:S(2)}, u32[]{:S(2)}) %collective-permute-start.2) | collective-permute-done | bytes 163872 | tf_op jit(solution)/shard_map/ppermute | solution.py:27
  65.3 0.0 collective-permute-done.3.other_side_ref
  65.3 1.2 %finish3.3 = bf16[2048,1024]{1,0:T(8,128)(2,1)} custom-call(f32[512,512]{1,0:T(8,128)S(1)} %get-tuple-element.49.centre_ref, bf16[160,512]{1,0:T(8,128)(2,1)S(1)} %collective-permute-done.2.one_side_ref, bf16[160,512]{1,0:T(8,128)(2,1)S(1)} %collective-permute-done.3.other_side_ref, ...), custom_call_target="tpu_custom_call", output_to_operand_aliasing={{}: (6, {})} | custom-call | flops 167772160 | bytes 7671808 | tf_op jit(solution)/shard_map/finish3/pallas_call | solution.py:50
Async XLA Ops:
  0.0 9.2 %copy-start.1 = (bf16[3,1024,512]{2,1,0:T(8,128)(2,1)S(1)}, bf16[3,1024,512]{2,1,0:T(8,128)(2,1)}, u32[]{:S(2)}) copy-start(bf16[3,1024,512]{2,1,0:T(8,128)(2,1)} %refs_4_.6) | copy-start | bytes 9437188
  0.0 9.2 %copy-start = (bf16[2048,1024]{1,0:T(8,128)(2,1)S(1)}, bf16[2048,1024]{1,0:T(8,128)(2,1)}, u32[]{:S(2)}) copy-start(bf16[2048,1024]{1,0:T(8,128)(2,1)} %refs_0_.5) | copy-start | bytes 12582916
  0.0 9.2 %copy-start.7 = (f32[1024]{0:T(1024)S(1)}, f32[1024]{0:T(1024)}, u32[]{:S(2)}) copy-start(f32[1024]{0:T(1024)} %param.13) | copy-start | bytes 12292
  0.0 9.2 %copy-start.8 = (f32[512]{0:T(512)S(1)}, f32[512]{0:T(512)}, u32[]{:S(2)}) copy-start(f32[512]{0:T(512)} %param.11) | copy-start | bytes 6148
  2.4 24.9 %collective-permute-start = (bf16[512,512]{1,0:T(8,128)(2,1)S(1)}, bf16[512,512]{1,0:T(8,128)(2,1)S(1)}, u32[]{:S(2)}, u32[]{:S(2)}) collective-permute-start(bf16[512,512]{1,0:T(8,128)(2,1)S(1)} %get-tuple-element.45), channel_id=1, source_target_pairs={{0,31},{1,2},{2,1},{3,4},{4,3},{5,6},{6,5},{7,8},{8,7},{9,10},{10,... | collective-permute-start | bytes 1572872 | tf_op jit(solution)/shard_map/ppermute | solution.py:27
  14.3 4.3 %copy-start.2 = (bf16[3,1024,512]{2,1,0:T(8,128)(2,1)S(1)}, bf16[3,1024,512]{2,1,0:T(8,128)(2,1)}, u32[]{:S(2)}) copy-start(bf16[3,1024,512]{2,1,0:T(8,128)(2,1)} %refs_4_.6) | copy-start | bytes 9437188
  14.4 4.2 %copy-start.3 = (bf16[3,1024,512]{2,1,0:T(8,128)(2,1)S(1)}, bf16[3,1024,512]{2,1,0:T(8,128)(2,1)}, u32[]{:S(2)}) copy-start(bf16[3,1024,512]{2,1,0:T(8,128)(2,1)} %refs_4_.7) | copy-start | bytes 9437188
  14.4 4.2 %copy-start.5 = (bf16[512,1024]{1,0:T(8,128)(2,1)S(1)}, bf16[512,1024]{1,0:T(8,128)(2,1)}, u32[]{:S(2)}) copy-start(bf16[512,1024]{1,0:T(8,128)(2,1)} %refs_6_.5) | copy-start | bytes 3145732
  14.4 18.4 %collective-permute-start.10 = (bf16[512,512]{1,0:T(8,128)(2,1)S(1)}, bf16[512,512]{1,0:T(8,128)(2,1)S(1)}, u32[]{:S(2)}, u32[]{:S(2)}) collective-permute-start(bf16[512,512]{1,0:T(8,128)(2,1)S(1)} %get-tuple-element.64), channel_id=1, source_target_pairs={{0,30},{1,31},{2,4},{3,5},{4,2},{5,3},{6,8},{7,9},{8,6},{9,7},{10,... | collective-permute-start | bytes 1572872 | tf_op jit(solution)/shard_map/ppermute | solution.py:27
  15.3 27.9 %collective-permute-start.11 = (bf16[512,512]{1,0:T(8,128)(2,1)S(1)}, bf16[512,512]{1,0:T(8,128)(2,1)S(1)}, u32[]{:S(2)}, u32[]{:S(2)}) collective-permute-start(bf16[512,512]{1,0:T(8,128)(2,1)S(1)} %get-tuple-element.65), channel_id=1, source_target_pairs={{0,2},{1,3},{2,0},{3,1},{4,6},{5,7},{6,4},{7,5},{8,10},{9,11},{10,... | collective-permute-start | bytes 1572872 | tf_op jit(solution)/shard_map/ppermute | solution.py:27
  18.0 20.5 %collective-permute-start.1 = (bf16[512,512]{1,0:T(8,128)(2,1)S(1)}, bf16[512,512]{1,0:T(8,128)(2,1)S(1)}, u32[]{:S(2)}, u32[]{:S(2)}) collective-permute-start(bf16[512,512]{1,0:T(8,128)(2,1)S(1)} %get-tuple-element.47), channel_id=1, source_target_pairs={{0,1},{1,0},{2,3},{3,2},{4,5},{5,4},{6,7},{7,6},{8,9},{9,8},{10,11... | collective-permute-start | bytes 1572872 | tf_op jit(solution)/shard_map/ppermute | solution.py:27
  23.6 20.4 %collective-permute-start.8 = (bf16[512,512]{1,0:T(8,128)(2,1)S(1)}, bf16[512,512]{1,0:T(8,128)(2,1)S(1)}, u32[]{:S(2)}, u32[]{:S(2)}) collective-permute-start(bf16[512,512]{1,0:T(8,128)(2,1)S(1)} %get-tuple-element.60), channel_id=1, source_target_pairs={{0,30},{1,31},{2,4},{3,5},{4,2},{5,3},{6,8},{7,9},{8,6},{9,7},{10,... | collective-permute-start | bytes 1572872 | tf_op jit(solution)/shard_map/ppermute | solution.py:27
  27.3 20.4 %collective-permute-start.9 = (bf16[512,512]{1,0:T(8,128)(2,1)S(1)}, bf16[512,512]{1,0:T(8,128)(2,1)S(1)}, u32[]{:S(2)}, u32[]{:S(2)}) collective-permute-start(bf16[512,512]{1,0:T(8,128)(2,1)S(1)} %get-tuple-element.61), channel_id=1, source_target_pairs={{0,2},{1,3},{2,0},{3,1},{4,6},{5,7},{6,4},{7,5},{8,10},{9,11},{10,... | collective-permute-start | bytes 1572872 | tf_op jit(solution)/shard_map/ppermute | solution.py:27
  32.7 22.5 %collective-permute-start.6 = (bf16[512,512]{1,0:T(8,128)(2,1)S(1)}, bf16[512,512]{1,0:T(8,128)(2,1)S(1)}, u32[]{:S(2)}, u32[]{:S(2)}) collective-permute-start(bf16[512,512]{1,0:T(8,128)(2,1)S(1)} %get-tuple-element.56), channel_id=1, source_target_pairs={{0,30},{1,31},{2,4},{3,5},{4,2},{5,3},{6,8},{7,9},{8,6},{9,7},{10,... | collective-permute-start | bytes 1572872 | tf_op jit(solution)/shard_map/ppermute | solution.py:27
  38.5 6.8 %copy-start.9 = (f32[512]{0:T(512)S(1)}, f32[512]{0:T(512)}, u32[]{:S(2)}) copy-start(f32[512]{0:T(512)} %param.15) | copy-start | bytes 6148
  38.5 20.3 %collective-permute-start.7 = (bf16[512,512]{1,0:T(8,128)(2,1)S(1)}, bf16[512,512]{1,0:T(8,128)(2,1)S(1)}, u32[]{:S(2)}, u32[]{:S(2)}) collective-permute-start(bf16[512,512]{1,0:T(8,128)(2,1)S(1)} %get-tuple-element.57), channel_id=1, source_target_pairs={{0,2},{1,3},{2,0},{3,1},{4,6},{5,7},{6,4},{7,5},{8,10},{9,11},{10,... | collective-permute-start | bytes 1572872 | tf_op jit(solution)/shard_map/ppermute | solution.py:27
  43.1 12.1 %copy-start.4 = (bf16[512,1024]{1,0:T(8,128)(2,1)S(1)}, bf16[512,1024]{1,0:T(8,128)(2,1)}, u32[]{:S(2)}) copy-start(bf16[512,1024]{1,0:T(8,128)(2,1)} %point_ref.9) | copy-start | bytes 3145732
  43.1 12.1 %copy-start.6 = (f32[1024]{0:T(1024)S(1)}, f32[1024]{0:T(1024)}, u32[]{:S(2)}) copy-start(f32[1024]{0:T(1024)} %param.17) | copy-start | bytes 12292
  43.2 19.8 %collective-permute-start.4 = (bf16[352,512]{1,0:T(8,128)(2,1)S(1)}, bf16[352,512]{1,0:T(8,128)(2,1)S(1)}, u32[]{:S(2)}, u32[]{:S(2)}) collective-permute-start(bf16[352,512]{1,0:T(8,128)(2,1)S(1)} %get-tuple-element.53), channel_id=1, source_target_pairs={{0,30},{1,31},{2,4},{3,5},{4,2},{5,3},{6,8},{7,9},{8,6},{9,7},{10,... | collective-permute-start | bytes 1081352 | tf_op jit(solution)/shard_map/ppermute | solution.py:27
  44.0 19.0 %collective-permute-start.5 = (bf16[352,512]{1,0:T(8,128)(2,1)S(1)}, bf16[352,512]{1,0:T(8,128)(2,1)S(1)}, u32[]{:S(2)}, u32[]{:S(2)}) collective-permute-start(bf16[352,512]{1,0:T(8,128)(2,1)S(1)} %get-tuple-element.54), channel_id=1, source_target_pairs={{0,2},{1,3},{2,0},{3,1},{4,6},{5,7},{6,4},{7,5},{8,10},{9,11},{10,... | collective-permute-start | bytes 1081352 | tf_op jit(solution)/shard_map/ppermute | solution.py:27
  47.7 17.6 %collective-permute-start.2 = (bf16[160,512]{1,0:T(8,128)(2,1)S(1)}, bf16[160,512]{1,0:T(8,128)(2,1)S(1)}, u32[]{:S(2)}, u32[]{:S(2)}) collective-permute-start(bf16[160,512]{1,0:T(8,128)(2,1)S(1)} %get-tuple-element.50), channel_id=1, source_target_pairs={{0,30},{1,31},{2,4},{3,5},{4,2},{5,3},{6,8},{7,9},{8,6},{9,7},{10,... | collective-permute-start | bytes 491528 | tf_op jit(solution)/shard_map/ppermute | solution.py:27
  55.2 10.1 %collective-permute-start.3 = (bf16[160,512]{1,0:T(8,128)(2,1)S(1)}, bf16[160,512]{1,0:T(8,128)(2,1)S(1)}, u32[]{:S(2)}, u32[]{:S(2)}) collective-permute-start(bf16[160,512]{1,0:T(8,128)(2,1)S(1)} %get-tuple-element.51), channel_id=1, source_target_pairs={{0,2},{1,3},{2,0},{3,1},{4,6},{5,7},{6,4},{7,5},{8,10},{9,11},{10,... | collective-permute-start | bytes 491528 | tf_op jit(solution)/shard_map/ppermute | solution.py:27

commit v9 on v8

--- a/solution.py
+++ b/solution.py
@@ -12,7 +12,7 @@
 ANY = pl.BlockSpec(memory_space=pl.ANY)
 HBM = pl.BlockSpec(memory_space=pltpu.HBM)
 SLOPE = math.sqrt(2.0 / math.pi)
-LAST_PIECE = 160
+LAST_PIECE = 128
 BF16 = jnp.bfloat16
 F32 = jnp.float32
 

time: 67.4 us -> 67.3 us (level)
  transfers between devices with their start and end apart: 12 -> 12, of which waited for: 5 -> 4; matrix products, arithmetic and copies ran while one was open for 0% -> 0% of each run, Pallas kernels for 46% -> 46%
where the time goes in v9:
time: 67.3 us; the launch traced here: 66.5 us
  Pallas kernels  34.3 us (51%)
  starting transfers between devices  23.8 us (35%)
  waiting for transfers between devices  8.1 us (12%)
    pallas_call x12, Pallas kernels, call(): pl.pallas_call(body, in_specs=specs, out_specs=[VMEM] * len(out_shape) if...  34.3 us
    ppermute x12, starting transfers between devices, swap(): return lax.ppermute(value, 'seq', sorted(pairs))  23.8 us
    ppermute x12, waiting for transfers between devices, swap(): return lax.ppermute(value, 'seq', sorted(pairs))  8.1 us
  transfers between devices with their start and end apart: 12, of which 4 were waited for; matrix products, arithmetic and copies ran while one was open for 0% of the time, Pallas kernels for 46%

profile of v9, /device:TPU:0, one launch (start us, length us, event | category | flops | bytes accessed | tf_op | source)
XLA Modules:
  0.0 66.5 jit_solution(9938128994384658545)
XLA Ops:
  0.0 0.0 copy-start.1
  0.0 0.0 copy-start
  0.0 0.0 copy-start.7
  0.0 0.0 copy-start.8
  0.0 2.4 %rim0.1 = (bf16[512,1024]{1,0:T(8,128)(2,1)S(1)}, bf16[512,512]{1,0:T(8,128)(2,1)S(1)}) custom-call(bf16[2048,1024]{1,0:T(8,128)(2,1)} %refs_0_.5, bf16[3,1024,512]{2,1,0:T(8,128)(2,1)} %refs_4_.6), custom_call_target="tpu_custom_call" | custom-call | flops 536870912 | bytes 7340032 | tf_op jit(solution)/shard_map/rim0/pallas_call | solution.py:50
  2.4 6.7 %collective-permute-start = (bf16[512,512]{1,0:T(8,128)(2,1)S(1)}, bf16[512,512]{1,0:T(8,128)(2,1)S(1)}, u32[]{:S(2)}, u32[]{:S(2)}) collective-permute-start(bf16[512,512]{1,0:T(8,128)(2,1)S(1)} %get-tuple-element.45), channel_id=1, source_target_pairs={{0,31},{1,2},{2,1},{3,4},{4,3},{5,6},{6,5},{7,8},{8,7},{9,10},{10,... | collective-permute-start | bytes 1572872 | tf_op jit(solution)/shard_map/ppermute | solution.py:27
  9.2 0.0 copy-done.1
  9.2 0.0 copy-done
  9.2 0.0 copy-done.7
  9.2 0.0 copy-done.8
  9.2 5.1 %layer1.1 = (bf16[512,1024]{1,0:T(8,128)(2,1)S(1)}, bf16[512,1024]{1,0:T(8,128)(2,1)S(1)}, bf16[512,1024]{1,0:T(8,128)(2,1)S(1)}, bf16[512,1024]{1,0:T(8,128)(2,...) custom-call(bf16[2048,1024]{1,0:T(8,128)(2,1)S(1)} %copy-done, ...), custom_call_target="tpu_custom_call" | custom-call | flops 3221225472 | bytes 12589056 | tf_op jit(solution)/shard_map/layer1/pallas_call | solution.py:50
  14.3 0.0 copy-start.2
  14.4 0.0 copy-start.3
  14.4 0.0 copy-start.5
  14.4 0.9 %collective-permute-start.10 = (bf16[512,512]{1,0:T(8,128)(2,1)S(1)}, bf16[512,512]{1,0:T(8,128)(2,1)S(1)}, u32[]{:S(2)}, u32[]{:S(2)}) collective-permute-start(bf16[512,512]{1,0:T(8,128)(2,1)S(1)} %get-tuple-element.64), channel_id=1, source_target_pairs={{0,30},{1,31},{2,4},{3,5},{4,2},{5,3},{6,8},{7,9},{8,6},{9,7},{10,... | collective-permute-start | bytes 1572872 | tf_op jit(solution)/shard_map/ppermute | solution.py:27
  15.3 0.0 collective-permute-start.11
  15.3 2.7 %rim3.1 = (bf16[512,1024]{1,0:T(8,128)(2,1)S(1)}, bf16[512,512]{1,0:T(8,128)(2,1)S(1)}) custom-call(bf16[2048,1024]{1,0:T(8,128)(2,1)} %refs_0_.5, bf16[3,1024,512]{2,1,0:T(8,128)(2,1)} %refs_4_.6), custom_call_target="tpu_custom_call" | custom-call | flops 536870912 | bytes 7340032 | tf_op jit(solution)/shard_map/rim3/pallas_call | solution.py:50
  18.0 0.6 collective-permute-start.1
  18.6 0.0 copy-done.2
  18.6 0.0 copy-done.3
  18.6 0.0 copy-done.5
  18.6 5.0 %layer2.1 = (bf16[512,1024]{1,0:T(8,128)(2,1)S(1)}, bf16[512,1024]{1,0:T(8,128)(2,1)S(1)}, bf16[512,512]{1,0:T(8,128)(2,1)S(1)}, bf16[512,512]{1,0:T(8,128)(2,1)S(1)}) custom-call(bf16[2048,1024]{1,0:T(8,128)(2,1)} %refs_0_.5, bf16[512,1024]{1,0:T(8,128)(2,1)S(1)} %get-tuple-element.38.refs_1_.refs_2_, ...), custom_call_target="tpu_custom_call" | custom-call | flops 3221225472 | bytes 14686208 | tf_op jit(solution)/shard_map/layer2/pallas_call | solution.py:50
  23.6 3.7 %collective-permute-start.8 = (bf16[512,512]{1,0:T(8,128)(2,1)S(1)}, bf16[512,512]{1,0:T(8,128)(2,1)S(1)}, u32[]{:S(2)}, u32[]{:S(2)}) collective-permute-start(bf16[512,512]{1,0:T(8,128)(2,1)S(1)} %get-tuple-element.60), channel_id=1, source_target_pairs={{0,30},{1,31},{2,4},{3,5},{4,2},{5,3},{6,8},{7,9},{8,6},{9,7},{10,... | collective-permute-start | bytes 1572872 | tf_op jit(solution)/shard_map/ppermute | solution.py:27
  27.3 0.0 collective-permute-done.refs_3_
  27.3 0.0 collective-permute-start.9
  27.3 4.0 %layer0.1 = (bf16[512,1024]{1,0:T(8,128)(2,1)S(1)}, bf16[512,1024]{1,0:T(8,128)(2,1)S(1)}, bf16[512,512]{1,0:T(8,128)(2,1)S(1)}, bf16[512,512]{1,0:T(8,128)(2,1)S(1)}) custom-call(bf16[2048,1024]{1,0:T(8,128)(2,1)} %refs_0_.5, bf16[512,1024]{1,0:T(8,128)(2,1)S(1)} %get-tuple-element.36.before_ref.refs_1_, ...), custom_call_target="tpu_custom_call" | custom-call | flops 3221225472 | bytes 14161920 | tf_op jit(solution)/shard_map/layer0/pallas_call | solution.py:50
  31.3 1.5 %collective-permute-done.10.one_side_ref = bf16[512,512]{1,0:T(8,128)(2,1)S(1)} collective-permute-done((bf16[512,512]{1,0:T(8,128)(2,1)S(1)}, bf16[512,512]{1,0:T(8,128)(2,1)S(1)}, u32[]{:S(2)}, u32[]{:S(2)}) %collective-permute-start.10) | collective-permute-done | bytes 524320 | tf_op jit(solution)/shard_map/ppermute | solution.py:27
  32.7 5.8 %collective-permute-start.6 = (bf16[512,512]{1,0:T(8,128)(2,1)S(1)}, bf16[512,512]{1,0:T(8,128)(2,1)S(1)}, u32[]{:S(2)}, u32[]{:S(2)}) collective-permute-start(bf16[512,512]{1,0:T(8,128)(2,1)S(1)} %get-tuple-element.56), channel_id=1, source_target_pairs={{0,30},{1,31},{2,4},{3,5},{4,2},{5,3},{6,8},{7,9},{8,6},{9,7},{10,... | collective-permute-start | bytes 1572872 | tf_op jit(solution)/shard_map/ppermute | solution.py:27
  38.5 0.0 collective-permute-done.1.refs_3_
  38.5 0.0 copy-start.9
  38.5 0.0 collective-permute-start.7
  38.6 4.6 %layer3.1 = (bf16[512,1024]{1,0:T(8,128)(2,1)S(1)}, bf16[512,1024]{1,0:T(8,128)(2,1)S(1)}, bf16[384,512]{1,0:T(8,128)(2,1)S(1)}, bf16[128,512]{1,0:T(8,128)(2,1)...) custom-call(bf16[2048,1024]{1,0:T(8,128)(2,1)} %refs_0_.5, ...), custom_call_target="tpu_custom_call" | custom-call | flops 3221225472 | bytes 14161920 | tf_op jit(solution)/shard_map/layer3/pallas_call | solution.py:50
  43.1 0.0 copy-start.4
  43.1 0.0 copy-start.6
  43.1 0.0 collective-permute-done.11.other_side_ref
  43.2 0.2 collective-permute-start.4
  43.3 0.6 collective-permute-done.8.one_side_ref
  44.0 1.4 %collective-permute-start.5 = (bf16[384,512]{1,0:T(8,128)(2,1)S(1)}, bf16[384,512]{1,0:T(8,128)(2,1)S(1)}, u32[]{:S(2)}, u32[]{:S(2)}) collective-permute-start(bf16[384,512]{1,0:T(8,128)(2,1)S(1)} %get-tuple-element.54), channel_id=1, source_target_pairs={{0,2},{1,3},{2,0},{3,1},{4,6},{5,7},{6,4},{7,5},{8,10},{9,11},{10,... | collective-permute-start | bytes 1179656 | tf_op jit(solution)/shard_map/ppermute | solution.py:27
  45.4 0.0 copy-done.9
  45.4 2.3 %centre.1 = (f32[512,512]{1,0:T(8,128)S(1)}, f32[512,512]{1,0:T(8,128)S(1)}, f32[512,512]{1,0:T(8,128)S(1)}, f32[512,512]{1,0:T(8,128)S(1)}) custom-call(bf16[512,1024]{1,0:T(8,128)(2,1)S(1)} %get-tuple-element.37.refs_0_, bf16[512,1024]{1,0:T(8,128)(2,1)S(1)} %get-tuple-element.44.refs_1_, bf16[512,1024]{1,0:T(8,128)(2,1)S(1)} %get-tuple-element.46.refs_2_, ...), custom_call_target="tpu_custom_call" | custom-call | flops 2147483648 | bytes 7342080 | tf_op jit(solution)/shard_map/centre/pallas_call | solution.py:50
  47.7 0.0 copy-done.4
  47.7 0.0 copy-done.6
  47.7 1.8 %finish1.1.rest_0_ = bf16[2048,1024]{1,0:T(8,128)(2,1)} custom-call(f32[512,512]{1,0:T(8,128)S(1)} %get-tuple-element.63.centre_ref, bf16[512,512]{1,0:T(8,128)(2,1)S(1)} %collective-permute-done.10.one_side_ref, bf16[512,512]{1,0:T(8,128)(2,1)S(1)} %collective-permute-done.11.other_side_ref, bf16[512,1024]{1,0:T(8,128)(2,1)S(1)} %get-tuple-element.66.one_ref, ...), custom_call_target="tpu_custom_call" | custom-call | flops 536870912 | bytes 4198400 | tf_op jit(solution)/shard_map/finish1/pallas_call | solution.py:50
  49.5 0.0 collective-permute-done.9.other_side_ref
  49.5 4.5 %collective-permute-start.2 = (bf16[128,512]{1,0:T(8,128)(2,1)S(1)}, bf16[128,512]{1,0:T(8,128)(2,1)S(1)}, u32[]{:S(2)}, u32[]{:S(2)}) collective-permute-start(bf16[128,512]{1,0:T(8,128)(2,1)S(1)} %get-tuple-element.50), channel_id=1, source_target_pairs={{0,30},{1,31},{2,4},{3,5},{4,2},{5,3},{6,8},{7,9},{8,6},{9,7},{10,... | collective-permute-start | bytes 393224 | tf_op jit(solution)/shard_map/ppermute | solution.py:27
  54.0 1.2 %collective-permute-done.6.one_side_ref = bf16[512,512]{1,0:T(8,128)(2,1)S(1)} collective-permute-done((bf16[512,512]{1,0:T(8,128)(2,1)S(1)}, bf16[512,512]{1,0:T(8,128)(2,1)S(1)}, u32[]{:S(2)}, u32[]{:S(2)}) %collective-permute-start.6) | collective-permute-done | bytes 524320 | tf_op jit(solution)/shard_map/ppermute | solution.py:27
  55.2 0.0 collective-permute-start.3
  55.2 1.8 %finish2.1.rest_0_ = bf16[2048,1024]{1,0:T(8,128)(2,1)} custom-call(f32[512,512]{1,0:T(8,128)S(1)} %get-tuple-element.59.centre_ref, bf16[512,512]{1,0:T(8,128)(2,1)S(1)} %collective-permute-done.8.one_side_ref, bf16[512,512]{1,0:T(8,128)(2,1)S(1)} %collective-permute-done.9.other_side_ref, ...), custom_call_target="tpu_custom_call", output_to_operand_aliasing={{}: (6, {})} | custom-call | flops 536870912 | bytes 8392704 | tf_op jit(solution)/shard_map/finish2/pallas_call | solution.py:50
  57.0 0.0 collective-permute-done.7.other_side_ref
  57.0 1.8 %finish0.1.rest_0_ = bf16[2048,1024]{1,0:T(8,128)(2,1)} custom-call(f32[512,512]{1,0:T(8,128)S(1)} %get-tuple-element.55.centre_ref, bf16[512,512]{1,0:T(8,128)(2,1)S(1)} %collective-permute-done.6.one_side_ref, bf16[512,512]{1,0:T(8,128)(2,1)S(1)} %collective-permute-done.7.other_side_ref, ...), custom_call_target="tpu_custom_call", output_to_operand_aliasing={{}: (6, {})} | custom-call | flops 536870912 | bytes 8392704 | tf_op jit(solution)/shard_map/finish0/pallas_call | solution.py:50
  58.8 4.8 %collective-permute-done.4.one_side_ref = bf16[384,512]{1,0:T(8,128)(2,1)S(1)} collective-permute-done((bf16[384,512]{1,0:T(8,128)(2,1)S(1)}, bf16[384,512]{1,0:T(8,128)(2,1)S(1)}, u32[]{:S(2)}, u32[]{:S(2)}) %collective-permute-start.4) | collective-permute-done | bytes 393248 | tf_op jit(solution)/shard_map/ppermute | solution.py:27
  63.6 0.0 collective-permute-done.5.other_side_ref
  63.6 1.6 %finish3.2.rest_0_ = bf16[2048,1024]{1,0:T(8,128)(2,1)} custom-call(f32[512,512]{1,0:T(8,128)S(1)} %get-tuple-element.49.centre_ref, bf16[384,512]{1,0:T(8,128)(2,1)S(1)} %collective-permute-done.4.one_side_ref, bf16[384,512]{1,0:T(8,128)(2,1)S(1)} %collective-permute-done.5.other_side_ref, ...), custom_call_target="tpu_custom_call", output_to_operand_aliasing={{}: (6, {})} | custom-call | flops 402653184 | bytes 8130560 | tf_op jit(solution)/shard_map/finish3/pallas_call | solution.py:50
  65.3 0.0 collective-permute-done.2.one_side_ref
  65.3 0.0 collective-permute-done.3.other_side_ref
  65.3 1.1 %finish3.3 = bf16[2048,1024]{1,0:T(8,128)(2,1)} custom-call(f32[512,512]{1,0:T(8,128)S(1)} %get-tuple-element.49.centre_ref, bf16[128,512]{1,0:T(8,128)(2,1)S(1)} %collective-permute-done.2.one_side_ref, bf16[128,512]{1,0:T(8,128)(2,1)S(1)} %collective-permute-done.3.other_side_ref, ...), custom_call_target="tpu_custom_call", output_to_operand_aliasing={{}: (6, {})} | custom-call | flops 134217728 | bytes 7606272 | tf_op jit(solution)/shard_map/finish3/pallas_call | solution.py:50
Async XLA Ops:
  0.0 9.2 %copy-start.1 = (bf16[3,1024,512]{2,1,0:T(8,128)(2,1)S(1)}, bf16[3,1024,512]{2,1,0:T(8,128)(2,1)}, u32[]{:S(2)}) copy-start(bf16[3,1024,512]{2,1,0:T(8,128)(2,1)} %refs_4_.6) | copy-start | bytes 9437188
  0.0 9.2 %copy-start = (bf16[2048,1024]{1,0:T(8,128)(2,1)S(1)}, bf16[2048,1024]{1,0:T(8,128)(2,1)}, u32[]{:S(2)}) copy-start(bf16[2048,1024]{1,0:T(8,128)(2,1)} %refs_0_.5) | copy-start | bytes 12582916
  0.0 9.2 %copy-start.7 = (f32[1024]{0:T(1024)S(1)}, f32[1024]{0:T(1024)}, u32[]{:S(2)}) copy-start(f32[1024]{0:T(1024)} %param.13) | copy-start | bytes 12292
  0.0 9.2 %copy-start.8 = (f32[512]{0:T(512)S(1)}, f32[512]{0:T(512)}, u32[]{:S(2)}) copy-start(f32[512]{0:T(512)} %param.11) | copy-start | bytes 6148
  2.4 24.9 %collective-permute-start = (bf16[512,512]{1,0:T(8,128)(2,1)S(1)}, bf16[512,512]{1,0:T(8,128)(2,1)S(1)}, u32[]{:S(2)}, u32[]{:S(2)}) collective-permute-start(bf16[512,512]{1,0:T(8,128)(2,1)S(1)} %get-tuple-element.45), channel_id=1, source_target_pairs={{0,31},{1,2},{2,1},{3,4},{4,3},{5,6},{6,5},{7,8},{8,7},{9,10},{10,... | collective-permute-start | bytes 1572872 | tf_op jit(solution)/shard_map/ppermute | solution.py:27
  14.3 4.3 %copy-start.2 = (bf16[3,1024,512]{2,1,0:T(8,128)(2,1)S(1)}, bf16[3,1024,512]{2,1,0:T(8,128)(2,1)}, u32[]{:S(2)}) copy-start(bf16[3,1024,512]{2,1,0:T(8,128)(2,1)} %refs_4_.6) | copy-start | bytes 9437188
  14.4 4.2 %copy-start.3 = (bf16[3,1024,512]{2,1,0:T(8,128)(2,1)S(1)}, bf16[3,1024,512]{2,1,0:T(8,128)(2,1)}, u32[]{:S(2)}) copy-start(bf16[3,1024,512]{2,1,0:T(8,128)(2,1)} %refs_4_.7) | copy-start | bytes 9437188
  14.4 4.2 %copy-start.5 = (bf16[512,1024]{1,0:T(8,128)(2,1)S(1)}, bf16[512,1024]{1,0:T(8,128)(2,1)}, u32[]{:S(2)}) copy-start(bf16[512,1024]{1,0:T(8,128)(2,1)} %refs_6_.5) | copy-start | bytes 3145732
  14.4 18.4 %collective-permute-start.10 = (bf16[512,512]{1,0:T(8,128)(2,1)S(1)}, bf16[512,512]{1,0:T(8,128)(2,1)S(1)}, u32[]{:S(2)}, u32[]{:S(2)}) collective-permute-start(bf16[512,512]{1,0:T(8,128)(2,1)S(1)} %get-tuple-element.64), channel_id=1, source_target_pairs={{0,30},{1,31},{2,4},{3,5},{4,2},{5,3},{6,8},{7,9},{8,6},{9,7},{10,... | collective-permute-start | bytes 1572872 | tf_op jit(solution)/shard_map/ppermute | solution.py:27
  15.3 27.9 %collective-permute-start.11 = (bf16[512,512]{1,0:T(8,128)(2,1)S(1)}, bf16[512,512]{1,0:T(8,128)(2,1)S(1)}, u32[]{:S(2)}, u32[]{:S(2)}) collective-permute-start(bf16[512,512]{1,0:T(8,128)(2,1)S(1)} %get-tuple-element.65), channel_id=1, source_target_pairs={{0,2},{1,3},{2,0},{3,1},{4,6},{5,7},{6,4},{7,5},{8,10},{9,11},{10,... | collective-permute-start | bytes 1572872 | tf_op jit(solution)/shard_map/ppermute | solution.py:27
  18.0 20.5 %collective-permute-start.1 = (bf16[512,512]{1,0:T(8,128)(2,1)S(1)}, bf16[512,512]{1,0:T(8,128)(2,1)S(1)}, u32[]{:S(2)}, u32[]{:S(2)}) collective-permute-start(bf16[512,512]{1,0:T(8,128)(2,1)S(1)} %get-tuple-element.47), channel_id=1, source_target_pairs={{0,1},{1,0},{2,3},{3,2},{4,5},{5,4},{6,7},{7,6},{8,9},{9,8},{10,11... | collective-permute-start | bytes 1572872 | tf_op jit(solution)/shard_map/ppermute | solution.py:27
  23.6 20.4 %collective-permute-start.8 = (bf16[512,512]{1,0:T(8,128)(2,1)S(1)}, bf16[512,512]{1,0:T(8,128)(2,1)S(1)}, u32[]{:S(2)}, u32[]{:S(2)}) collective-permute-start(bf16[512,512]{1,0:T(8,128)(2,1)S(1)} %get-tuple-element.60), channel_id=1, source_target_pairs={{0,30},{1,31},{2,4},{3,5},{4,2},{5,3},{6,8},{7,9},{8,6},{9,7},{10,... | collective-permute-start | bytes 1572872 | tf_op jit(solution)/shard_map/ppermute | solution.py:27
  27.3 22.2 %collective-permute-start.9 = (bf16[512,512]{1,0:T(8,128)(2,1)S(1)}, bf16[512,512]{1,0:T(8,128)(2,1)S(1)}, u32[]{:S(2)}, u32[]{:S(2)}) collective-permute-start(bf16[512,512]{1,0:T(8,128)(2,1)S(1)} %get-tuple-element.61), channel_id=1, source_target_pairs={{0,2},{1,3},{2,0},{3,1},{4,6},{5,7},{6,4},{7,5},{8,10},{9,11},{10,... | collective-permute-start | bytes 1572872 | tf_op jit(solution)/shard_map/ppermute | solution.py:27
  32.7 22.5 %collective-permute-start.6 = (bf16[512,512]{1,0:T(8,128)(2,1)S(1)}, bf16[512,512]{1,0:T(8,128)(2,1)S(1)}, u32[]{:S(2)}, u32[]{:S(2)}) collective-permute-start(bf16[512,512]{1,0:T(8,128)(2,1)S(1)} %get-tuple-element.56), channel_id=1, source_target_pairs={{0,30},{1,31},{2,4},{3,5},{4,2},{5,3},{6,8},{7,9},{8,6},{9,7},{10,... | collective-permute-start | bytes 1572872 | tf_op jit(solution)/shard_map/ppermute | solution.py:27
  38.5 6.8 %copy-start.9 = (f32[512]{0:T(512)S(1)}, f32[512]{0:T(512)}, u32[]{:S(2)}) copy-start(f32[512]{0:T(512)} %param.15) | copy-start | bytes 6148
  38.5 18.5 %collective-permute-start.7 = (bf16[512,512]{1,0:T(8,128)(2,1)S(1)}, bf16[512,512]{1,0:T(8,128)(2,1)S(1)}, u32[]{:S(2)}, u32[]{:S(2)}) collective-permute-start(bf16[512,512]{1,0:T(8,128)(2,1)S(1)} %get-tuple-element.57), channel_id=1, source_target_pairs={{0,2},{1,3},{2,0},{3,1},{4,6},{5,7},{6,4},{7,5},{8,10},{9,11},{10,... | collective-permute-start | bytes 1572872 | tf_op jit(solution)/shard_map/ppermute | solution.py:27
  43.1 4.6 %copy-start.4 = (bf16[512,1024]{1,0:T(8,128)(2,1)S(1)}, bf16[512,1024]{1,0:T(8,128)(2,1)}, u32[]{:S(2)}) copy-start(bf16[512,1024]{1,0:T(8,128)(2,1)} %point_ref.9) | copy-start | bytes 3145732
  43.1 4.6 %copy-start.6 = (f32[1024]{0:T(1024)S(1)}, f32[1024]{0:T(1024)}, u32[]{:S(2)}) copy-start(f32[1024]{0:T(1024)} %param.17) | copy-start | bytes 12292
  43.2 20.5 %collective-permute-start.4 = (bf16[384,512]{1,0:T(8,128)(2,1)S(1)}, bf16[384,512]{1,0:T(8,128)(2,1)S(1)}, u32[]{:S(2)}, u32[]{:S(2)}) collective-permute-start(bf16[384,512]{1,0:T(8,128)(2,1)S(1)} %get-tuple-element.53), channel_id=1, source_target_pairs={{0,30},{1,31},{2,4},{3,5},{4,2},{5,3},{6,8},{7,9},{8,6},{9,7},{10,... | collective-permute-start | bytes 1179656 | tf_op jit(solution)/shard_map/ppermute | solution.py:27
  44.0 19.7 %collective-permute-start.5 = (bf16[384,512]{1,0:T(8,128)(2,1)S(1)}, bf16[384,512]{1,0:T(8,128)(2,1)S(1)}, u32[]{:S(2)}, u32[]{:S(2)}) collective-permute-start(bf16[384,512]{1,0:T(8,128)(2,1)S(1)} %get-tuple-element.54), channel_id=1, source_target_pairs={{0,2},{1,3},{2,0},{3,1},{4,6},{5,7},{6,4},{7,5},{8,10},{9,11},{10,... | collective-permute-start | bytes 1179656 | tf_op jit(solution)/shard_map/ppermute | solution.py:27
  49.5 15.8 %collective-permute-start.2 = (bf16[128,512]{1,0:T(8,128)(2,1)S(1)}, bf16[128,512]{1,0:T(8,128)(2,1)S(1)}, u32[]{:S(2)}, u32[]{:S(2)}) collective-permute-start(bf16[128,512]{1,0:T(8,128)(2,1)S(1)} %get-tuple-element.50), channel_id=1, source_target_pairs={{0,30},{1,31},{2,4},{3,5},{4,2},{5,3},{6,8},{7,9},{8,6},{9,7},{10,... | collective-permute-start | bytes 393224 | tf_op jit(solution)/shard_map/ppermute | solution.py:27
  55.2 10.1 %collective-permute-start.3 = (bf16[128,512]{1,0:T(8,128)(2,1)S(1)}, bf16[128,512]{1,0:T(8,128)(2,1)S(1)}, u32[]{:S(2)}, u32[]{:S(2)}) collective-permute-start(bf16[128,512]{1,0:T(8,128)(2,1)S(1)} %get-tuple-element.51), channel_id=1, source_target_pairs={{0,2},{1,3},{2,0},{3,1},{4,6},{5,7},{6,4},{7,5},{8,10},{9,11},{10,... | collective-permute-start | bytes 393224 | tf_op jit(solution)/shard_map/ppermute | solution.py:27

commit v10 on v9

--- a/solution.py
+++ b/solution.py
@@ -12,7 +12,7 @@
 ANY = pl.BlockSpec(memory_space=pl.ANY)
 HBM = pl.BlockSpec(memory_space=pltpu.HBM)
 SLOPE = math.sqrt(2.0 / math.pi)
-LAST_PIECE = 128
+LAST_PIECE = 96
 BF16 = jnp.bfloat16
 F32 = jnp.float32
 

time: 67.3 us -> 67.9 us (level)
  no operation moved by 1% of the time
where the time goes in v10:
time: 67.9 us; the launch traced here: 67.2 us
  Pallas kernels  34.3 us (51%)
  starting transfers between devices  23.8 us (35%)
  waiting for transfers between devices  8.7 us (13%)
    pallas_call x12, Pallas kernels, call(): pl.pallas_call(body, in_specs=specs, out_specs=[VMEM] * len(out_shape) if...  34.3 us
    ppermute x12, starting transfers between devices, swap(): return lax.ppermute(value, 'seq', sorted(pairs))  23.8 us
    ppermute x12, waiting for transfers between devices, swap(): return lax.ppermute(value, 'seq', sorted(pairs))  8.7 us
  transfers between devices with their start and end apart: 12, of which 4 were waited for; matrix products, arithmetic and copies ran while one was open for 0% of the time, Pallas kernels for 46%

profile of v10, /device:TPU:0, one launch (start us, length us, event | category | flops | bytes accessed | tf_op | source)
XLA Modules:
  0.0 67.2 jit_solution(13178792019874692072)
XLA Ops:
  0.0 0.0 copy-start.1
  0.0 0.0 copy-start
  0.0 0.0 copy-start.7
  0.0 0.0 copy-start.8
  0.0 2.4 %rim0.1 = (bf16[512,1024]{1,0:T(8,128)(2,1)S(1)}, bf16[512,512]{1,0:T(8,128)(2,1)S(1)}) custom-call(bf16[2048,1024]{1,0:T(8,128)(2,1)} %refs_0_.5, bf16[3,1024,512]{2,1,0:T(8,128)(2,1)} %refs_4_.6), custom_call_target="tpu_custom_call" | custom-call | flops 536870912 | bytes 7340032 | tf_op jit(solution)/shard_map/rim0/pallas_call | solution.py:50
  2.4 6.7 %collective-permute-start = (bf16[512,512]{1,0:T(8,128)(2,1)S(1)}, bf16[512,512]{1,0:T(8,128)(2,1)S(1)}, u32[]{:S(2)}, u32[]{:S(2)}) collective-permute-start(bf16[512,512]{1,0:T(8,128)(2,1)S(1)} %get-tuple-element.45), channel_id=1, source_target_pairs={{0,31},{1,2},{2,1},{3,4},{4,3},{5,6},{6,5},{7,8},{8,7},{9,10},{10,... | collective-permute-start | bytes 1572872 | tf_op jit(solution)/shard_map/ppermute | solution.py:27
  9.2 0.0 copy-done.1
  9.2 0.0 copy-done
  9.2 0.0 copy-done.7
  9.2 0.0 copy-done.8
  9.2 5.1 %layer1.1 = (bf16[512,1024]{1,0:T(8,128)(2,1)S(1)}, bf16[512,1024]{1,0:T(8,128)(2,1)S(1)}, bf16[512,1024]{1,0:T(8,128)(2,1)S(1)}, bf16[512,1024]{1,0:T(8,128)(2,...) custom-call(bf16[2048,1024]{1,0:T(8,128)(2,1)S(1)} %copy-done, ...), custom_call_target="tpu_custom_call" | custom-call | flops 3221225472 | bytes 12589056 | tf_op jit(solution)/shard_map/layer1/pallas_call | solution.py:50
  14.3 0.0 copy-start.2
  14.4 0.0 copy-start.3
  14.4 0.0 copy-start.5
  14.4 0.9 %collective-permute-start.10 = (bf16[512,512]{1,0:T(8,128)(2,1)S(1)}, bf16[512,512]{1,0:T(8,128)(2,1)S(1)}, u32[]{:S(2)}, u32[]{:S(2)}) collective-permute-start(bf16[512,512]{1,0:T(8,128)(2,1)S(1)} %get-tuple-element.64), channel_id=1, source_target_pairs={{0,30},{1,31},{2,4},{3,5},{4,2},{5,3},{6,8},{7,9},{8,6},{9,7},{10,... | collective-permute-start | bytes 1572872 | tf_op jit(solution)/shard_map/ppermute | solution.py:27
  15.3 0.0 collective-permute-start.11
  15.3 2.7 %rim3.1 = (bf16[512,1024]{1,0:T(8,128)(2,1)S(1)}, bf16[512,512]{1,0:T(8,128)(2,1)S(1)}) custom-call(bf16[2048,1024]{1,0:T(8,128)(2,1)} %refs_0_.5, bf16[3,1024,512]{2,1,0:T(8,128)(2,1)} %refs_4_.6), custom_call_target="tpu_custom_call" | custom-call | flops 536870912 | bytes 7340032 | tf_op jit(solution)/shard_map/rim3/pallas_call | solution.py:50
  18.0 0.6 collective-permute-start.1
  18.6 0.0 copy-done.2
  18.6 0.0 copy-done.3
  18.6 0.0 copy-done.5
  18.6 5.0 %layer2.1 = (bf16[512,1024]{1,0:T(8,128)(2,1)S(1)}, bf16[512,1024]{1,0:T(8,128)(2,1)S(1)}, bf16[512,512]{1,0:T(8,128)(2,1)S(1)}, bf16[512,512]{1,0:T(8,128)(2,1)S(1)}) custom-call(bf16[2048,1024]{1,0:T(8,128)(2,1)} %refs_0_.5, bf16[512,1024]{1,0:T(8,128)(2,1)S(1)} %get-tuple-element.38.refs_1_.refs_2_, ...), custom_call_target="tpu_custom_call" | custom-call | flops 3221225472 | bytes 14686208 | tf_op jit(solution)/shard_map/layer2/pallas_call | solution.py:50
  23.6 3.7 %collective-permute-start.8 = (bf16[512,512]{1,0:T(8,128)(2,1)S(1)}, bf16[512,512]{1,0:T(8,128)(2,1)S(1)}, u32[]{:S(2)}, u32[]{:S(2)}) collective-permute-start(bf16[512,512]{1,0:T(8,128)(2,1)S(1)} %get-tuple-element.60), channel_id=1, source_target_pairs={{0,30},{1,31},{2,4},{3,5},{4,2},{5,3},{6,8},{7,9},{8,6},{9,7},{10,... | collective-permute-start | bytes 1572872 | tf_op jit(solution)/shard_map/ppermute | solution.py:27
  27.3 0.0 collective-permute-done.refs_3_
  27.3 0.0 collective-permute-start.9
  27.3 4.0 %layer0.1 = (bf16[512,1024]{1,0:T(8,128)(2,1)S(1)}, bf16[512,1024]{1,0:T(8,128)(2,1)S(1)}, bf16[512,512]{1,0:T(8,128)(2,1)S(1)}, bf16[512,512]{1,0:T(8,128)(2,1)S(1)}) custom-call(bf16[2048,1024]{1,0:T(8,128)(2,1)} %refs_0_.5, bf16[512,1024]{1,0:T(8,128)(2,1)S(1)} %get-tuple-element.36.before_ref.refs_1_, ...), custom_call_target="tpu_custom_call" | custom-call | flops 3221225472 | bytes 14161920 | tf_op jit(solution)/shard_map/layer0/pallas_call | solution.py:50
  31.3 1.5 %collective-permute-done.10.one_side_ref = bf16[512,512]{1,0:T(8,128)(2,1)S(1)} collective-permute-done((bf16[512,512]{1,0:T(8,128)(2,1)S(1)}, bf16[512,512]{1,0:T(8,128)(2,1)S(1)}, u32[]{:S(2)}, u32[]{:S(2)}) %collective-permute-start.10) | collective-permute-done | bytes 524320 | tf_op jit(solution)/shard_map/ppermute | solution.py:27
  32.7 5.8 %collective-permute-start.6 = (bf16[512,512]{1,0:T(8,128)(2,1)S(1)}, bf16[512,512]{1,0:T(8,128)(2,1)S(1)}, u32[]{:S(2)}, u32[]{:S(2)}) collective-permute-start(bf16[512,512]{1,0:T(8,128)(2,1)S(1)} %get-tuple-element.56), channel_id=1, source_target_pairs={{0,30},{1,31},{2,4},{3,5},{4,2},{5,3},{6,8},{7,9},{8,6},{9,7},{10,... | collective-permute-start | bytes 1572872 | tf_op jit(solution)/shard_map/ppermute | solution.py:27
  38.5 0.0 collective-permute-done.1.refs_3_
  38.5 0.0 copy-start.9
  38.5 0.0 collective-permute-start.7
  38.6 4.6 %layer3.1 = (bf16[512,1024]{1,0:T(8,128)(2,1)S(1)}, bf16[512,1024]{1,0:T(8,128)(2,1)S(1)}, bf16[416,512]{1,0:T(8,128)(2,1)S(1)}, bf16[96,512]{1,0:T(8,128)(2,1)S...) custom-call(bf16[2048,1024]{1,0:T(8,128)(2,1)} %refs_0_.5, ...), custom_call_target="tpu_custom_call" | custom-call | flops 3221225472 | bytes 14161920 | tf_op jit(solution)/shard_map/layer3/pallas_call | solution.py:50
  43.1 0.0 copy-start.4
  43.1 0.0 copy-start.6
  43.1 0.0 collective-permute-done.11.other_side_ref
  43.2 0.2 collective-permute-start.4
  43.3 0.6 collective-permute-done.8.one_side_ref
  44.0 1.4 %collective-permute-start.5 = (bf16[416,512]{1,0:T(8,128)(2,1)S(1)}, bf16[416,512]{1,0:T(8,128)(2,1)S(1)}, u32[]{:S(2)}, u32[]{:S(2)}) collective-permute-start(bf16[416,512]{1,0:T(8,128)(2,1)S(1)} %get-tuple-element.54), channel_id=1, source_target_pairs={{0,2},{1,3},{2,0},{3,1},{4,6},{5,7},{6,4},{7,5},{8,10},{9,11},{10,... | collective-permute-start | bytes 1277960 | tf_op jit(solution)/shard_map/ppermute | solution.py:27
  45.4 0.0 copy-done.9
  45.4 2.3 %centre.1 = (f32[512,512]{1,0:T(8,128)S(1)}, f32[512,512]{1,0:T(8,128)S(1)}, f32[512,512]{1,0:T(8,128)S(1)}, f32[512,512]{1,0:T(8,128)S(1)}) custom-call(bf16[512,1024]{1,0:T(8,128)(2,1)S(1)} %get-tuple-element.37.refs_0_, bf16[512,1024]{1,0:T(8,128)(2,1)S(1)} %get-tuple-element.44.refs_1_, bf16[512,1024]{1,0:T(8,128)(2,1)S(1)} %get-tuple-element.46.refs_2_, ...), custom_call_target="tpu_custom_call" | custom-call | flops 2147483648 | bytes 7342080 | tf_op jit(solution)/shard_map/centre/pallas_call | solution.py:50
  47.7 0.0 copy-done.4
  47.7 0.0 copy-done.6
  47.7 1.8 %finish1.1.rest_0_ = bf16[2048,1024]{1,0:T(8,128)(2,1)} custom-call(f32[512,512]{1,0:T(8,128)S(1)} %get-tuple-element.63.centre_ref, bf16[512,512]{1,0:T(8,128)(2,1)S(1)} %collective-permute-done.10.one_side_ref, bf16[512,512]{1,0:T(8,128)(2,1)S(1)} %collective-permute-done.11.other_side_ref, bf16[512,1024]{1,0:T(8,128)(2,1)S(1)} %get-tuple-element.66.one_ref, ...), custom_call_target="tpu_custom_call" | custom-call | flops 536870912 | bytes 4198400 | tf_op jit(solution)/shard_map/finish1/pallas_call | solution.py:50
  49.5 0.0 collective-permute-done.9.other_side_ref
  49.5 4.5 %collective-permute-start.2 = (bf16[96,512]{1,0:T(8,128)(2,1)S(1)}, bf16[96,512]{1,0:T(8,128)(2,1)S(1)}, u32[]{:S(2)}, u32[]{:S(2)}) collective-permute-start(bf16[96,512]{1,0:T(8,128)(2,1)S(1)} %get-tuple-element.50), channel_id=1, source_target_pairs={{0,30},{1,31},{2,4},{3,5},{4,2},{5,3},{6,8},{7,9},{8,6},{9,7},{10,... | collective-permute-start | bytes 294920 | tf_op jit(solution)/shard_map/ppermute | solution.py:27
  54.0 1.2 %collective-permute-done.6.one_side_ref = bf16[512,512]{1,0:T(8,128)(2,1)S(1)} collective-permute-done((bf16[512,512]{1,0:T(8,128)(2,1)S(1)}, bf16[512,512]{1,0:T(8,128)(2,1)S(1)}, u32[]{:S(2)}, u32[]{:S(2)}) %collective-permute-start.6) | collective-permute-done | bytes 524320 | tf_op jit(solution)/shard_map/ppermute | solution.py:27
  55.2 0.0 collective-permute-start.3
  55.2 1.8 %finish2.1.rest_0_ = bf16[2048,1024]{1,0:T(8,128)(2,1)} custom-call(f32[512,512]{1,0:T(8,128)S(1)} %get-tuple-element.59.centre_ref, bf16[512,512]{1,0:T(8,128)(2,1)S(1)} %collective-permute-done.8.one_side_ref, bf16[512,512]{1,0:T(8,128)(2,1)S(1)} %collective-permute-done.9.other_side_ref, ...), custom_call_target="tpu_custom_call", output_to_operand_aliasing={{}: (6, {})} | custom-call | flops 536870912 | bytes 8392704 | tf_op jit(solution)/shard_map/finish2/pallas_call | solution.py:50
  57.0 0.0 collective-permute-done.7.other_side_ref
  57.0 1.8 %finish0.1.rest_0_ = bf16[2048,1024]{1,0:T(8,128)(2,1)} custom-call(f32[512,512]{1,0:T(8,128)S(1)} %get-tuple-element.55.centre_ref, bf16[512,512]{1,0:T(8,128)(2,1)S(1)} %collective-permute-done.6.one_side_ref, bf16[512,512]{1,0:T(8,128)(2,1)S(1)} %collective-permute-done.7.other_side_ref, ...), custom_call_target="tpu_custom_call", output_to_operand_aliasing={{}: (6, {})} | custom-call | flops 536870912 | bytes 8392704 | tf_op jit(solution)/shard_map/finish0/pallas_call | solution.py:50
  58.8 5.4 %collective-permute-done.4.one_side_ref = bf16[416,512]{1,0:T(8,128)(2,1)S(1)} collective-permute-done((bf16[416,512]{1,0:T(8,128)(2,1)S(1)}, bf16[416,512]{1,0:T(8,128)(2,1)S(1)}, u32[]{:S(2)}, u32[]{:S(2)}) %collective-permute-start.4) | collective-permute-done | bytes 426016 | tf_op jit(solution)/shard_map/ppermute | solution.py:27
  64.2 0.0 collective-permute-done.5.other_side_ref
  64.2 1.7 %finish3.2.rest_0_ = bf16[2048,1024]{1,0:T(8,128)(2,1)} custom-call(f32[512,512]{1,0:T(8,128)S(1)} %get-tuple-element.49.centre_ref, bf16[416,512]{1,0:T(8,128)(2,1)S(1)} %collective-permute-done.4.one_side_ref, bf16[416,512]{1,0:T(8,128)(2,1)S(1)} %collective-permute-done.5.other_side_ref, ...), custom_call_target="tpu_custom_call", output_to_operand_aliasing={{}: (6, {})} | custom-call | flops 436207616 | bytes 8196096 | tf_op jit(solution)/shard_map/finish3/pallas_call | solution.py:50
  66.0 0.0 collective-permute-done.2.one_side_ref
  66.0 0.0 collective-permute-done.3.other_side_ref
  66.0 1.0 %finish3.3 = bf16[2048,1024]{1,0:T(8,128)(2,1)} custom-call(f32[512,512]{1,0:T(8,128)S(1)} %get-tuple-element.49.centre_ref, bf16[96,512]{1,0:T(8,128)(2,1)S(1)} %collective-permute-done.2.one_side_ref, bf16[96,512]{1,0:T(8,128)(2,1)S(1)} %collective-permute-done.3.other_side_ref, ...), custom_call_target="tpu_custom_call", output_to_operand_aliasing={{}: (6, {})} | custom-call | flops 100663296 | bytes 7540736 | tf_op jit(solution)/shard_map/finish3/pallas_call | solution.py:50
Async XLA Ops:
  0.0 9.2 %copy-start.1 = (bf16[3,1024,512]{2,1,0:T(8,128)(2,1)S(1)}, bf16[3,1024,512]{2,1,0:T(8,128)(2,1)}, u32[]{:S(2)}) copy-start(bf16[3,1024,512]{2,1,0:T(8,128)(2,1)} %refs_4_.6) | copy-start | bytes 9437188
  0.0 9.2 %copy-start = (bf16[2048,1024]{1,0:T(8,128)(2,1)S(1)}, bf16[2048,1024]{1,0:T(8,128)(2,1)}, u32[]{:S(2)}) copy-start(bf16[2048,1024]{1,0:T(8,128)(2,1)} %refs_0_.5) | copy-start | bytes 12582916
  0.0 9.2 %copy-start.7 = (f32[1024]{0:T(1024)S(1)}, f32[1024]{0:T(1024)}, u32[]{:S(2)}) copy-start(f32[1024]{0:T(1024)} %param.13) | copy-start | bytes 12292
  0.0 9.2 %copy-start.8 = (f32[512]{0:T(512)S(1)}, f32[512]{0:T(512)}, u32[]{:S(2)}) copy-start(f32[512]{0:T(512)} %param.11) | copy-start | bytes 6148
  2.4 24.9 %collective-permute-start = (bf16[512,512]{1,0:T(8,128)(2,1)S(1)}, bf16[512,512]{1,0:T(8,128)(2,1)S(1)}, u32[]{:S(2)}, u32[]{:S(2)}) collective-permute-start(bf16[512,512]{1,0:T(8,128)(2,1)S(1)} %get-tuple-element.45), channel_id=1, source_target_pairs={{0,31},{1,2},{2,1},{3,4},{4,3},{5,6},{6,5},{7,8},{8,7},{9,10},{10,... | collective-permute-start | bytes 1572872 | tf_op jit(solution)/shard_map/ppermute | solution.py:27
  14.3 4.3 %copy-start.2 = (bf16[3,1024,512]{2,1,0:T(8,128)(2,1)S(1)}, bf16[3,1024,512]{2,1,0:T(8,128)(2,1)}, u32[]{:S(2)}) copy-start(bf16[3,1024,512]{2,1,0:T(8,128)(2,1)} %refs_4_.6) | copy-start | bytes 9437188
  14.4 4.2 %copy-start.3 = (bf16[3,1024,512]{2,1,0:T(8,128)(2,1)S(1)}, bf16[3,1024,512]{2,1,0:T(8,128)(2,1)}, u32[]{:S(2)}) copy-start(bf16[3,1024,512]{2,1,0:T(8,128)(2,1)} %refs_4_.7) | copy-start | bytes 9437188
  14.4 4.2 %copy-start.5 = (bf16[512,1024]{1,0:T(8,128)(2,1)S(1)}, bf16[512,1024]{1,0:T(8,128)(2,1)}, u32[]{:S(2)}) copy-start(bf16[512,1024]{1,0:T(8,128)(2,1)} %refs_6_.5) | copy-start | bytes 3145732
  14.4 18.4 %collective-permute-start.10 = (bf16[512,512]{1,0:T(8,128)(2,1)S(1)}, bf16[512,512]{1,0:T(8,128)(2,1)S(1)}, u32[]{:S(2)}, u32[]{:S(2)}) collective-permute-start(bf16[512,512]{1,0:T(8,128)(2,1)S(1)} %get-tuple-element.64), channel_id=1, source_target_pairs={{0,30},{1,31},{2,4},{3,5},{4,2},{5,3},{6,8},{7,9},{8,6},{9,7},{10,... | collective-permute-start | bytes 1572872 | tf_op jit(solution)/shard_map/ppermute | solution.py:27
  15.3 27.9 %collective-permute-start.11 = (bf16[512,512]{1,0:T(8,128)(2,1)S(1)}, bf16[512,512]{1,0:T(8,128)(2,1)S(1)}, u32[]{:S(2)}, u32[]{:S(2)}) collective-permute-start(bf16[512,512]{1,0:T(8,128)(2,1)S(1)} %get-tuple-element.65), channel_id=1, source_target_pairs={{0,2},{1,3},{2,0},{3,1},{4,6},{5,7},{6,4},{7,5},{8,10},{9,11},{10,... | collective-permute-start | bytes 1572872 | tf_op jit(solution)/shard_map/ppermute | solution.py:27
  18.0 20.5 %collective-permute-start.1 = (bf16[512,512]{1,0:T(8,128)(2,1)S(1)}, bf16[512,512]{1,0:T(8,128)(2,1)S(1)}, u32[]{:S(2)}, u32[]{:S(2)}) collective-permute-start(bf16[512,512]{1,0:T(8,128)(2,1)S(1)} %get-tuple-element.47), channel_id=1, source_target_pairs={{0,1},{1,0},{2,3},{3,2},{4,5},{5,4},{6,7},{7,6},{8,9},{9,8},{10,11... | collective-permute-start | bytes 1572872 | tf_op jit(solution)/shard_map/ppermute | solution.py:27
  23.6 20.4 %collective-permute-start.8 = (bf16[512,512]{1,0:T(8,128)(2,1)S(1)}, bf16[512,512]{1,0:T(8,128)(2,1)S(1)}, u32[]{:S(2)}, u32[]{:S(2)}) collective-permute-start(bf16[512,512]{1,0:T(8,128)(2,1)S(1)} %get-tuple-element.60), channel_id=1, source_target_pairs={{0,30},{1,31},{2,4},{3,5},{4,2},{5,3},{6,8},{7,9},{8,6},{9,7},{10,... | collective-permute-start | bytes 1572872 | tf_op jit(solution)/shard_map/ppermute | solution.py:27
  27.3 22.2 %collective-permute-start.9 = (bf16[512,512]{1,0:T(8,128)(2,1)S(1)}, bf16[512,512]{1,0:T(8,128)(2,1)S(1)}, u32[]{:S(2)}, u32[]{:S(2)}) collective-permute-start(bf16[512,512]{1,0:T(8,128)(2,1)S(1)} %get-tuple-element.61), channel_id=1, source_target_pairs={{0,2},{1,3},{2,0},{3,1},{4,6},{5,7},{6,4},{7,5},{8,10},{9,11},{10,... | collective-permute-start | bytes 1572872 | tf_op jit(solution)/shard_map/ppermute | solution.py:27
  32.7 22.5 %collective-permute-start.6 = (bf16[512,512]{1,0:T(8,128)(2,1)S(1)}, bf16[512,512]{1,0:T(8,128)(2,1)S(1)}, u32[]{:S(2)}, u32[]{:S(2)}) collective-permute-start(bf16[512,512]{1,0:T(8,128)(2,1)S(1)} %get-tuple-element.56), channel_id=1, source_target_pairs={{0,30},{1,31},{2,4},{3,5},{4,2},{5,3},{6,8},{7,9},{8,6},{9,7},{10,... | collective-permute-start | bytes 1572872 | tf_op jit(solution)/shard_map/ppermute | solution.py:27
  38.5 6.8 %copy-start.9 = (f32[512]{0:T(512)S(1)}, f32[512]{0:T(512)}, u32[]{:S(2)}) copy-start(f32[512]{0:T(512)} %param.15) | copy-start | bytes 6148
  38.5 18.5 %collective-permute-start.7 = (bf16[512,512]{1,0:T(8,128)(2,1)S(1)}, bf16[512,512]{1,0:T(8,128)(2,1)S(1)}, u32[]{:S(2)}, u32[]{:S(2)}) collective-permute-start(bf16[512,512]{1,0:T(8,128)(2,1)S(1)} %get-tuple-element.57), channel_id=1, source_target_pairs={{0,2},{1,3},{2,0},{3,1},{4,6},{5,7},{6,4},{7,5},{8,10},{9,11},{10,... | collective-permute-start | bytes 1572872 | tf_op jit(solution)/shard_map/ppermute | solution.py:27
  43.1 4.6 %copy-start.4 = (bf16[512,1024]{1,0:T(8,128)(2,1)S(1)}, bf16[512,1024]{1,0:T(8,128)(2,1)}, u32[]{:S(2)}) copy-start(bf16[512,1024]{1,0:T(8,128)(2,1)} %point_ref.9) | copy-start | bytes 3145732
  43.1 4.6 %copy-start.6 = (f32[1024]{0:T(1024)S(1)}, f32[1024]{0:T(1024)}, u32[]{:S(2)}) copy-start(f32[1024]{0:T(1024)} %param.17) | copy-start | bytes 12292
  43.2 21.1 %collective-permute-start.4 = (bf16[416,512]{1,0:T(8,128)(2,1)S(1)}, bf16[416,512]{1,0:T(8,128)(2,1)S(1)}, u32[]{:S(2)}, u32[]{:S(2)}) collective-permute-start(bf16[416,512]{1,0:T(8,128)(2,1)S(1)} %get-tuple-element.53), channel_id=1, source_target_pairs={{0,30},{1,31},{2,4},{3,5},{4,2},{5,3},{6,8},{7,9},{8,6},{9,7},{10,... | collective-permute-start | bytes 1277960 | tf_op jit(solution)/shard_map/ppermute | solution.py:27
  44.0 20.3 %collective-permute-start.5 = (bf16[416,512]{1,0:T(8,128)(2,1)S(1)}, bf16[416,512]{1,0:T(8,128)(2,1)S(1)}, u32[]{:S(2)}, u32[]{:S(2)}) collective-permute-start(bf16[416,512]{1,0:T(8,128)(2,1)S(1)} %get-tuple-element.54), channel_id=1, source_target_pairs={{0,2},{1,3},{2,0},{3,1},{4,6},{5,7},{6,4},{7,5},{8,10},{9,11},{10,... | collective-permute-start | bytes 1277960 | tf_op jit(solution)/shard_map/ppermute | solution.py:27
  49.5 16.4 %collective-permute-start.2 = (bf16[96,512]{1,0:T(8,128)(2,1)S(1)}, bf16[96,512]{1,0:T(8,128)(2,1)S(1)}, u32[]{:S(2)}, u32[]{:S(2)}) collective-permute-start(bf16[96,512]{1,0:T(8,128)(2,1)S(1)} %get-tuple-element.50), channel_id=1, source_target_pairs={{0,30},{1,31},{2,4},{3,5},{4,2},{5,3},{6,8},{7,9},{8,6},{9,7},{10,... | collective-permute-start | bytes 294920 | tf_op jit(solution)/shard_map/ppermute | solution.py:27
  55.2 10.8 %collective-permute-start.3 = (bf16[96,512]{1,0:T(8,128)(2,1)S(1)}, bf16[96,512]{1,0:T(8,128)(2,1)S(1)}, u32[]{:S(2)}, u32[]{:S(2)}) collective-permute-start(bf16[96,512]{1,0:T(8,128)(2,1)S(1)} %get-tuple-element.51), channel_id=1, source_target_pairs={{0,2},{1,3},{2,0},{3,1},{4,6},{5,7},{6,4},{7,5},{8,10},{9,11},{10,... | collective-permute-start | bytes 294920 | tf_op jit(solution)/shard_map/ppermute | solution.py:27
